TPU v7x, 128 devices: a whole 4x4x4 slice. The times are simulated.
128 devices in a mesh: ma: 32 (over y, z, core), sa: 4 (over x).
Axes of the slice: x: 4, y: 4, z: 4, core: 2. Of those that a mesh axis runs over, the one named last changes fastest.
Arguments:
- initial_heat_matrix: float32 [128, 128, 8192], P('ma', 'sa'), may hold values from -6 to 6
- conductivity: float32 [128, 8192], P('sa'), may hold values from 0.5 to 2
- laser_x: int32 [128, 2], P('ma'), may hold values from 0 to 127
- laser_y: int32 [128, 2], P('ma'), may hold values from 0 to 127
- pixel_cell: int32 [128, 512], P('sa', 'ma'), may hold values from 0 to 127, as said below
- observed: float32 [128, 512], P('sa', 'ma'), may hold values from -6 to 6
- obs_var: float32 [128, 512], P('sa', 'ma'), may hold values from 20 to 400
Outputs:
- analysis: float32 [128, 128, 8192], P('ma', 'sa')
Inputs may be any that keep to these rules, and one draw needn't show every extreme that they name: `pixel_cell`: pixel column j views a surface cell y of its own plane; y lies within 2 of j // 4 and in the same aligned group of 4 cells as that value.
All inputs are finite; a program needn't handle non-finite values.
Results may differ from a plain program's by a relative error of at most 0.000096.
Values sent between devices are 32-bit elements; how exact they have to be, the bound alone decides.
No kernel may reach another device: no remote copies, remote signals or barrier semaphores. Data moves between devices by JAX's collectives and lax.ppermute only.
A program may use at most 192 MiB of HBM per device.

v0:
```python
import jax
import jax.numpy as jnp
from jax import lax
from jax.sharding import Mesh
from jax.sharding import PartitionSpec as P

CELLS_DEPTHWISE = 64
STEPS = 2
MA_SA = ("ma_0", "ma_1", "ma_2", "sa")
MA = ("ma_0", "ma_1", "ma_2")


step_dt = 0.025
alpha_cond = 0.05
laser_power = 12.0
beam_spot_width = 18.0


def extended(block, sides, width):
    for axis, dim in sides:
        count = lax.axis_size(axis)
        forward = [(i, i + 1) for i in range(count - 1)]
        backward = [(target, source) for source, target in forward]
        low = lax.ppermute(
            lax.slice_in_dim(block, block.shape[dim] - width, None, axis=dim), axis, forward
        )
        high = lax.ppermute(lax.slice_in_dim(block, 0, width, axis=dim), axis, backward)
        block = jnp.concatenate([low, block, high], axis=dim)
    return block


def cut_along(x, dim, devices):
    before, after = (x.shape[:dim], x.shape[dim + 1 :])
    return jnp.moveaxis(x.reshape(*before, devices, -1, *after), dim, 0)


def in_order(pieces, dim):
    pieces = jnp.moveaxis(pieces, 0, dim)
    lengths = pieces.shape
    return pieces.reshape(*lengths[:dim], lengths[dim] * lengths[dim + 1], *lengths[dim + 2 :])


def moved_by_axis(pieces, axes, sequence):
    inside = pieces.shape[1:]
    filled = pieces.reshape(*(lax.axis_size(a) for a in axes), *inside)
    for k in sequence:
        filled = lax.all_to_all(filled, axes[k], k, k, tiled=True)
    return filled.reshape(-1, *inside)


def exchange_by_chip(x, groups, sequence, split_dim, concat_dim):
    devices = lax.axis_size(groups[0]) * lax.axis_size(groups[1])
    pieces = cut_along(x, split_dim, devices)
    return in_order(moved_by_axis(pieces, groups, sequence), concat_dim)


def conduct(field_ext, cond_ext, first_plane, spot_x, spot_y):
    kext = cond_ext[None] * (1.0 + alpha_cond * field_ext * field_ext)
    fpad = jnp.pad(field_ext, ((0, 0), (0, 0), (1, 1), (1, 1)))
    kpad = jnp.pad(kext, ((0, 0), (0, 0), (1, 1), (1, 1)))
    centre = fpad[:, 1:-1, 1:-1, 1:-1]
    kcentre = kpad[:, 1:-1, 1:-1, 1:-1]
    shifted = [
        (slice(2, None), slice(1, -1), slice(1, -1)),
        (slice(None, -2), slice(1, -1), slice(1, -1)),
        (slice(1, -1), slice(2, None), slice(1, -1)),
        (slice(1, -1), slice(None, -2), slice(1, -1)),
        (slice(1, -1), slice(1, -1), slice(2, None)),
        (slice(1, -1), slice(1, -1), slice(None, -2)),
    ]
    flux = jnp.zeros_like(centre)
    for pick in shifted:
        neighbour = fpad[(slice(None),) + pick]
        kneigh = kpad[(slice(None),) + pick]
        flux = flux + 0.5 * (kcentre + kneigh) * (neighbour - centre)
    width = centre.shape[1]
    rows_y = centre.shape[2]
    depth = centre.shape[3]
    xglob = first_plane + jnp.arange(width, dtype=jnp.int32)
    yglob = jnp.arange(rows_y, dtype=jnp.int32)
    delta_x = (xglob[None, :] - spot_x[:, None]).astype(jnp.float32)
    delta_y = (yglob[None, :] - spot_y[:, None]).astype(jnp.float32)
    spot = laser_power * jnp.exp(
        -(delta_x[:, :, None] ** 2 + delta_y[:, None, :] ** 2) / beam_spot_width
    )
    surface_top = (jnp.arange(depth, dtype=jnp.int32) == depth - 1).astype(jnp.float32)
    heat = spot[:, :, :, None] * surface_top[None, None, None, :]
    return centre + step_dt * (flux + heat)


def transform(block, mix):
    fmean = jnp.mean(block, axis=0)
    anom = block - fmean[None]
    return fmean[None] + jnp.einsum("jxc,jk->kxc", anom, mix, precision=lax.Precision.HIGHEST)


def lower_factor(amat):
    count = amat.shape[0]
    positions = jnp.arange(count, dtype=jnp.int32)

    def column_step(index_j, factor):
        row_j = lax.dynamic_slice_in_dim(factor, index_j, 1, 0)[0]
        row_j = jnp.where(positions < index_j, row_j, 0.0)
        column = lax.dynamic_slice_in_dim(amat, index_j, 1, 1)[:, 0]
        rest = column - jnp.dot(factor, row_j, precision=lax.Precision.HIGHEST)
        pivot = jnp.sqrt(lax.dynamic_slice_in_dim(rest, index_j, 1, 0)[0])
        fresh = jnp.where(
            positions > index_j, rest / pivot, jnp.where(positions == index_j, pivot, 0.0)
        )
        return jnp.where((positions == index_j)[None, :], fresh[:, None], factor)

    return lax.fori_loop(0, count, column_step, jnp.zeros_like(amat))


def lower_inverse(factor):
    count = factor.shape[0]
    positions = jnp.arange(count, dtype=jnp.int32)

    def row_step(index_i, inverse):
        row_i = lax.dynamic_slice_in_dim(factor, index_i, 1, 0)[0]
        pivot = lax.dynamic_slice_in_dim(row_i, index_i, 1, 0)[0]
        unit = (positions == index_i).astype(jnp.float32)
        fresh = (unit - jnp.dot(row_i, inverse, precision=lax.Precision.HIGHEST)) / pivot
        return jnp.where((positions == index_i)[:, None], fresh[None, :], inverse)

    return lax.fori_loop(0, count, row_step, jnp.zeros_like(factor))


def per_device(initial_heat_matrix, conductivity, laser_x, laser_y, pixel_cell, observed, obs_var):
    members, planes, columns = initial_heat_matrix.shape
    depth = CELLS_DEPTHWISE
    rows_y = columns // depth
    first = lax.axis_index("sa") * planes
    field = initial_heat_matrix.reshape(members, planes, rows_y, depth)
    cond_grid = conductivity.reshape(1, planes, rows_y, depth)
    for tstep in range(STEPS):
        stacked = jnp.concatenate([field, cond_grid], axis=0)
        wider = extended(stacked, (("sa", 1),), 1)
        field = conduct(
            wider[:members], wider[members], first, laser_x[:, tstep], laser_y[:, tstep]
        )
    member_states = field.reshape(members, planes, columns)
    top_layer = field[:, :, :, depth - 1]
    surface = exchange_by_chip(top_layer, (("ma_0", "ma_1"), "ma_2"), (1, 0), 2, 0)
    group_rows = surface.shape[2]
    local_rows = pixel_cell % group_rows
    onehot = (
        local_rows[:, None, :] == jnp.arange(group_rows, dtype=jnp.int32)[None, :, None]
    ).astype(jnp.float32)
    seen = jnp.einsum("kxy,xyj->kxj", surface, onehot, precision=lax.Precision.HIGHEST)
    seen_mean = jnp.mean(seen, axis=0)
    seen_anom = seen - seen_mean[None]
    innovation = observed - seen_mean
    weight = 1.0 / obs_var
    gram_part = jnp.einsum(
        "kxj,lxj->kl", seen_anom * weight[None], seen_anom, precision=lax.Precision.HIGHEST
    )
    proj_part = jnp.einsum(
        "kxj,xj->k", seen_anom, weight * innovation, precision=lax.Precision.HIGHEST
    )
    gram, proj = lax.psum((gram_part, proj_part), MA_SA)
    count = gram.shape[0]
    eye = jnp.eye(count, dtype=jnp.float32)
    amat = eye + gram / (count - 1)
    factor = lower_factor(amat)
    inverse = lower_inverse(factor)
    wroot = inverse.T
    middle_sol = jnp.dot(inverse, proj, precision=lax.Precision.HIGHEST)
    wmean = jnp.dot(wroot, middle_sol, precision=lax.Precision.HIGHEST) / (count - 1)
    mix = wroot + wmean[:, None]
    done = transform(exchange_by_chip(member_states, (("ma_0", "ma_1"), "ma_2"), (1, 0), 2, 0), mix)
    return lax.all_to_all(done, MA, split_axis=0, concat_axis=2, tiled=True)


def solution(mesh):
    torus = Mesh(mesh.devices.reshape(4, 4, 2, mesh.shape["sa"]), ("ma_0", "ma_1", "ma_2", "sa"))
    in_specs = (
        P(MA, "sa", None),
        P("sa", None),
        P(MA, None),
        P(MA, None),
        P("sa", MA),
        P("sa", MA),
        P("sa", MA),
    )
    out_specs = P(MA, "sa", None)
    return jax.shard_map(
        per_device, mesh=torus, in_specs=in_specs, out_specs=out_specs, check_vma=False
    )
```

profile of v0, /device:TPU:1, one launch (start us, length us, event | category | flops | bytes accessed | tf_op | source)
XLA Modules:
  0.0 836.7 jit_solution(15582130406128456784)
XLA Ops:
  6.5 2.0 reshape.163
  8.5 7.9 reshape.162
  16.4 4.0 constant_dynamic-update-slice_fusion.1
  20.7 4.0 copy-done
  24.7 4.0 collective-permute-start
  28.7 1.3 collective-permute-start.1
  30.4 4.6 collective-permute-done
  35.0 3.8 collective-permute-done.1
  38.8 1.8 maximum_bitcast_fusion.1
  40.6 4.2 fusion.23
  44.8 31.0 %fusion.35 = f32[4,32,128,64]{3,2,1,0:T(8,128)S(1)} fusion(f32[4,32,128,64]{3,2,1,0:T(8,128)} %reshape.162, f32[4,34,128,64]{3,2,1,0:T(8,128)S(1)} %get-tuple-element.280, f32[4,34,128,64]{3,2,1,0:T(8,128)} %get-tuple-element.281, f32[5,32,128,64]{3,2,1,0:T(8,128)} %copy-done, f32[5,1,128,64]{3,2,1,0:T(8,128)S(1)} %collective-permute-done, ...), kind=kLoop, calls=%fused_computation.64 | loop fusion | flops 36700160 | bytes 52888064 | tf_op jit(solution)/shard_map/add | solution.py:88
  75.9 3.1 collective-permute-start.2
  79.0 1.5 collective-permute-start.3
  80.6 3.5 collective-permute-done.2
  84.1 3.9 collective-permute-done.3
  88.1 4.5 fusion.25
  92.6 23.1 %fusion.58 = f32[4,32,128,64]{3,2,1,0:T(8,128)} fusion(f32[4,32,128,64]{3,2,1,0:T(8,128)S(1)} %fusion.35, f32[4,34,128,64]{3,2,1,0:T(8,128)S(1)} %get-tuple-element.278, f32[4,34,128,64]{3,2,1,0:T(8,128)} %get-tuple-element.279, f32[5,1,128,64]{3,2,1,0:T(8,128)S(1)} %collective-permute-done.2, f32[1,32,128,64]{3,2,1,0:T(8,128)S(1)} %reshape.163, ...), kind=kLoop, calls=%fused_computation.87 | loop fusion | flops 38797312 | bytes 53936640 | tf_op jit(solution)/shard_map/add | solution.py:88
  115.7 8.8 %slice.196 = f32[4,32,128,1]{3,2,1,0:T(8,128)} slice(f32[4,32,128,64]{3,2,1,0:T(8,128)} %fusion.58), slice={[0:4], [0:32], [0:128], [63:64]} | slice | bytes 131072 | tf_op jit(solution)/shard_map/slice | solution.py:143
  124.5 7.6 reshape_reshape.9
  132.1 6.3 copy.31
  138.8 6.5 all_to_all.38
  145.9 0.8 reduce.1
  146.9 0.8 reshape.180
  147.7 5.8 reshape.164
  153.5 4.9 copy.28
  158.5 8.1 all_to_all.39
  166.6 7.8 all-to-all-start.3
  174.7 5.3 copy.29
  180.0 0.9 all-to-all-done.3
  180.9 5.8 all-to-all-start.1
  188.3 1.5 convolution_bitcast_fusion.3
  190.3 116.1 %psum.15 = f32[128]{0:T(128)S(1)} all-reduce(f32[128]{0:T(128)S(1)} %convolution_bitcast_fusion.6), channel_id=1, replica_groups=mesh['ma_0'=4,'ma_1'=4,'ma_2'=2,'sa'=4] {'ma_0','ma_1','ma_2','sa'}, use_global_device_ids=true, to_apply=%region_7.8 | all-reduce | flops 128 | bytes 1024 | tf_op jit(solution)/shard_map/psum | solution.py:161
  306.3 51.8 %all-reduce.6.cloned.1.call-done = f32[128,128]{1,0:T(8,128)} async-done(((f32[128,128]{1,0:T(8,128)}), f32[128,128]{1,0:T(8,128)}) %all-reduce.6.cloned.1.call-update) | async-done | bytes 65552 | tf_op jit(solution)/shard_map/psum | solution.py:161
  358.2 0.9 multiply_add_fusion
  359.1 204.1 %while.33 = (s32[]{:T(128)}, f32[128,128]{1,0:T(8,128)S(1)}, f32[128,128]{0,1:T(8,128)S(1)}, s32[]{:T(128)}, s32[]{:T(128)}) while((s32[]{:T(128)}, f32[128,128]{1,0:T(8,128)S(1)}, f32[128,128]{0,1:T(8,128)S(1)}, s32[]{:T(128)}, s32[]{:T(128)}) %tuple.86), condition=%wide.region_4.5_spmd.clone.clone, body=%wide.region_3.4_spmd.clone.clone.sunk | while | flops 246915 | bytes 332648 | solution.py:112
  563.3 187.5 %while.32 = (s32[]{:T(128)}, f32[128,128]{1,0:T(8,128)S(1)}, f32[128,128]{1,0:T(8,128)S(1)}, s32[]{:T(128)}, s32[]{:T(128)}, /*index=5*/s32[]{:T(128)}) while((s32[]{:T(128)}, f32[128,128]{1,0:T(8,128)S(1)}, f32[128,128]{1,0:T(8,128)S(1)}, s32[]{:T(128)}, s32[]{:T(128)}, /*index=5*/s32[]{:T(128)}) %tuple.89), condition=%wide.region_6.7_spmd.clone, body=%wide.region_5.6_spmd.clone.sunk | while | flops 246404 | bytes 200048 | solution.py:126
  565.3 0.7 fusion.121
  566.8 0.7 fusion.121
  574.1 0.7 fusion.121
  575.6 0.7 fusion.121
  582.9 0.7 fusion.121
  751.1 5.5 copy.39
  756.6 5.3 reshape_reshape.11
  761.9 2.8 reduce_sum.18
  764.8 5.3 fusion.88
  770.1 2.4 copy.40
  772.6 54.8 %all_to_all.40 = f32[128,32,256]{2,1,0:T(8,128)S(1)} all-to-all(f32[128,32,256]{2,1,0:T(8,128)S(1)} %copy.40), channel_id=1, replica_groups=mesh['ma_0'=4,'ma_1'=4,'ma_2'=2,'sa'=4] {'ma_0','ma_1','ma_2'}, dimensions={0} | all-to-all | bytes 8388608 | tf_op jit(solution)/shard_map/all_to_all | solution.py:172
  827.4 2.5 copy.43
  (1326 shorter events, 302.6 us)
Async XLA Ops:
  16.4 13.5 %copy-start.5 = (s32[4,2]{0,1:T(2,128)S(1)}, s32[4,2]{0,1:T(2,128)}, u32[]{:S(2)}) copy-start(s32[4,2]{0,1:T(2,128)} %param.13) | copy-start | bytes 100
  16.4 13.6 %copy-start.6 = (s32[4,2]{0,1:T(2,128)S(1)}, s32[4,2]{0,1:T(2,128)}, u32[]{:S(2)}) copy-start(s32[4,2]{0,1:T(2,128)} %param.14) | copy-start | bytes 100
  20.6 4.0 copy-start
  24.7 10.3 %collective-permute-start = (f32[5,1,128,64]{3,2,1,0:T(8,128)S(1)}, f32[5,1,128,64]{3,2,1,0:T(8,128)S(1)}, u32[]{:S(2)}, u32[]{:S(2)}) collective-permute-start(f32[5,1,128,64]{3,2,1,0:T(8,128)S(1)} %get-tuple-element.284), channel_id=1, source_target_pairs={{0,1},{1,2},{2,3},{4,5},{5,6},{6,7},{8,9},{9,10},{10,11},{12,13},{... | collective-permute-start | bytes 491528 | tf_op jit(solution)/shard_map/ppermute | solution.py:24
  28.7 10.2 %collective-permute-start.1 = (f32[5,1,128,64]{3,2,1,0:T(8,128)S(1)}, f32[5,1,128,64]{3,2,1,0:T(8,128)S(1)}, u32[]{:S(2)}, u32[]{:S(2)}) collective-permute-start(f32[5,1,128,64]{3,2,1,0:T(8,128)S(1)} %get-tuple-element.285), channel_id=1, source_target_pairs={{1,0},{2,1},{3,2},{5,4},{6,5},{7,6},{9,8},{10,9},{11,10},{13,12},{... | collective-permute-start | bytes 491528 | tf_op jit(solution)/shard_map/ppermute | solution.py:27
  30.0 10.6 %copy-start.1 = (f32[5,32,128,64]{3,2,1,0:T(8,128)S(1)}, f32[5,32,128,64]{3,2,1,0:T(8,128)}, u32[]{:S(2)}) copy-start(f32[5,32,128,64]{3,2,1,0:T(8,128)} %copy-done) | copy-start | bytes 15728644
  75.9 8.2 collective-permute-start.2
  79.0 9.0 %collective-permute-start.3 = (f32[5,1,128,64]{3,2,1,0:T(8,128)S(1)}, f32[5,1,128,64]{3,2,1,0:T(8,128)S(1)}, u32[]{:S(2)}, u32[]{:S(2)}) collective-permute-start(f32[5,1,128,64]{3,2,1,0:T(8,128)S(1)} %get-tuple-element.283), channel_id=1, source_target_pairs={{1,0},{2,1},{3,2},{5,4},{6,5},{7,6},{9,8},{10,9},{11,10},{13,12},{... | collective-permute-start | bytes 491528 | tf_op jit(solution)/shard_map/ppermute | solution.py:27
  153.5 20.9 %copy-start.4 = (s32[32,16]{0,1:T(8,128)S(1)}, s32[32,16]{0,1:T(8,128)}, u32[]{:S(2)}) copy-start(s32[32,16]{0,1:T(8,128)} %param.15) | copy-start | bytes 6148
  153.5 21.0 %copy-start.2 = (f32[32,16]{0,1:T(8,128)S(1)}, f32[32,16]{0,1:T(8,128)}, u32[]{:S(2)}) copy-start(f32[32,16]{0,1:T(8,128)} %param.17) | copy-start | bytes 6148
  153.5 21.1 %copy-start.3 = (f32[32,16]{0,1:T(8,128)S(1)}, f32[32,16]{0,1:T(8,128)}, u32[]{:S(2)}) copy-start(f32[32,16]{0,1:T(8,128)} %param.16) | copy-start | bytes 6148
  166.6 14.3 %all-to-all-start.3 = ((f32[16,1,1024]{2,1,0:T(1,128)}), f32[16,1,1024]{2,1,0:T(1,128)S(1)}, u32[]{:S(2)}, u32[]{:S(2)}) async-start(f32[16,1,1024]{2,1,0:T(1,128)} %reshape.180), calls=%async_computation.3 | async-start | bytes 131072 | tf_op jit(solution)/shard_map/all_to_all | solution.py:47
  180.9 570.2 %all-to-all-start.1 = ((f32[16,2,4,32,256]{4,2,1,3,0:T(4,128)}), f32[16,2,4,32,256]{4,2,1,3,0:T(4,128)}, u32[]{:S(2)}, u32[]{:S(2)}) async-start(f32[16,2,4,32,256]{4,2,1,3,0:T(4,128)} %copy.29), calls=%async_computation.1 | async-start | bytes 8388608 | tf_op jit(solution)/shard_map/all_to_all | solution.py:47
  186.7 171.5 %all-reduce.6.cloned.1.call-start = ((), (), s32[]{:S(2)}) async-start(), calls=%async_computation.5 | async-start | bytes 131072 | tf_op jit(solution)/shard_map/psum | solution.py:161
Sparse Core Ops, SparseCore 0:
  192.3 165.8 all-reduce.5
where the time goes:
time: 840 us; the launch traced here: 837 us
  local copies, waits for them, and re-layouts  234 us (28%)
  blocking collectives  185 us (22%)
  matrix products  124 us (15%)
  other arithmetic  97.6 us (12%)
  loops' own time  90.1 us (11%)
  waiting for transfers between devices  68.6 us (8%)
  starting transfers between devices  23.4 us (3%)
  between operations  13.8 us (2%)
    psum x1, blocking collectives, per_device(): gram, proj = lax.psum((gram_part, proj_part), MA_SA)  116 us
    dot_general x128, matrix products, row_step(): jnp.dot(row_i, inverse, precision=lax.Precision.HIGHEST)  93.3 us
    another operation x1, loops' own time, lower_factor(): return lax.fori_loop(0, count, column_step, jnp.zeros_like(amat))  85.8 us
    dynamic_slice x128, local copies, waits for them, and re-layouts, column_step(): pivot = jnp.sqrt(lax.dynamic_slice_in_dim(rest, index_j, 1, 0)[0])  82.4 us
    dynamic_slice x128, local copies, waits for them, and re-layouts, row_step(): pivot = lax.dynamic_slice_in_dim(row_i, index_i, 1, 0)[0]  76.3 us
    all_to_all x1, blocking collectives, per_device(): return lax.all_to_all(done, MA, split_axis=0, concat_axis=2, tiled=True)  54.8 us
    add x2, other arithmetic, conduct(): return centre + step_dt * (flux + heat)  54.1 us
    psum x1, waiting for transfers between devices, per_device(): gram, proj = lax.psum((gram_part, proj_part), MA_SA)  51.8 us
  transfers between devices with their start and end apart: 7, of which 6 were waited for; matrix products, arithmetic and copies ran while one was open for 37% of the time, Pallas kernels for 0%

commit v1 on v0

v1 whole, which is shorter than its diff:
```python
import functools

import jax
import jax.numpy as jnp
from jax import lax
from jax.experimental import pallas as pl
from jax.experimental.pallas import tpu as pltpu
from jax.sharding import Mesh
from jax.sharding import PartitionSpec as P

DEPTH = 64
STEPS = 2
LANES = 128
MA = ("ma_0", "ma_1", "ma_2")
MA_SA = ("ma_0", "ma_1", "ma_2", "sa")

step_dt = 0.025
alpha_cond = 0.05
laser_power = 12.0
beam_spot_width = 18.0

HALO_TILE = 8


def _roll(x, shift, axis):
    return pltpu.roll(x, shift, axis)


def _stencil_step(src, cond, row_first, tiles, edges, exs, ey_at, emit, extra):
    lane = lax.broadcasted_iota(jnp.int32, (8, LANES), 1)
    sub = lax.broadcasted_iota(jnp.int32, (8, LANES), 0)
    low_half = lane < DEPTH
    zpos = lane & (DEPTH - 1)
    z_last = zpos == DEPTH - 1
    z_first = zpos == 0
    sub_last = sub == 7
    sub_first = sub == 0
    pairs = (src.shape[1] - LANES) // (2 * LANES)

    def load(row, v):
        cols = pl.ds(pl.multiple_of(v * LANES, LANES), LANES)
        u = src[pl.ds(row, 8), cols]
        k = cond[pl.ds(row, 8), cols]
        return u, k * (1.0 + alpha_cond * (u * u))

    rows = [row_first + 8 * i for i in range(tiles)]
    first = [load(r, 0) for r in rows]
    us = [a for a, _ in first]
    ks = [b for _, b in first]
    rus = [_roll(a, DEPTH, 1) for a in us]
    rks = [_roll(b, DEPTH, 1) for b in ks]
    rfs = [a * b for a, b in first]

    def one(v, half, d, carry):
        us, ks, rus, rks, rfs, ext = carry
        nxt = [load(r, v + 1) for r in rows]
        run = [_roll(a, DEPTH, 1) for a, _ in nxt]
        rkn = [_roll(b, DEPTH, 1) for _, b in nxt]
        if edges:
            ul, kl = load(row_first - 8, v)
            uh, kh = load(row_first + 8 * tiles, v)
            ux, kx = [ul] + us + [uh], [kl] + ks + [kh]
        else:
            ux, kx = us, ks
        rot_u = [_roll(a, 7, 0) for a in ux]
        rot_k = [_roll(a, 7, 0) for a in kx]
        fx, rfx = [], []
        count = len(ux)
        for i in range(count - 1 if edges else count):
            j = min(i + 1, count - 1)
            xp = jnp.where(sub_last, rot_u[j], rot_u[i])
            kp = jnp.where(sub_last, rot_k[j], rot_k[i])
            face = (kx[i] + kp) * (xp - ux[i])
            fx.append(face)
            rfx.append(_roll(face, 1, 0))
        shift = 1 if edges else 0
        new_rfs = []
        ey = ey_at(v)
        for i in range(tiles):
            u, k = us[i], ks[i]
            yp = jnp.where(low_half, rus[i], run[i])
            kyp = jnp.where(low_half, rks[i], rkn[i])
            fy = (k + kyp) * (yp - u)
            rfy = _roll(fy, DEPTH, 1)
            new_rfs.append(rfy)
            acc = fy - jnp.where(low_half, rfs[i], rfy)
            zp = jnp.where(z_last, 0.0, _roll(u, LANES - 1, 1))
            kzp = jnp.where(z_last, 0.0, _roll(k, LANES - 1, 1))
            fz = (k + kzp) * (zp - u)
            acc = acc + (fz - jnp.where(z_first, k * u, _roll(fz, 1, 1)))
            below = rfx[max(i + shift - 1, 0)]
            acc = acc + (fx[i + shift] - jnp.where(sub_first, below, rfx[i + shift]))
            new = u + (0.5 * step_dt) * acc + exs[i] * ey
            ext = emit(d, v, half, i, new, ext)
        return [a for a, _ in nxt], [b for _, b in nxt], run, rkn, new_rfs, ext

    def pair(d, carry):
        carry = one(2 * d, 0, d, carry)
        return one(2 * d + 1, 1, d, carry)

    carry = lax.fori_loop(0, pairs, pair, (us, ks, rus, rks, rfs, extra))
    return carry[-1]


def _forecast_body(
    planes, u_ref, c_ref, lo_ref, hi_ref, clo_ref, chi_ref, ex_ref, ey_ref, pc_ref, obs_ref, var_ref,
    out_ref, surf_ref, e_ref, ce_ref, u1_ref,
):
    m = pl.program_id(0)
    columns = u_ref.shape[2]
    main = pl.ds(HALO_TILE, planes)
    low = pl.ds(HALO_TILE - 2, 2)
    high = pl.ds(HALO_TILE + planes, 2)
    body = pl.ds(0, columns)
    lane = lax.broadcasted_iota(jnp.int32, (8, LANES), 1)
    insert = (lane & (DEPTH - 1)) == DEPTH - 1
    tiles = planes // 8

    @pl.when(m == 0)
    def _():
        for ref in (e_ref, ce_ref, u1_ref):
            ref[pl.ds(0, HALO_TILE), :] = jnp.zeros((HALO_TILE, ref.shape[1]), jnp.float32)
            ref[pl.ds(HALO_TILE + planes, HALO_TILE), :] = jnp.zeros((HALO_TILE, ref.shape[1]), jnp.float32)
            ref[main, pl.ds(columns, LANES)] = jnp.zeros((planes, LANES), jnp.float32)
        ce_ref[main, body] = c_ref[...]
        ce_ref[low, body] = clo_ref[0]
        ce_ref[high, body] = chi_ref[0]
        wide = lax.broadcasted_iota(jnp.int32, (planes, LANES), 1)
        cell = jnp.where(wide < DEPTH, 2 * wide, 2 * wide - (LANES - 1))
        weight = 1.0 / var_ref[...]
        value = weight * obs_ref[...]
        pc = pc_ref[...]
        wsum = jnp.zeros((planes, LANES), jnp.float32)
        rsum = jnp.zeros((planes, LANES), jnp.float32)
        for j in range(pc.shape[1]):
            hit = pc[:, j : j + 1] == cell
            wsum = wsum + jnp.where(hit, weight[:, j : j + 1], 0.0)
            rsum = rsum + jnp.where(hit, value[:, j : j + 1], 0.0)
        surf_ref[:, 4, :] = wsum
        surf_ref[:, 5, :] = rsum
        surf_ref[:, 6, :] = jnp.zeros((planes, LANES), jnp.float32)
        surf_ref[:, 7, :] = jnp.zeros((planes, LANES), jnp.float32)

    e_ref[main, body] = u_ref[0]
    e_ref[low, body] = lo_ref[0]
    e_ref[high, body] = hi_ref[0]

    def ey_row(t):
        def at(v):
            cols = pl.ds(pl.multiple_of(v * LANES, LANES), LANES)
            return ey_ref[0, pl.ds(t, 1), cols]

        return at

    def emit1(d, v, half, i, new, ext):
        cols = pl.ds(pl.multiple_of(v * LANES, LANES), LANES)
        rows = pl.ds(8 * i, 8)
        if i == 0 or i == tiles + 1:
            new = jnp.where(ce_ref[rows, cols] > 0.0, new, 0.0)
        u1_ref[rows, cols] = new
        return ext

    ex1 = [ex_ref[0, 0, pl.ds(8 * i, 8), :] for i in range(tiles + 2)]
    _stencil_step(e_ref, ce_ref, 0, tiles + 2, False, ex1, ey_row(0), emit1, ())

    def emit2(d, v, half, i, new, ext):
        out_ref[d, 0, pl.ds(8 * i, 8), pl.ds(half * LANES, LANES)] = new
        ext = list(ext)
        ext[i] = jnp.where(insert, new, _roll(ext[i], LANES - 1, 1))
        return tuple(ext)

    ex2 = [ex_ref[0, 1, pl.ds(8 * (i + 1), 8), :] for i in range(tiles)]
    start = tuple(jnp.zeros((8, LANES), jnp.float32) for _ in range(tiles))
    surface = _stencil_step(u1_ref, ce_ref, HALO_TILE, tiles, True, ex2, ey_row(1), emit2, start)
    for k in range(4):

        @pl.when(m == k)
        def _():
            for i in range(tiles):
                surf_ref[pl.ds(8 * i, 8), k, :] = surface[i]


def forecast(u, cond, low, high, ex, ey, pixel_cell, observed, obs_var, blocks):
    members, planes, columns = u.shape
    per = columns // blocks
    ext = planes + 2 * HALO_TILE
    whole = lambda shape: pl.BlockSpec(shape, lambda m: (0,) * len(shape))
    scratch = pltpu.VMEM((ext, columns + LANES), jnp.float32)
    pix = pixel_cell.shape
    return pl.pallas_call(
        functools.partial(_forecast_body, planes),
        grid=(members,),
        in_specs=[
            pl.BlockSpec((1, planes, columns), lambda m: (m, 0, 0)),
            whole((planes, columns)),
            pl.BlockSpec((1, 2, columns), lambda m: (m, 0, 0)),
            pl.BlockSpec((1, 2, columns), lambda m: (m, 0, 0)),
            pl.BlockSpec((1, 2, columns), lambda m: (members, 0, 0)),
            pl.BlockSpec((1, 2, columns), lambda m: (members, 0, 0)),
            pl.BlockSpec((1, STEPS, ext, LANES), lambda m: (m, 0, 0, 0)),
            pl.BlockSpec((1, STEPS, columns), lambda m: (m, 0, 0)),
            whole(pix),
            whole(pix),
            whole(pix),
        ],
        out_specs=[
            pl.BlockSpec((blocks, 1, planes, per), lambda m: (0, m, 0, 0)),
            whole((planes, 8, LANES)),
        ],
        out_shape=[
            jax.ShapeDtypeStruct((blocks, members, planes, per), jnp.float32),
            jax.ShapeDtypeStruct((planes, 8, LANES), jnp.float32),
        ],
        scratch_shapes=[scratch, scratch, scratch],
        compiler_params=pltpu.CompilerParams(
            dimension_semantics=("arbitrary",), vmem_limit_bytes=32 << 20
        ),
        cost_estimate=pl.CostEstimate(flops=200_000_000, bytes_accessed=10_000_000, transcendentals=0),
        name="forecast",
    )(u, cond, low, high, low, high, ex, ey, pixel_cell, observed, obs_var)


def _nt(a, b):
    return lax.dot_general(
        a, b, (((1,), (1,)), ((), ())), precision=lax.Precision.HIGHEST, preferred_element_type=jnp.float32
    )


def _member_rows(ref, full_ref, groups):
    for k in range(4):
        full_ref[pl.ds(k, groups, stride=4), :] = ref[pl.ds(k, groups, stride=8), :]


def _gram_body(recv_ref, out_ref, s_ref):
    groups = recv_ref.shape[0] // 8
    count = groups * 4
    _member_rows(recv_ref, s_ref, groups)
    wsum = jnp.sum(recv_ref[pl.ds(4, groups, stride=8), :], axis=0, keepdims=True)
    rsum = jnp.sum(recv_ref[pl.ds(5, groups, stride=8), :], axis=0, keepdims=True)
    s = s_ref[...]
    mean = jnp.sum(s, axis=0, keepdims=True) * (1.0 / count)
    anom = s - mean
    gram = _nt(anom * wsum, anom)
    q = rsum - wsum * mean
    proj = _nt(jnp.broadcast_to(q, (8, LANES)), anom)
    s_ref[...] = gram
    for k in range(4):
        out_ref[pl.ds(k, groups, stride=8), :] = s_ref[pl.ds(k, groups, stride=4), :]
    for k in range(4, 8):
        out_ref[pl.ds(k, groups, stride=8), :] = jnp.broadcast_to(proj[0:1], (groups, LANES))


def gram_message(recv):
    rows = recv.shape[0]
    return pl.pallas_call(
        _gram_body,
        out_shape=jax.ShapeDtypeStruct((rows, LANES), jnp.float32),
        scratch_shapes=[pltpu.VMEM((rows // 2, LANES), jnp.float32)],
        cost_estimate=pl.CostEstimate(flops=40_000_000, bytes_accessed=300_000, transcendentals=0),
        name="gram",
    )(recv)


def _total_body(recv_ref, out_ref):
    total = recv_ref[0]
    for i in range(1, recv_ref.shape[0]):
        total = total + recv_ref[i]
    for i in range(out_ref.shape[0]):
        out_ref[i] = total


def total_message(recv, copies):
    return pl.pallas_call(
        _total_body,
        out_shape=jax.ShapeDtypeStruct((copies,) + recv.shape[1:], jnp.float32),
        cost_estimate=pl.CostEstimate(flops=100_000, bytes_accessed=700_000, transcendentals=0),
        name="total",
    )(recv)


GROUP = 4


def _mix_body(recv_ref, hi_ref, lo_ref, a_ref, rows_ref):
    groups, slabs = recv_ref.shape[0], recv_ref.shape[1]
    count = 4 * groups
    for g in range(groups):
        total = recv_ref[g, 0]
        for s in range(1, slabs):
            total = total + recv_ref[g, s]
        rows_ref[pl.ds(8 * g, 8), :] = total
    _member_rows(rows_ref, a_ref, groups)
    proj = rows_ref[pl.ds(4, 1), :]
    ntile = count // 8
    sub = lax.broadcasted_iota(jnp.int32, (8, LANES), 0)
    lane = lax.broadcasted_iota(jnp.int32, (8, LANES), 1)
    a, inv, diag = [], [], []
    for i in range(ntile):
        eye = (lane == sub + 8 * i).astype(jnp.float32)
        a.append(eye + a_ref[pl.ds(8 * i, 8), :] * (1.0 / (count - 1)))
        inv.append(eye)
        diag.append(jnp.ones((8, LANES), jnp.float32))

    def row_of(tile, r):
        return jnp.broadcast_to(tile[r : r + 1, :], (8, LANES))

    for j0 in range(0, count, GROUP):
        base = j0 // 8
        cols = [
            {i: jnp.broadcast_to(a[i][:, j0 + t : j0 + t + 1], (8, LANES)) for i in range(base, ntile)}
            for t in range(GROUP)
        ]
        r0 = j0 % 8
        arow = [row_of(a[base], r0 + t) for t in range(GROUP)]
        irow = [row_of(inv[base], r0 + t) for t in range(GROUP)]
        for t in range(GROUP):
            pivot = row_of(cols[t][base], r0 + t)
            recip = 1.0 / pivot
            diag[base] = jnp.where(sub == r0 + t, pivot, diag[base])
            for s in range(t + 1, GROUP):
                factor = row_of(cols[t][base], r0 + s) * recip
                for i in range(base, ntile):
                    cols[s][i] = cols[s][i] - factor * cols[t][i]
                arow[s] = arow[s] - factor * arow[t]
                irow[s] = irow[s] - factor * irow[t]
            arow[t] = arow[t] * recip
            irow[t] = irow[t] * recip
            cols[t][base] = jnp.where(sub > r0 + t, cols[t][base], 0.0)
        for i in range(base, ntile):
            for t in range(GROUP):
                a[i] = a[i] - cols[t][i] * arow[t]
                inv[i] = inv[i] - cols[t][i] * irow[t]
    for i in range(ntile):
        a_ref[pl.ds(8 * i, 8), :] = inv[i] / jnp.sqrt(diag[i])
    linv = a_ref[...]
    middle = _nt(jnp.broadcast_to(proj, (8, LANES)), linv)
    wmean = lax.dot_general(
        middle, linv, (((1,), (0,)), ((), ())), precision=lax.Precision.HIGHEST, preferred_element_type=jnp.float32
    ) * (1.0 / (count - 1))
    mix = linv + wmean[0:1]
    mix = mix + (1.0 - jnp.sum(mix, axis=1, keepdims=True)) * (1.0 / count)
    hi = mix.astype(jnp.bfloat16)
    hi_ref[...] = hi
    lo_ref[...] = (mix - hi.astype(jnp.float32)).astype(jnp.bfloat16)


def mix_matrices(recv):
    groups = recv.shape[0]
    count = 4 * groups
    shape = jax.ShapeDtypeStruct((count, count), jnp.bfloat16)
    return pl.pallas_call(
        _mix_body,
        out_shape=[shape, shape],
        scratch_shapes=[
            pltpu.VMEM((count, LANES), jnp.float32),
            pltpu.VMEM((2 * count, LANES), jnp.float32),
        ],
        cost_estimate=pl.CostEstimate(flops=200_000_000, bytes_accessed=600_000, transcendentals=0),
        name="mix",
    )(recv)


def _transform_body(f_ref, hi_ref, lo_ref, out_ref):
    count = hi_ref.shape[0]
    hi = hi_ref[...]
    lo = lo_ref[...]
    src = f_ref.reshape(count * 8, LANES)
    dst = out_ref.reshape(count * 8, LANES)
    for x in range(8):
        rows = pl.ds(x, count, stride=8)
        f = src[rows, :]
        fhi = f.astype(jnp.bfloat16)
        flo = (f - fhi.astype(jnp.float32)).astype(jnp.bfloat16)
        out = jnp.dot(hi, fhi, preferred_element_type=jnp.float32)
        out = out + jnp.dot(hi, flo, preferred_element_type=jnp.float32)
        out = out + jnp.dot(lo, fhi, preferred_element_type=jnp.float32)
        dst[rows, :] = out


def transform(block, hi, lo):
    count, planes, per = block.shape
    spec = pl.BlockSpec((count, 8, LANES), lambda x, c: (0, x, c))
    mat = pl.BlockSpec((count, count), lambda x, c: (0, 0))
    return pl.pallas_call(
        _transform_body,
        grid=(planes // 8, per // LANES),
        in_specs=[spec, mat, mat],
        out_specs=spec,
        out_shape=jax.ShapeDtypeStruct(block.shape, jnp.float32),
        compiler_params=pltpu.CompilerParams(
            dimension_semantics=("arbitrary", "arbitrary"), vmem_limit_bytes=32 << 20
        ),
        cost_estimate=pl.CostEstimate(flops=900_000_000, bytes_accessed=8_500_000, transcendentals=0),
        name="transform",
    )(block, hi, lo)


def heat_factors(laser_x, laser_y, first, planes, columns):
    xs = first - HALO_TILE + jnp.arange(planes + 2 * HALO_TILE, dtype=jnp.int32)
    dx = (xs[None, None, :] - laser_x[:, :, None]).astype(jnp.float32)
    ex = (step_dt * laser_power) * jnp.exp(-(dx * dx) / beam_spot_width)
    ex = jnp.broadcast_to(ex[..., None], ex.shape + (LANES,))
    col = jnp.arange(columns, dtype=jnp.int32)
    dy = (col // DEPTH - laser_y[:, :, None]).astype(jnp.float32)
    ey = jnp.where(col % DEPTH == DEPTH - 1, jnp.exp(-(dy * dy) / beam_spot_width), 0.0)
    return ex, ey


def per_device(initial_heat_matrix, conductivity, laser_x, laser_y, pixel_cell, observed, obs_var):
    members, planes, columns = initial_heat_matrix.shape
    blocks = 1
    for axis in MA:
        blocks *= lax.axis_size(axis)
    slabs = lax.axis_size("sa")
    first = lax.axis_index("sa") * planes
    u = initial_heat_matrix
    forward = [(i, i + 1) for i in range(slabs - 1)]
    backward = [(b, a) for a, b in forward]
    top = jnp.concatenate([u[:, planes - 2 :], conductivity[None, planes - 2 :]], axis=0)
    bottom = jnp.concatenate([u[:, :2], conductivity[None, :2]], axis=0)
    low = lax.ppermute(top, "sa", forward)
    high = lax.ppermute(bottom, "sa", backward)
    ex, ey = heat_factors(laser_x, laser_y, first, planes, columns)
    sent, surf = forecast(u, conductivity, low, high, ex, ey, pixel_cell, observed, obs_var, blocks)

    seen = lax.all_to_all(surf, MA, 0, 0, tiled=True)
    rows = gram_message(seen.reshape(blocks * 8, LANES))
    mine = lax.all_to_all(rows.reshape(blocks, 8, LANES), MA, 0, 0, tiled=True)
    copies = total_message(mine, blocks * slabs)
    every = lax.all_to_all(copies, MA_SA, 0, 0, tiled=True)
    hi, lo = mix_matrices(every.reshape(blocks, slabs, 8, LANES))

    held = lax.all_to_all(sent, MA, 0, 0, tiled=True)
    done = transform(held.reshape(blocks * members, planes, columns // blocks), hi, lo)
    back = lax.all_to_all(done.reshape(held.shape), MA, 0, 0, tiled=True)
    return back.transpose(1, 2, 0, 3).reshape(members, planes, columns)


def solution(mesh):
    torus = Mesh(mesh.devices.reshape(4, 4, 2, mesh.shape["sa"]), ("ma_0", "ma_1", "ma_2", "sa"))
    in_specs = (
        P(MA, "sa", None),
        P("sa", None),
        P(MA, None),
        P(MA, None),
        P("sa", MA),
        P("sa", MA),
        P("sa", MA),
    )
    out_specs = P(MA, "sa", None)
    return jax.shard_map(
        per_device, mesh=torus, in_specs=in_specs, out_specs=out_specs, check_vma=False
    )
```

time: 840 us -> 258 us (0.31)
  local copies, waits for them, and re-layouts: 234 us -> 15.4 us
  matrix products: 124 us -> 0 us
  other arithmetic: 97.6 us -> 1.42 us
  loops' own time: 90.1 us -> 0 us
  blocking collectives: 185 us -> 107 us
  Pallas kernels: 0 us -> 74.2 us
  waiting for transfers between devices: 68.6 us -> 48.8 us
  between operations: 13.8 us -> 0.13 us
  starting transfers between devices: 23.4 us -> 9.94 us
    dynamic_slice x256 -> x0, local copies, waits for them, and re-layouts: 159 us -> none  [the longest x128 82.4 us: column_step(): pivot = jnp.sqrt(lax.dynamic_slice_in_dim(rest, index_j, 1, 0)[0])]
    dot_general x262 -> x0, matrix products: 124 us -> none  [the longest x128 93.3 us: row_step(): jnp.dot(row_i, inverse, precision=lax.Precision.HIGHEST)]
    psum x1 -> x0, blocking collectives: 116 us -> none  [per_device(): gram, proj = lax.psum((gram_part, proj_part), MA_SA)]
    another operation x2 -> x0, loops' own time: 90.1 us -> none  [the longest x1 85.8 us: lower_factor(): return lax.fori_loop(0, count, column_step, jnp.zeros_like(amat))]
    pallas_call x0 -> x5, Pallas kernels: none -> 74.2 us  [the longest x1 55.9 us: forecast(): pl.pallas_call(functools.partial(_forecast_body, planes), grid=(members,)...]
    add x4 -> x1, other arithmetic: 54.9 us -> 0.01 us  [heat_factors(): xs = first - HALO_TILE + jnp.arange(planes + 2 * HALO_TILE, dtype=jnp.int32)]
    psum x1 -> x0, waiting for transfers between devices: 51.8 us -> none  [per_device(): gram, proj = lax.psum((gram_part, proj_part), MA_SA)]
    all_to_all x2 -> x1, waiting for transfers between devices: 0.94 us -> 44.2 us  [per_device(): held = lax.all_to_all(sent, MA, 0, 0, tiled=True)]
  transfers between devices with their start and end apart: 7 -> 3, of which waited for: 6 -> 3; matrix products, arithmetic and copies ran while one was open for 37% -> 2% of each run, Pallas kernels for 0% -> 3%
where the time goes in v1:
time: 258 us; the launch traced here: 257 us
  blocking collectives  107 us (41%)
  Pallas kernels  74.2 us (29%)
  waiting for transfers between devices  48.8 us (19%)
  local copies, waits for them, and re-layouts  15.4 us (6%)
  starting transfers between devices  9.94 us (4%)
    all_to_all x1, blocking collectives, per_device(): back = lax.all_to_all(done.reshape(held.shape), MA, 0, 0, tiled=True)  57.5 us
    pallas_call x1, Pallas kernels, forecast(): pl.pallas_call(functools.partial(_forecast_body, planes), grid=(members,)...  55.9 us
    all_to_all x1, waiting for transfers between devices, per_device(): held = lax.all_to_all(sent, MA, 0, 0, tiled=True)  44.2 us
    all_to_all x1, blocking collectives, per_device(): every = lax.all_to_all(copies, MA_SA, 0, 0, tiled=True)  19.6 us
    all_to_all x1, blocking collectives, per_device(): seen = lax.all_to_all(surf, MA, 0, 0, tiled=True)  17.6 us
    all_to_all x1, blocking collectives, per_device(): mine = lax.all_to_all(rows.reshape(blocks, 8, LANES), MA, 0, 0, tiled=True)  12.4 us
    unnamed x14, local copies, waits for them, and re-layouts  10 us
    pallas_call x1, Pallas kernels, mix_matrices(): pl.pallas_call(_mix_body, out_shape=[shape, shape], scratch_shapes=[pltpu...  8.05 us
  transfers between devices with their start and end apart: 3, of which 3 were waited for; matrix products, arithmetic and copies ran while one was open for 2% of the time, Pallas kernels for 3%

profile of v1, /device:TPU:1, one launch (start us, length us, event | category | flops | bytes accessed | tf_op | source)
XLA Modules:
  0.0 257.1 jit_solution(1277371300705020509)
XLA Ops:
  0.0 1.7 fusion.6
  1.7 1.1 slice_bitcast_fusion
  2.8 0.2 pad_maximum_fusion
  3.0 4.0 %collective-permute-start = (f32[5,2,8192]{2,1,0:T(2,128)S(1)}, f32[5,2,8192]{2,1,0:T(2,128)S(1)}, u32[]{:S(2)}, u32[]{:S(2)}) collective-permute-start(f32[5,2,8192]{2,1,0:T(2,128)S(1)} %pad_maximum_fusion), channel_id=1, source_target_pairs={{0,1},{1,2},{2,3},{4,5},{5,6},{6,7},{8,9},{9,10},{10,11},{12,13},{... | collective-permute-start | bytes 983048 | tf_op jit(solution)/shard_map/ppermute | solution.py:421
  6.9 0.2 pad_maximum_fusion.1
  7.1 1.3 collective-permute-start.1
  8.4 0.8 copy.15
  9.2 0.3 exponential_select_fusion.ey_ref
  9.6 0.8 exponential_multiply_fusion
  10.3 0.8 copy.16.pc_ref
  11.1 0.8 copy.17.obs_ref
  11.9 0.8 copy.18.var_ref
  12.6 0.6 collective-permute-done.lo_ref.clo_ref
  13.3 4.0 %collective-permute-done.1.hi_ref.chi_ref = f32[5,2,8192]{2,1,0:T(2,128)S(1)} collective-permute-done((f32[5,2,8192]{2,1,0:T(2,128)S(1)}, f32[5,2,8192]{2,1,0:T(2,128)S(1)}, u32[]{:S(2)}, u32[]{:S(2)}) %collective-permute-start.1) | collective-permute-done | bytes 327712 | tf_op jit(solution)/shard_map/ppermute | solution.py:422
  17.3 0.1 broadcast_in_dim.26.ex_ref
  17.4 0.0 copy-start
  17.4 2.2 copy-done
  19.6 0.0 copy-start.2
  19.6 1.2 copy-done.2
  20.8 55.9 %forecast.1 = (f32[32,4,32,256]{3,2,1,0:T(8,128)S(1)}, f32[32,8,128]{2,1,0:T(8,128)S(1)}) custom-call(f32[4,32,8192]{2,1,0:T(8,128)S(1)} %copy-done, f32[32,8192]{1,0:T(8,128)S(1)} %copy-done.2, f32[5,2,8192]{2,1,0:T(2,128)S(1)} %collective-permute-done.lo_ref.clo_ref, f32[5,2,8192]{2,1,0:T(2,128)S(1)} %collective-permute-done.1.hi_ref.chi_ref, ...), custom_call_target="tpu_custom_call" | custom-call | flops 200000000 | bytes 10000000 | tf_op jit(solution)/shard_map/forecast/pallas_call | solution.py:190
  76.7 0.0 copy-start.1
  76.7 2.0 copy-done.1
  78.7 17.6 %all_to_all.25 = f32[32,8,128]{2,1,0:T(8,128)} all-to-all(f32[32,8,128]{2,1,0:T(8,128)S(1)} %get-tuple-element.10), channel_id=1, replica_groups=mesh['ma_0'=4,'ma_1'=4,'ma_2'=2,'sa'=4] {'ma_0','ma_1','ma_2'}, dimensions={0} | all-to-all | bytes 262144 | tf_op jit(solution)/shard_map/all_to_all | solution.py:426
  96.3 2.0 gram.1
  98.2 12.4 %all_to_all.26.recv_ref = f32[32,8,128]{2,1,0:T(8,128)} all-to-all(f32[32,8,128]{2,1,0:T(8,128)} %bitcast.16), channel_id=1, replica_groups=mesh['ma_0'=4,'ma_1'=4,'ma_2'=2,'sa'=4] {'ma_0','ma_1','ma_2'}, dimensions={0} | all-to-all | bytes 262144 | tf_op jit(solution)/shard_map/all_to_all | solution.py:428
  110.6 1.8 total.1
  112.4 19.6 %all_to_all.27 = f32[128,8,128]{2,1,0:T(8,128)} all-to-all(f32[128,8,128]{2,1,0:T(8,128)} %total.1), channel_id=1, replica_groups=mesh['ma_0'=4,'ma_1'=4,'ma_2'=2,'sa'=4] {'ma_0','ma_1','ma_2','sa'}, dimensions={0} | all-to-all | bytes 1048576 | tf_op jit(solution)/shard_map/all_to_all | solution.py:430
  132.0 4.7 %all-to-all-start = ((f32[32,4,32,256]{3,2,1,0:T(8,128)}), f32[32,4,32,256]{3,2,1,0:T(8,128)}, u32[]{:S(2)}, u32[]{:S(2)}) async-start(f32[32,4,32,256]{3,2,1,0:T(8,128)} %copy-done.1), calls=%async_computation | async-start | bytes 8388608 | tf_op jit(solution)/shard_map/all_to_all | solution.py:433
  136.7 8.1 %mix.1 = (bf16[128,128]{1,0:T(8,128)(2,1)}, bf16[128,128]{1,0:T(8,128)(2,1)}) custom-call(f32[32,4,8,128]{3,2,1,0:T(8,128)} %bitcast.14), custom_call_target="tpu_custom_call" | custom-call | flops 200000000 | bytes 600000 | tf_op jit(solution)/shard_map/mix/pallas_call | solution.py:351
  144.8 44.2 %all-to-all-done = f32[32,4,32,256]{3,2,1,0:T(8,128)} async-done(((f32[32,4,32,256]{3,2,1,0:T(8,128)}), f32[32,4,32,256]{3,2,1,0:T(8,128)}, u32[]{:S(2)}, u32[]{:S(2)}) %all-to-all-start) | async-done | bytes 4194336 | tf_op jit(solution)/shard_map/all_to_all | solution.py:433
  189.0 0.0 copy-start.3
  189.0 0.8 copy-done.3
  189.7 0.0 copy-start.4
  189.8 0.8 copy-done.4
  190.5 6.5 %transform.1 = f32[128,32,256]{2,1,0:T(8,128)S(1)} custom-call(f32[128,32,256]{2,1,0:T(8,128)} %bitcast.2.f_ref, bf16[128,128]{1,0:T(8,128)(2,1)S(1)} %copy-done.3, bf16[128,128]{1,0:T(8,128)(2,1)S(1)} %copy-done.4), custom_call_target="tpu_custom_call" | custom-call | flops 900000000 | bytes 8500000 | tf_op jit(solution)/shard_map/transform/pallas_call | solution.py:384
  197.1 57.5 %all_to_all.28 = f32[32,4,32,256]{3,2,1,0:T(8,128)S(1)} all-to-all(f32[32,4,32,256]{3,2,1,0:T(8,128)S(1)} %bitcast.12), channel_id=1, replica_groups=mesh['ma_0'=4,'ma_1'=4,'ma_2'=2,'sa'=4] {'ma_0','ma_1','ma_2'}, dimensions={0} | all-to-all | bytes 8388608 | tf_op jit(solution)/shard_map/all_to_all | solution.py:435
  254.6 2.5 copy.20
  (4 shorter events, 0.0 us)
Async XLA Ops:
  3.0 10.3 %collective-permute-start = (f32[5,2,8192]{2,1,0:T(2,128)S(1)}, f32[5,2,8192]{2,1,0:T(2,128)S(1)}, u32[]{:S(2)}, u32[]{:S(2)}) collective-permute-start(f32[5,2,8192]{2,1,0:T(2,128)S(1)} %pad_maximum_fusion), channel_id=1, source_target_pairs={{0,1},{1,2},{2,3},{4,5},{5,6},{6,7},{8,9},{9,10},{10,11},{12,13},{... | collective-permute-start | bytes 983048 | tf_op jit(solution)/shard_map/ppermute | solution.py:421
  7.1 10.2 %collective-permute-start.1 = (f32[5,2,8192]{2,1,0:T(2,128)S(1)}, f32[5,2,8192]{2,1,0:T(2,128)S(1)}, u32[]{:S(2)}, u32[]{:S(2)}) collective-permute-start(f32[5,2,8192]{2,1,0:T(2,128)S(1)} %pad_maximum_fusion.1), channel_id=1, source_target_pairs={{1,0},{2,1},{3,2},{5,4},{6,5},{7,6},{9,8},{10,9},{11,10},{13,12},{... | collective-permute-start | bytes 983048 | tf_op jit(solution)/shard_map/ppermute | solution.py:422
  17.4 2.2 copy-start
  19.6 1.2 copy-start.2
  76.7 2.0 copy-start.1
  132.0 57.0 %all-to-all-start = ((f32[32,4,32,256]{3,2,1,0:T(8,128)}), f32[32,4,32,256]{3,2,1,0:T(8,128)}, u32[]{:S(2)}, u32[]{:S(2)}) async-start(f32[32,4,32,256]{3,2,1,0:T(8,128)} %copy-done.1), calls=%async_computation | async-start | bytes 8388608 | tf_op jit(solution)/shard_map/all_to_all | solution.py:433
  189.0 0.8 copy-start.3
  189.7 0.8 copy-start.4

commit v2 on v1

v2 whole, which is shorter than its diff:
```python
import functools

import jax
import jax.numpy as jnp
from jax import lax
from jax.experimental import pallas as pl
from jax.experimental.pallas import tpu as pltpu
from jax.sharding import Mesh
from jax.sharding import PartitionSpec as P

DEPTH = 64
STEPS = 2
LANES = 128
MA = ("ma_0", "ma_1", "ma_2")
MA_SA = ("ma_0", "ma_1", "ma_2", "sa")

step_dt = 0.025
alpha_cond = 0.05
laser_power = 12.0
beam_spot_width = 18.0

def _roll(x, shift, axis):
    return pltpu.roll(x, shift, axis)


def _wide_pair(a, b, low_half):
    return jnp.where(low_half, a, _roll(b, DEPTH, 1)), jnp.where(low_half, _roll(a, DEPTH, 1), b)


ROWS = 48
FIRST_ROW = 8
UNROLL = 4
FILL_UNROLL = 8
CHUNK = 5


def _stencil_step(src, cond, base, tiles, exs, ey_at, emit, extra):
    lane = lax.broadcasted_iota(jnp.int32, (8, LANES), 1)
    low_half = lane < DEPTH
    zpos = lane & (DEPTH - 1)
    z_last = zpos == DEPTH - 1
    z_first = zpos == 0

    def load(y, i):
        at = pl.ds(y * ROWS + (base + i), 8, stride=tiles)
        u = src[at, :]
        c = cond[at, :]
        return u, c + c * (alpha_cond * (u * u))

    def face(one, two):
        return (one[1] + two[1]) * (two[0] - one[0])

    results = []
    for i0 in range(0, tiles, CHUNK):
        some = range(i0, min(i0 + CHUNK, tiles))
        here, fys = [], []
        for i in some:
            u, k = load(DEPTH - 1, i)
            before = (
                jnp.where(low_half, 0.0, _roll(u, DEPTH, 1)),
                jnp.where(low_half, 0.0, _roll(k, DEPTH, 1)),
            )
            here.append(load(0, i))
            fys.append(face(before, here[-1]))

        def one(y, carry, some=some):
            here, fys, ext = carry
            after = [load(y + 1, i) for i in some]
            line = [load(y, some[0] - 1)] + list(here) + [load(y, some[-1] + 1)]
            ey = jnp.broadcast_to(ey_at(y), (8, LANES))
            fx = face(line[0], line[1])
            new_fys, values = [], []
            for j, i in enumerate(some):
                u, k = here[j]
                fy = face(here[j], after[j])
                new_fys.append(fy)
                fx_next = face(line[j + 1], line[j + 2])
                acc = (fy - fys[j]) + (fx_next - fx)
                fx = fx_next
                up = jnp.where(z_last, 0.0, _roll(u, LANES - 1, 1))
                kp = jnp.where(z_last, 0.0, _roll(k, LANES - 1, 1))
                fz = (k + kp) * (up - u)
                acc = acc + (fz - jnp.where(z_first, k * u, _roll(fz, 1, 1)))
                values.append(u + (0.5 * step_dt) * acc + exs[i] * ey)
            return (after, new_fys, ext), values

        def several(a, carry, one=one, some=some):
            body = 2 * UNROLL
            rows = []
            for q in range(UNROLL):
                carry, even = one(2 * (a * UNROLL + q), carry)
                carry, odd = one(2 * (a * UNROLL + q) + 1, carry)
                emit(a * UNROLL + q, some, even, odd)
                rows += [even, odd]
            here, fys, ext = carry
            if ext:
                kept = []
                for j in range(len(some)):
                    acc = _roll(ext[j], LANES - body, 1)
                    for q in range(body):
                        shift = (LANES - (body - 1 - q)) % LANES
                        moved = _roll(rows[q][j], shift, 1) if shift else rows[q][j]
                        acc = jnp.where(zpos == DEPTH - body + q, moved, acc)
                    kept.append(acc)
                ext = tuple(kept)
            return here, fys, ext

        ext = tuple(extra[i] for i in some) if extra else ()
        results += lax.fori_loop(0, DEPTH // 2 // UNROLL, several, (here, fys, ext))[2]
    return results


def _forecast_body(
    planes, u_ref, c_ref, lo_ref, hi_ref, clo_ref, chi_ref, ex_ref, ey_ref, out_ref, surf_ref, e_ref, ce_ref, u1_ref
):
    m = pl.program_id(0)
    lane = lax.broadcasted_iota(jnp.int32, (8, LANES), 1)
    low_half = lane < DEPTH
    tiles = planes // 8
    half = DEPTH // 2

    def close(ref):
        for r in range(0, ROWS, 8):
            first = ref[pl.ds(r, 8), :]
            ref[pl.ds(DEPTH * ROWS + r, 8), :] = jnp.where(low_half, _roll(first, DEPTH, 1), 0.0)

    def fill(ref, main, low, high):
        def some(a, carry):
            ca = pl.ds(pl.multiple_of(a * LANES, LANES), LANES)
            cb = pl.ds(pl.multiple_of((a + half) * LANES, LANES), LANES)
            for read, row, size in [(main, FIRST_ROW + 8 * i, 8) for i in range(tiles)] + [
                (low, FIRST_ROW - 2, 2),
                (high, FIRST_ROW + planes, 2),
            ]:
                start = row - FIRST_ROW if size == 8 else 0
                even, odd = _wide_pair(read(start, size, ca), read(start, size, cb), low_half[:size])
                ref[pl.ds(2 * a * ROWS + row, size), :] = even
                ref[pl.ds((2 * a + 1) * ROWS + row, size), :] = odd
            return carry

        def several(a, carry):
            for q in range(FILL_UNROLL):
                carry = some(a * FILL_UNROLL + q, carry)
            return carry

        lax.fori_loop(0, half // FILL_UNROLL, several, 0)
        close(ref)

    @pl.when(m == 0)
    def _():
        def blank(i, carry):
            for ref in (e_ref, ce_ref, u1_ref):
                for r in (0, ROWS - 8):
                    ref[pl.ds(i * ROWS + r, 8), :] = jnp.zeros((8, LANES), jnp.float32)
            return carry

        lax.fori_loop(0, DEPTH + 1, blank, 0, unroll=13)
        fill(
            ce_ref,
            lambda s, n, c: c_ref[pl.ds(s, n), c],
            lambda s, n, c: clo_ref[0, pl.ds(s, n), c],
            lambda s, n, c: chi_ref[0, pl.ds(s, n), c],
        )

    fill(
        e_ref,
        lambda s, n, c: u_ref[0, pl.ds(s, n), c],
        lambda s, n, c: lo_ref[0, pl.ds(s, n), c],
        lambda s, n, c: hi_ref[0, pl.ds(s, n), c],
    )

    def ey_row(t):
        return lambda y: ey_ref[0, t, pl.ds(y, 1), :]

    wide = tiles + 1
    base1 = FIRST_ROW - 4
    ex1 = [ex_ref[0, 0, pl.ds(base1 + i, 8, stride=wide), :] for i in range(wide)]

    def emit1(a, some, even, odd):
        for p, values in ((0, even), (1, odd)):
            for i, value in zip(some, values):
                at = pl.ds((2 * a + p) * ROWS + base1 + i, 8, stride=wide)
                u1_ref[at, :] = jnp.where(ce_ref[at, :] > 0.0, value, 0.0)

    _stencil_step(e_ref, ce_ref, base1, wide, ex1, ey_row(0), emit1, ())
    close(u1_ref)

    ex2 = [ex_ref[0, 1, pl.ds(FIRST_ROW + i, 8, stride=tiles), :] for i in range(tiles)]
    out = out_ref.reshape(DEPTH * planes, LANES)

    def emit2(a, some, even, odd):
        for j, i in enumerate(some):
            one, two = _wide_pair(even[j], odd[j], low_half)
            out[pl.ds(a * planes + i, 8, stride=tiles), :] = one
            out[pl.ds((a + half) * planes + i, 8, stride=tiles), :] = two

    start = tuple(jnp.zeros((8, LANES), jnp.float32) for _ in range(tiles))
    surface = _stencil_step(u1_ref, ce_ref, FIRST_ROW, tiles, ex2, ey_row(1), emit2, start)
    surf = surf_ref.reshape(planes, LANES)
    for i in range(tiles):
        surf[pl.ds(i, 8, stride=tiles), :] = surface[i]


def forecast(u, cond, low, high, ex, ey, blocks):
    members, planes, columns = u.shape
    halves = columns // blocks // LANES
    whole = lambda shape: pl.BlockSpec(shape, lambda m: (0,) * len(shape))
    scratch = pltpu.VMEM(((DEPTH + 1) * ROWS, LANES), jnp.float32)
    return pl.pallas_call(
        functools.partial(_forecast_body, planes),
        grid=(members,),
        in_specs=[
            pl.BlockSpec((1, planes, columns), lambda m: (m, 0, 0)),
            whole((planes, columns)),
            pl.BlockSpec((1, 2, columns), lambda m: (m, 0, 0)),
            pl.BlockSpec((1, 2, columns), lambda m: (m, 0, 0)),
            pl.BlockSpec((1, 2, columns), lambda m: (members, 0, 0)),
            pl.BlockSpec((1, 2, columns), lambda m: (members, 0, 0)),
            pl.BlockSpec((1, STEPS, ROWS, LANES), lambda m: (m, 0, 0, 0)),
            pl.BlockSpec((1, STEPS, DEPTH, LANES), lambda m: (m, 0, 0, 0)),
        ],
        out_specs=[
            pl.BlockSpec((blocks, 1, halves, planes, LANES), lambda m: (0, m, 0, 0, 0)),
            pl.BlockSpec((2, 1, planes // 2, LANES), lambda m: (0, m, 0, 0)),
        ],
        out_shape=[
            jax.ShapeDtypeStruct((blocks, members, halves, planes, LANES), jnp.float32),
            jax.ShapeDtypeStruct((2, members, planes // 2, LANES), jnp.float32),
        ],
        scratch_shapes=[scratch, scratch, scratch],
        compiler_params=pltpu.CompilerParams(
            dimension_semantics=("arbitrary",), vmem_limit_bytes=32 << 20
        ),
        cost_estimate=pl.CostEstimate(flops=200_000_000, bytes_accessed=10_000_000, transcendentals=0),
        name="forecast",
    )(u, cond, low, high, low, high, ex, ey)


def _nt(a, b):
    return lax.dot_general(
        a, b, (((1,), (1,)), ((), ())), precision=lax.Precision.HIGHEST, preferred_element_type=jnp.float32
    )


def _cell_sums_body(pc_ref, obs_ref, var_ref, out_ref):
    planes = pc_ref.shape[0]
    cell = lax.broadcasted_iota(jnp.int32, (planes, LANES), 1)
    weight = 1.0 / var_ref[...]
    value = weight * obs_ref[...]
    pc = pc_ref[...]
    wsum = jnp.zeros((planes, LANES), jnp.float32)
    rsum = jnp.zeros((planes, LANES), jnp.float32)
    for j in range(pc.shape[1]):
        hit = pc[:, j : j + 1] == cell
        wsum = wsum + jnp.where(hit, weight[:, j : j + 1], 0.0)
        rsum = rsum + jnp.where(hit, value[:, j : j + 1], 0.0)
    cut = planes // 2
    for part in range(2):
        out_ref[part, 0] = wsum[part * cut : (part + 1) * cut]
        out_ref[part, 1] = rsum[part * cut : (part + 1) * cut]


def cell_sums(pixel_cell, observed, obs_var):
    planes = pixel_cell.shape[0]
    return pl.pallas_call(
        _cell_sums_body,
        out_shape=jax.ShapeDtypeStruct((2, 2, planes // 2, LANES), jnp.float32),
        cost_estimate=pl.CostEstimate(flops=400_000, bytes_accessed=100_000, transcendentals=0),
        name="cell_sums",
    )(pixel_cell, observed, obs_var)


def _gram_body(seen_ref, sums_ref, out_ref):
    planes = sums_ref.shape[2]
    sources = sums_ref.shape[0]
    count = seen_ref.shape[0] // planes
    total = sums_ref[0]
    for i in range(1, sources):
        total = total + sums_ref[i]
    gram = jnp.zeros((count, count), jnp.float32)
    proj = jnp.zeros((8, count), jnp.float32)
    for x in range(planes):
        s = seen_ref[pl.ds(x, count, stride=planes), :]
        wsum = total[0, x : x + 1]
        rsum = total[1, x : x + 1]
        mean = jnp.sum(s, axis=0, keepdims=True) * (1.0 / count)
        anom = s - mean
        gram = gram + _nt(anom * wsum, anom)
        proj = proj + _nt(jnp.broadcast_to(rsum - wsum * mean, (8, LANES)), anom)
    out_ref[pl.ds(0, count), :] = gram
    out_ref[pl.ds(count, 8), :] = proj


def gram_part(seen, sums):
    planes = sums.shape[2]
    count = seen.shape[0] // planes
    return pl.pallas_call(
        _gram_body,
        out_shape=jax.ShapeDtypeStruct((count + 8, count), jnp.float32),
        cost_estimate=pl.CostEstimate(flops=80_000_000, bytes_accessed=1_700_000, transcendentals=0),
        name="gram",
    )(seen, sums)


GROUP = 4


def _mix_body(p0_ref, p1_ref, p2_ref, p3_ref, hi_ref, lo_ref, a_ref):
    count = hi_ref.shape[0]

    def total(rows):
        return (p0_ref[rows, :] + p1_ref[rows, :]) + (p2_ref[rows, :] + p3_ref[rows, :])

    proj = total(pl.ds(count, 8))
    ntile = count // 8
    sub = lax.broadcasted_iota(jnp.int32, (8, LANES), 0)
    lane = lax.broadcasted_iota(jnp.int32, (8, LANES), 1)
    a, inv, diag = [], [], []
    for i in range(ntile):
        eye = (lane == sub + 8 * i).astype(jnp.float32)
        a.append(eye + total(pl.ds(8 * i, 8)) * (1.0 / (count - 1)))
        inv.append(eye)
        diag.append(jnp.ones((8, LANES), jnp.float32))

    def row_of(tile, r):
        return jnp.broadcast_to(tile[r : r + 1, :], (8, LANES))

    for j0 in range(0, count, GROUP):
        base = j0 // 8
        cols = [
            {i: jnp.broadcast_to(a[i][:, j0 + t : j0 + t + 1], (8, LANES)) for i in range(base, ntile)}
            for t in range(GROUP)
        ]
        r0 = j0 % 8
        arow = [row_of(a[base], r0 + t) for t in range(GROUP)]
        irow = [row_of(inv[base], r0 + t) for t in range(GROUP)]
        for t in range(GROUP):
            pivot = row_of(cols[t][base], r0 + t)
            recip = 1.0 / pivot
            diag[base] = jnp.where(sub == r0 + t, pivot, diag[base])
            for s in range(t + 1, GROUP):
                factor = row_of(cols[t][base], r0 + s) * recip
                for i in range(base, ntile):
                    cols[s][i] = cols[s][i] - factor * cols[t][i]
                arow[s] = arow[s] - factor * arow[t]
                irow[s] = irow[s] - factor * irow[t]
            arow[t] = arow[t] * recip
            irow[t] = irow[t] * recip
            cols[t][base] = jnp.where(sub > r0 + t, cols[t][base], 0.0)
        for i in range(base, ntile):
            for t in range(GROUP):
                a[i] = a[i] - cols[t][i] * arow[t]
                inv[i] = inv[i] - cols[t][i] * irow[t]
    for i in range(ntile):
        a_ref[pl.ds(8 * i, 8), :] = inv[i] / jnp.sqrt(diag[i])
    linv = a_ref[...]
    middle = _nt(proj, linv)
    wmean = lax.dot_general(
        middle, linv, (((1,), (0,)), ((), ())), precision=lax.Precision.HIGHEST, preferred_element_type=jnp.float32
    ) * (1.0 / (count - 1))
    mix = linv + wmean[0:1]
    mix = mix + (1.0 - jnp.sum(mix, axis=1, keepdims=True)) * (1.0 / count)
    hi = mix.astype(jnp.bfloat16)
    hi_ref[...] = hi
    lo_ref[...] = (mix - hi.astype(jnp.float32)).astype(jnp.bfloat16)


def mix_matrices(parts):
    count = parts[0].shape[1]
    shape = jax.ShapeDtypeStruct((count, count), jnp.bfloat16)
    return pl.pallas_call(
        _mix_body,
        out_shape=[shape, shape],
        scratch_shapes=[pltpu.VMEM((count, LANES), jnp.float32)],
        cost_estimate=pl.CostEstimate(flops=200_000_000, bytes_accessed=600_000, transcendentals=0),
        name="mix",
    )(*parts)


def _transform_body(f_ref, hi_ref, lo_ref, out_ref):
    count = hi_ref.shape[0]
    hi = hi_ref[...]
    lo = lo_ref[...]
    src = f_ref.reshape(count * 8, LANES)
    dst = out_ref.reshape(count * 8, LANES)
    for x in range(8):
        rows = pl.ds(x, count, stride=8)
        f = src[rows, :]
        fhi = f.astype(jnp.bfloat16)
        flo = (f - fhi.astype(jnp.float32)).astype(jnp.bfloat16)
        out = jnp.dot(hi, fhi, preferred_element_type=jnp.float32)
        out = out + jnp.dot(hi, flo, preferred_element_type=jnp.float32)
        out = out + jnp.dot(lo, fhi, preferred_element_type=jnp.float32)
        dst[rows, :] = out


def transform(block, hi, lo):
    count, halves, planes, _ = block.shape
    spec = pl.BlockSpec((count, 1, 8, LANES), lambda x, c: (0, c, x, 0))
    mat = pl.BlockSpec((count, count), lambda x, c: (0, 0))
    return pl.pallas_call(
        _transform_body,
        grid=(planes // 8, halves),
        in_specs=[spec, mat, mat],
        out_specs=spec,
        out_shape=jax.ShapeDtypeStruct(block.shape, jnp.float32),
        compiler_params=pltpu.CompilerParams(
            dimension_semantics=("arbitrary", "arbitrary"), vmem_limit_bytes=32 << 20
        ),
        cost_estimate=pl.CostEstimate(flops=900_000_000, bytes_accessed=8_500_000, transcendentals=0),
        name="transform",
    )(block, hi, lo)


def heat_factors(laser_x, laser_y, first):
    xs = first - FIRST_ROW + jnp.arange(ROWS, dtype=jnp.int32)
    dx = (xs[None, None, :] - laser_x[:, :, None]).astype(jnp.float32)
    ex = (step_dt * laser_power) * jnp.exp(-(dx * dx) / beam_spot_width)
    ex = jnp.broadcast_to(ex[..., None], ex.shape + (LANES,))
    lane = jnp.arange(LANES, dtype=jnp.int32)
    ys = jnp.arange(DEPTH, dtype=jnp.int32)[:, None] + (lane // DEPTH * DEPTH)[None, :]
    dy = (ys - laser_y[:, :, None, None]).astype(jnp.float32)
    ey = jnp.where(lane % DEPTH == DEPTH - 1, jnp.exp(-(dy * dy) / beam_spot_width), 0.0)
    return ex, ey


def for_halves(x, blocks):
    return jnp.broadcast_to(x[None], (blocks // 2,) + x.shape).reshape((blocks,) + x.shape[1:])


def per_device(initial_heat_matrix, conductivity, laser_x, laser_y, pixel_cell, observed, obs_var):
    members, planes, columns = initial_heat_matrix.shape
    blocks = 1
    for axis in MA:
        blocks *= lax.axis_size(axis)
    slabs = lax.axis_size("sa")
    first = lax.axis_index("sa") * planes
    u = initial_heat_matrix
    forward = [(i, i + 1) for i in range(slabs - 1)]
    backward = [(b, a) for a, b in forward]
    top = jnp.concatenate([u[:, planes - 2 :], conductivity[None, planes - 2 :]], axis=0)
    bottom = jnp.concatenate([u[:, :2], conductivity[None, :2]], axis=0)
    low = lax.ppermute(top, "sa", forward)
    high = lax.ppermute(bottom, "sa", backward)
    sums = cell_sums(pixel_cell, observed, obs_var)
    sums = lax.all_to_all(for_halves(sums, blocks), MA, 0, 0, tiled=True)
    ex, ey = heat_factors(laser_x, laser_y, first)
    sent, surf = forecast(u, conductivity, low, high, ex, ey, blocks)

    seen = lax.all_to_all(for_halves(surf, blocks), MA, 0, 0, tiled=True)
    part = gram_part(seen.reshape(blocks * members * planes // 2, LANES), sums)
    part = part + lax.ppermute(part, "ma_2", [(0, 1), (1, 0)])
    parts = [part] + [
        lax.ppermute(part, "sa", [(i, (i + s) % slabs) for i in range(slabs)]) for s in range(1, slabs)
    ]
    hi, lo = mix_matrices(parts)

    held = lax.all_to_all(sent, MA, 0, 0, tiled=True)
    done = transform(held.reshape((blocks * members,) + held.shape[2:]), hi, lo)
    back = lax.all_to_all(done.reshape(held.shape), MA, 0, 0, tiled=True)
    return back.transpose(1, 3, 0, 2, 4).reshape(members, planes, columns)


def solution(mesh):
    torus = Mesh(mesh.devices.reshape(4, 4, 2, mesh.shape["sa"]), ("ma_0", "ma_1", "ma_2", "sa"))
    in_specs = (
        P(MA, "sa", None),
        P("sa", None),
        P(MA, None),
        P(MA, None),
        P("sa", MA),
        P("sa", MA),
        P("sa", MA),
    )
    out_specs = P(MA, "sa", None)
    return jax.shard_map(
        per_device, mesh=torus, in_specs=in_specs, out_specs=out_specs, check_vma=False
    )
```

time: 258 us -> 214 us (0.83)
  Pallas kernels: 74.2 us -> 46.6 us
  blocking collectives: 107 us -> 81.7 us
  waiting for transfers between devices: 48.8 us -> 30 us
  starting transfers between devices: 9.94 us -> 25.3 us
  local copies, waits for them, and re-layouts: 15.4 us -> 27.5 us
    pallas_call x1, Pallas kernels: 55.9 us -> 24.7 us  [forecast(): pl.pallas_call(functools.partial(_forecast_body, planes), grid=(members,)...]
    all_to_all x3 -> x1, blocking collectives: 49.6 us -> 24.2 us  [per_device(): seen = lax.all_to_all(for_halves(surf, blocks), MA, 0, 0, tiled=True)]
    all_to_all x1, waiting for transfers between devices: 44.2 us -> 26.4 us  [per_device(): held = lax.all_to_all(sent, MA, 0, 0, tiled=True)]
    all_to_all x0 -> x1, starting transfers between devices: none -> 9.05 us  [per_device(): sums = lax.all_to_all(for_halves(sums, blocks), MA, 0, 0, tiled=True)]
    ppermute x0 -> x4, starting transfers between devices: none -> 6.36 us  [the longest x3 6.02 us: per_device(): lax.ppermute(part, 'sa', [(i, (i + s) % slabs) for i in range(slabs)])]
    transpose x0 -> x1, local copies, waits for them, and re-layouts: none -> 5.18 us  [per_device(): return back.transpose(1, 3, 0, 2, 4).reshape(members, planes, columns)]
    ppermute x1, waiting for transfers between devices: 3.98 us -> 0.01 us  [per_device(): high = lax.ppermute(bottom, 'sa', backward)]
    reshape x1, local copies, waits for them, and re-layouts: 2.51 us -> 6.41 us  [per_device(): return back.transpose(1, 3, 0, 2, 4).reshape(members, planes, columns)]
  transfers between devices with their start and end apart: 3 -> 8, of which waited for: 3 -> 4; matrix products, arithmetic and copies ran while one was open for 2% -> 3% of each run, Pallas kernels for 3% -> 19%
where the time goes in v2:
time: 214 us; the launch traced here: 213 us
  blocking collectives  81.7 us (38%)
  Pallas kernels  46.6 us (22%)
  waiting for transfers between devices  30 us (14%)
  local copies, waits for them, and re-layouts  27.5 us (13%)
  starting transfers between devices  25.3 us (12%)
    all_to_all x1, blocking collectives, per_device(): back = lax.all_to_all(done.reshape(held.shape), MA, 0, 0, tiled=True)  57.5 us
    all_to_all x1, waiting for transfers between devices, per_device(): held = lax.all_to_all(sent, MA, 0, 0, tiled=True)  26.4 us
    pallas_call x1, Pallas kernels, forecast(): pl.pallas_call(functools.partial(_forecast_body, planes), grid=(members,)...  24.7 us
    all_to_all x1, blocking collectives, per_device(): seen = lax.all_to_all(for_halves(surf, blocks), MA, 0, 0, tiled=True)  24.2 us
    unnamed x28, local copies, waits for them, and re-layouts  11.2 us
    all_to_all x1, starting transfers between devices, per_device(): sums = lax.all_to_all(for_halves(sums, blocks), MA, 0, 0, tiled=True)  9.05 us
    pallas_call x1, Pallas kernels, mix_matrices(): pl.pallas_call(_mix_body, out_shape=[shape, shape], scratch_shapes=[pltpu...  7.97 us
    pallas_call x1, Pallas kernels, transform(): pl.pallas_call(_transform_body, grid=(planes // 8, halves), in_specs=[spe...  6.53 us
  transfers between devices with their start and end apart: 8, of which 4 were waited for; matrix products, arithmetic and copies ran while one was open for 3% of the time, Pallas kernels for 19%

profile of v2, /device:TPU:1, one launch (start us, length us, event | category | flops | bytes accessed | tf_op | source)
XLA Modules:
  0.0 212.7 jit_solution(13596849830634008386)
XLA Ops:
  0.0 1.8 fusion.2
  1.8 1.1 slice_bitcast_fusion
  2.9 0.2 pad_maximum_fusion
  3.1 4.0 %collective-permute-start = (f32[5,2,8192]{2,1,0:T(2,128)S(1)}, f32[5,2,8192]{2,1,0:T(2,128)S(1)}, u32[]{:S(2)}, u32[]{:S(2)}) collective-permute-start(f32[5,2,8192]{2,1,0:T(2,128)S(1)} %pad_maximum_fusion), channel_id=1, source_target_pairs={{0,1},{1,2},{2,3},{4,5},{5,6},{6,7},{8,9},{9,10},{10,11},{12,13},{... | collective-permute-start | bytes 983048 | tf_op jit(solution)/shard_map/ppermute | solution.py:443
  7.0 1.4 copy.16.pc_ref
  8.4 1.4 copy.17.obs_ref
  9.8 1.4 copy.18.var_ref
  11.2 0.2 pad_maximum_fusion.1
  11.3 1.3 collective-permute-start.1
  12.6 1.7 cell_sums.1
  14.3 1.6 broadcast_in_dim.44
  15.9 9.1 %all-to-all-start.2 = ((f32[32,2,16,128]{3,2,1,0:T(8,128)}), f32[32,2,16,128]{3,2,1,0:T(8,128)S(1)}, u32[]{:S(2)}, u32[]{:S(2)}) async-start(f32[32,2,16,128]{3,2,1,0:T(8,128)} %bitcast.5), calls=%async_computation.2 | async-start | bytes 1048576 | tf_op jit(solution)/shard_map/all_to_all | solution.py:446
  25.0 0.1 copy.15
  25.1 0.1 exponential_multiply_fusion
  25.2 0.1 exponential_select_fusion.ey_ref
  25.3 0.0 collective-permute-done.lo_ref.clo_ref
  25.3 0.0 collective-permute-done.1.hi_ref.chi_ref
  25.4 0.1 broadcast_in_dim.20.ex_ref
  25.5 0.0 copy-start
  25.5 2.2 %copy-done = f32[4,32,8192]{2,1,0:T(8,128)S(1)} copy-done((f32[4,32,8192]{2,1,0:T(8,128)S(1)}, f32[4,32,8192]{2,1,0:T(8,128)}, u32[]{:S(2)}) %copy-start) | copy-done | bytes 4194328
  27.7 24.7 %forecast.1 = (f32[32,4,2,32,128]{4,3,2,1,0:T(8,128)S(1)}, f32[2,4,16,128]{3,2,1,0:T(8,128)S(1)}) custom-call(f32[4,32,8192]{2,1,0:T(8,128)S(1)} %copy-done, f32[32,8192]{1,0:T(8,128)S(1)} %copy-done.2, f32[5,2,8192]{2,1,0:T(2,128)S(1)} %collective-permute-done.lo_ref.clo_ref, f32[5,2,8192]{2,1,0:T(2,128)S(1)} %collective-permute-done.1.hi_ref.chi_ref, ...), custom_call_target="tpu_custom_call" | custom-call | flops 200000000 | bytes 10000000 | tf_op jit(solution)/shard_map/forecast/pallas_call | solution.py:209
  52.3 0.0 copy-start.1
  52.4 2.0 copy-done.1
  54.4 0.0 all-to-all-done.2.sums_ref
  54.4 0.1 broadcast_in_dim.23
  54.5 24.2 %all_to_all.20 = f32[32,4,16,128]{3,2,1,0:T(8,128)} all-to-all(f32[32,4,16,128]{3,2,1,0:T(8,128)S(1)} %bitcast.13), channel_id=1, replica_groups=mesh['ma_0'=4,'ma_1'=4,'ma_2'=2,'sa'=4] {'ma_0','ma_1','ma_2'}, dimensions={0} | all-to-all | bytes 2097152 | tf_op jit(solution)/shard_map/all_to_all | solution.py:450
  78.7 4.7 %all-to-all-start = ((f32[32,4,2,32,128]{4,3,2,1,0:T(8,128)}), f32[32,4,2,32,128]{4,3,2,1,0:T(8,128)}, u32[]{:S(2)}, u32[]{:S(2)}) async-start(f32[32,4,2,32,128]{4,3,2,1,0:T(8,128)} %copy-done.1), calls=%async_computation | async-start | bytes 8388608 | tf_op jit(solution)/shard_map/all_to_all | solution.py:458
  83.3 5.7 %gram.1 = f32[136,128]{1,0:T(8,128)} custom-call(f32[2048,128]{1,0:T(8,128)} %bitcast.12, f32[32,2,16,128]{3,2,1,0:T(8,128)} %copy-done.5), custom_call_target="tpu_custom_call" | custom-call | flops 80000000 | bytes 1700000 | tf_op jit(solution)/shard_map/gram/pallas_call | solution.py:297
  89.1 0.3 collective-permute-start.2
  89.4 1.1 collective-permute-done.2
  90.6 0.9 add.48.p0_ref
  91.5 2.4 %collective-permute-start.3 = (f32[136,128]{1,0:T(8,128)S(1)}, f32[136,128]{1,0:T(8,128)S(1)}, u32[]{:S(2)}, u32[]{:S(2)}) collective-permute-start(f32[136,128]{1,0:T(8,128)S(1)} %add.48.p0_ref), channel_id=1, source_target_pairs={{0,1},{1,2},{2,3},{3,0},{4,5},{5,6},{6,7},{7,4},{8,9},{9,10},{10,1... | collective-permute-start | bytes 208904 | tf_op jit(solution)/shard_map/ppermute | solution.py:454
  93.9 2.5 %collective-permute-start.4 = (f32[136,128]{1,0:T(8,128)S(1)}, f32[136,128]{1,0:T(8,128)S(1)}, u32[]{:S(2)}, u32[]{:S(2)}) collective-permute-start(f32[136,128]{1,0:T(8,128)S(1)} %add.48.p0_ref), channel_id=1, source_target_pairs={{0,2},{1,3},{2,0},{3,1},{4,6},{5,7},{6,4},{7,5},{8,10},{9,11},{10,... | collective-permute-start | bytes 208904 | tf_op jit(solution)/shard_map/ppermute | solution.py:454
  96.3 1.1 collective-permute-start.5
  97.5 0.1 collective-permute-done.3.p1_ref
  97.6 2.3 %collective-permute-done.4.p2_ref = f32[136,128]{1,0:T(8,128)S(1)} collective-permute-done((f32[136,128]{1,0:T(8,128)S(1)}, f32[136,128]{1,0:T(8,128)S(1)}, u32[]{:S(2)}, u32[]{:S(2)}) %collective-permute-start.4) | collective-permute-done | bytes 69664 | tf_op jit(solution)/shard_map/ppermute | solution.py:454
  99.9 0.0 collective-permute-done.5.p3_ref
  99.9 0.0 copy-done.6
  99.9 0.6 copy-done.10
  100.5 0.6 copy-done.11
  101.2 8.0 %mix.1 = (bf16[128,128]{1,0:T(8,128)(2,1)}, bf16[128,128]{1,0:T(8,128)(2,1)}) custom-call(f32[136,128]{1,0:T(8,128)} %copy-done.6, f32[136,128]{1,0:T(8,128)} %copy-done.9, f32[136,128]{1,0:T(8,128)} %copy-done.10, f32[136,128]{1,0:T(8,128)} %copy-done.11), custom_call_target="tpu_custom_call" | custom-call | flops 200000000 | bytes 600000 | tf_op jit(solution)/shard_map/mix/pallas_call | solution.py:371
  109.1 26.4 %all-to-all-done = f32[32,4,2,32,128]{4,3,2,1,0:T(8,128)} async-done(((f32[32,4,2,32,128]{4,3,2,1,0:T(8,128)}), f32[32,4,2,32,128]{4,3,2,1,0:T(8,128)}, u32[]{:S(2)}, u32[]{:S(2)}) %all-to-all-start) | async-done | bytes 4194336 | tf_op jit(solution)/shard_map/all_to_all | solution.py:458
  135.5 0.8 copy-done.3
  136.3 0.8 copy-done.4
  137.1 6.5 %transform.1 = f32[128,2,32,128]{3,2,1,0:T(8,128)S(1)} custom-call(f32[128,2,32,128]{3,2,1,0:T(8,128)} %bitcast.2.f_ref, bf16[128,128]{1,0:T(8,128)(2,1)S(1)} %copy-done.3, bf16[128,128]{1,0:T(8,128)(2,1)S(1)} %copy-done.4), custom_call_target="tpu_custom_call" | custom-call | flops 900000000 | bytes 8500000 | tf_op jit(solution)/shard_map/transform/pallas_call | solution.py:401
  143.6 57.5 %all_to_all.21 = f32[32,4,2,32,128]{4,3,2,1,0:T(8,128)S(1)} all-to-all(f32[32,4,2,32,128]{4,3,2,1,0:T(8,128)S(1)} %bitcast.10), channel_id=1, replica_groups=mesh['ma_0'=4,'ma_1'=4,'ma_2'=2,'sa'=4] {'ma_0','ma_1','ma_2'}, dimensions={0} | all-to-all | bytes 8388608 | tf_op jit(solution)/shard_map/all_to_all | solution.py:460
  201.1 5.2 %copy.19 = f32[4,32,32,2,128]{4,3,2,1,0:T(2,128)} copy(f32[4,32,32,2,128]{4,1,3,0,2:T(8,128)S(1)} %bitcast.11) | data formatting | bytes 8388608 | tf_op jit(solution)/shard_map/transpose | solution.py:461
  206.3 6.4 %reshape.72 = f32[4,32,8192]{2,1,0:T(8,128)} reshape(f32[4,32,32,2,128]{4,3,2,1,0:T(2,128)} %copy.19) | data formatting | bytes 8388608 | tf_op jit(solution)/shard_map/reshape | solution.py:461
  (20 shorter events, 0.1 us)
Async XLA Ops:
  0.0 25.5 %copy-start.2 = (f32[32,8192]{1,0:T(8,128)S(1)}, f32[32,8192]{1,0:T(8,128)}, u32[]{:S(2)}) copy-start(f32[32,8192]{1,0:T(8,128)} %c_ref.1) | copy-start | bytes 3145732
  0.0 25.0 %copy-start.7 = (s32[4,2]{0,1:T(2,128)S(1)}, s32[4,2]{0,1:T(2,128)}, u32[]{:S(2)}) copy-start(s32[4,2]{0,1:T(2,128)} %param.10) | copy-start | bytes 100
  0.0 25.1 %copy-start.8 = (s32[4,2]{0,1:T(2,128)S(1)}, s32[4,2]{0,1:T(2,128)}, u32[]{:S(2)}) copy-start(s32[4,2]{0,1:T(2,128)} %param.9) | copy-start | bytes 100
  3.1 22.3 %collective-permute-start = (f32[5,2,8192]{2,1,0:T(2,128)S(1)}, f32[5,2,8192]{2,1,0:T(2,128)S(1)}, u32[]{:S(2)}, u32[]{:S(2)}) collective-permute-start(f32[5,2,8192]{2,1,0:T(2,128)S(1)} %pad_maximum_fusion), channel_id=1, source_target_pairs={{0,1},{1,2},{2,3},{4,5},{5,6},{6,7},{8,9},{9,10},{10,11},{12,13},{... | collective-permute-start | bytes 983048 | tf_op jit(solution)/shard_map/ppermute | solution.py:443
  11.3 14.0 %collective-permute-start.1 = (f32[5,2,8192]{2,1,0:T(2,128)S(1)}, f32[5,2,8192]{2,1,0:T(2,128)S(1)}, u32[]{:S(2)}, u32[]{:S(2)}) collective-permute-start(f32[5,2,8192]{2,1,0:T(2,128)S(1)} %pad_maximum_fusion.1), channel_id=1, source_target_pairs={{1,0},{2,1},{3,2},{5,4},{6,5},{7,6},{9,8},{10,9},{11,10},{13,12},{... | collective-permute-start | bytes 983048 | tf_op jit(solution)/shard_map/ppermute | solution.py:444
  15.9 38.5 %all-to-all-start.2 = ((f32[32,2,16,128]{3,2,1,0:T(8,128)}), f32[32,2,16,128]{3,2,1,0:T(8,128)S(1)}, u32[]{:S(2)}, u32[]{:S(2)}) async-start(f32[32,2,16,128]{3,2,1,0:T(8,128)} %bitcast.5), calls=%async_computation.2 | async-start | bytes 1048576 | tf_op jit(solution)/shard_map/all_to_all | solution.py:446
  25.5 2.2 %copy-start = (f32[4,32,8192]{2,1,0:T(8,128)S(1)}, f32[4,32,8192]{2,1,0:T(8,128)}, u32[]{:S(2)}) copy-start(f32[4,32,8192]{2,1,0:T(8,128)} %u_ref.1) | copy-start | bytes 12582916
  52.3 2.0 copy-start.1
  54.4 24.3 %copy-start.5 = (f32[32,2,16,128]{3,2,1,0:T(8,128)}, f32[32,2,16,128]{3,2,1,0:T(8,128)S(1)}, u32[]{:S(2)}) copy-start(f32[32,2,16,128]{3,2,1,0:T(8,128)S(1)} %all-to-all-done.2.sums_ref) | copy-start | bytes 1572868
  78.7 56.9 %all-to-all-start = ((f32[32,4,2,32,128]{4,3,2,1,0:T(8,128)}), f32[32,4,2,32,128]{4,3,2,1,0:T(8,128)}, u32[]{:S(2)}, u32[]{:S(2)}) async-start(f32[32,4,2,32,128]{4,3,2,1,0:T(8,128)} %copy-done.1), calls=%async_computation | async-start | bytes 8388608 | tf_op jit(solution)/shard_map/all_to_all | solution.py:458
  89.1 1.5 collective-permute-start.2
  91.5 8.5 %copy-start.6 = (f32[136,128]{1,0:T(8,128)}, f32[136,128]{1,0:T(8,128)S(1)}, u32[]{:S(2)}) copy-start(f32[136,128]{1,0:T(8,128)S(1)} %add.48.p0_ref) | copy-start | bytes 208900
  91.5 6.1 %collective-permute-start.3 = (f32[136,128]{1,0:T(8,128)S(1)}, f32[136,128]{1,0:T(8,128)S(1)}, u32[]{:S(2)}, u32[]{:S(2)}) collective-permute-start(f32[136,128]{1,0:T(8,128)S(1)} %add.48.p0_ref), channel_id=1, source_target_pairs={{0,1},{1,2},{2,3},{3,0},{4,5},{5,6},{6,7},{7,4},{8,9},{9,10},{10,1... | collective-permute-start | bytes 208904 | tf_op jit(solution)/shard_map/ppermute | solution.py:454
  93.9 6.0 %collective-permute-start.4 = (f32[136,128]{1,0:T(8,128)S(1)}, f32[136,128]{1,0:T(8,128)S(1)}, u32[]{:S(2)}, u32[]{:S(2)}) collective-permute-start(f32[136,128]{1,0:T(8,128)S(1)} %add.48.p0_ref), channel_id=1, source_target_pairs={{0,2},{1,3},{2,0},{3,1},{4,6},{5,7},{6,4},{7,5},{8,10},{9,11},{10,... | collective-permute-start | bytes 208904 | tf_op jit(solution)/shard_map/ppermute | solution.py:454
  96.3 3.6 %collective-permute-start.5 = (f32[136,128]{1,0:T(8,128)S(1)}, f32[136,128]{1,0:T(8,128)S(1)}, u32[]{:S(2)}, u32[]{:S(2)}) collective-permute-start(f32[136,128]{1,0:T(8,128)S(1)} %add.48.p0_ref), channel_id=1, source_target_pairs={{0,3},{1,0},{2,1},{3,2},{4,7},{5,4},{6,5},{7,6},{8,11},{9,8},{10,9... | collective-permute-start | bytes 208904 | tf_op jit(solution)/shard_map/ppermute | solution.py:454
  97.6 2.4 %copy-start.9 = (f32[136,128]{1,0:T(8,128)}, f32[136,128]{1,0:T(8,128)S(1)}, u32[]{:S(2)}) copy-start(f32[136,128]{1,0:T(8,128)S(1)} %collective-permute-done.3.p1_ref) | copy-start | bytes 208900
  99.9 0.6 copy-start.10
  100.5 0.6 copy-start.11
  135.5 0.8 copy-start.3
  136.3 0.8 copy-start.4

commit v3 on v2

v3 whole, which is shorter than its diff:
```python
import functools

import jax
import jax.numpy as jnp
from jax import lax
from jax.experimental import pallas as pl
from jax.experimental.pallas import tpu as pltpu
from jax.sharding import Mesh
from jax.sharding import PartitionSpec as P

DEPTH = 64
STEPS = 2
LANES = 128
MA = ("ma_0", "ma_1", "ma_2")
MA_SA = ("ma_0", "ma_1", "ma_2", "sa")

step_dt = 0.025
alpha_cond = 0.05
laser_power = 12.0
beam_spot_width = 18.0

def _roll(x, shift, axis):
    return pltpu.roll(x, shift, axis)


def _wide_pair(a, b, low_half):
    return jnp.where(low_half, a, _roll(b, DEPTH, 1)), jnp.where(low_half, _roll(a, DEPTH, 1), b)


UNROLL = {2: 8, 3: 8}
FILL_UNROLL = 16


def _stencil_step(src, cond, pitch, base, tiles, apart, exs, ey_at, emit, surface):
    lane = lax.broadcasted_iota(jnp.int32, (8, LANES), 1)
    low_half = lane < DEPTH
    zpos = lane & (DEPTH - 1)
    z_last = zpos == DEPTH - 1
    z_first = zpos == 0
    unroll = UNROLL[tiles]

    def load(y, i):
        at = pl.ds(y * pitch + (base + i), 8, stride=tiles)
        u = src[at, :]
        c = cond[at, :]
        return u, c + c * (alpha_cond * (u * u))

    def face(one, two):
        return (one[1] + two[1]) * (two[0] - one[0])

    here = [load(0, i) for i in range(tiles)]
    fys = []
    for i in range(tiles):
        u, k = load(DEPTH - 1, i)
        before = (
            jnp.where(low_half, 0.0, _roll(u, DEPTH, 1)),
            jnp.where(low_half, 0.0, _roll(k, DEPTH, 1)),
        )
        fys.append(face(before, here[i]))

    def one(y, here, fys):
        after = [load(y + 1, i) for i in range(tiles)]
        line = {i: here[i] for i in range(tiles)}
        for i in range(-apart, tiles + apart):
            if i not in line and (i + apart in range(tiles) or i - apart in range(tiles)):
                line[i] = load(y, i)
        fx = {i: face(line[i], line[i + apart]) for i in range(-apart, tiles) if i in line}
        ey = jnp.broadcast_to(ey_at(y), (8, LANES))
        new_fys, values = [], []
        for i in range(tiles):
            u, k = here[i]
            fy = face(here[i], after[i])
            new_fys.append(fy)
            acc = (fy - fys[i]) + (fx[i] - fx[i - apart])
            up = jnp.where(z_last, 0.0, _roll(u, LANES - 1, 1))
            kp = jnp.where(z_last, 0.0, _roll(k, LANES - 1, 1))
            fz = (k + kp) * (up - u)
            acc = acc + (fz - jnp.where(z_first, k * u, _roll(fz, 1, 1)))
            values.append(u + (0.5 * step_dt) * acc + exs[i] * ey)
        return after, new_fys, values

    def several(a, carry):
        here, fys, tops = carry
        rows = []
        for q in range(unroll):
            here, fys, even = one(2 * (a * unroll + q), here, fys)
            here, fys, odd = one(2 * (a * unroll + q) + 1, here, fys)
            emit(a * unroll + q, even, odd)
            rows += [even, odd]
        if surface:
            kept = []
            for i in range(tiles):
                acc = _roll(tops[i], (LANES - len(rows)) % LANES, 1)
                for q, values in enumerate(rows):
                    shift = (LANES - (len(rows) - 1 - q)) % LANES
                    moved = _roll(values[i], shift, 1) if shift else values[i]
                    acc = jnp.where(zpos == DEPTH - len(rows) + q, moved, acc)
                kept.append(acc)
            tops = kept
        return here, fys, tops

    tops = [jnp.zeros((8, LANES), jnp.float32) for _ in range(tiles)] if surface else []
    return lax.fori_loop(0, DEPTH // 2 // unroll, several, (here, fys, tops))[2]


def _close(ref, pitch):
    lane = lax.broadcasted_iota(jnp.int32, (8, LANES), 1)
    for r in range(0, pitch, 8):
        first = ref[pl.ds(r, 8), :]
        ref[pl.ds(DEPTH * pitch + r, 8), :] = jnp.where(lane < DEPTH, _roll(first, DEPTH, 1), 0.0)


def _fill(ref, pitch, pieces):
    half = DEPTH // 2
    lane = lax.broadcasted_iota(jnp.int32, (8, LANES), 1)
    low_half = lane < DEPTH

    def several(b, carry):
        for q in range(FILL_UNROLL):
            a = b * FILL_UNROLL + q
            ca = pl.ds(pl.multiple_of(a * LANES, LANES), LANES)
            cb = pl.ds(pl.multiple_of((a + half) * LANES, LANES), LANES)
            for read, start, size, row, stride in pieces:
                even, odd = _wide_pair(read(pl.ds(start, size), ca), read(pl.ds(start, size), cb), low_half[:size])
                ref[pl.ds(2 * a * pitch + row, size, stride=stride), :] = even
                ref[pl.ds((2 * a + 1) * pitch + row, size, stride=stride), :] = odd
        return carry

    lax.fori_loop(0, half // FILL_UNROLL, several, 0)
    _close(ref, pitch)


def _two_steps(m, e_ref, ce_ref, u1_ref, ex_ref, ey_ref, surf_ref, pitch, step1, step2, edged, put):
    def ey_row(t):
        return lambda y: ey_ref[0, t, pl.ds(y, 1), :]

    def factors(t, base, tiles):
        return [ex_ref[0, t, pl.ds(base + i, 8, stride=tiles), :] for i in range(tiles)]

    base, tiles, apart = step1

    def emit1(a, even, odd):
        for p, values in ((0, even), (1, odd)):
            for i, value in enumerate(values):
                at = pl.ds((2 * a + p) * pitch + base + i, 8, stride=tiles)
                u1_ref[at, :] = jnp.where(ce_ref[at, :] > 0.0, value, 0.0) if edged else value

    _stencil_step(e_ref, ce_ref, pitch, base, tiles, apart, factors(0, base, tiles), ey_row(0), emit1, False)
    _close(u1_ref, pitch)
    base, count, apart = step2
    low_half = lax.broadcasted_iota(jnp.int32, (8, LANES), 1) < DEPTH

    def emit2(a, even, odd):
        for i in range(count):
            one, two = _wide_pair(even[i], odd[i], low_half)
            put(a, i, one)
            put(a + DEPTH // 2, i, two)

    tops = _stencil_step(u1_ref, ce_ref, pitch, base, count, apart, factors(1, base, count), ey_row(1), emit2, True)
    return tops


INNER_PITCH = 32
OUTER_PITCH = 40
OUTER_ROW = 8


def _inner_body(u_ref, c_ref, ex_ref, ey_ref, out_ref, surf_ref, e_ref, ce_ref, u1_ref):
    m = pl.program_id(0)
    planes = u_ref.shape[1]
    half = planes // 2
    pitch = INNER_PITCH

    @pl.when(m == 0)
    def _():
        _fill(ce_ref, pitch, [(lambda r, c: c_ref[r, c], 8 * i, 8, 8 * i, 1) for i in range(planes // 8)])

    _fill(e_ref, pitch, [(lambda r, c: u_ref[0, r, c], 8 * i, 8, 8 * i, 1) for i in range(planes // 8)])
    out = out_ref.reshape(DEPTH * half, LANES)

    def put(v, i, value):
        out[pl.ds(v * half + i, 8, stride=2), :] = value

    tops = _two_steps(
        m, e_ref, ce_ref, u1_ref, ex_ref, ey_ref, surf_ref, pitch, (4, 3, 1), (8, 2, 1), False, put
    )
    surf = surf_ref.reshape(half, LANES)
    for i in range(2):
        surf[pl.ds(i, 8, stride=2), :] = tops[i]


def _outer_body(
    u_ref, c_ref, lo_ref, hi_ref, clo_ref, chi_ref, ex_ref, ey_ref, out_ref, surf_ref, e_ref, ce_ref, u1_ref
):
    m = pl.program_id(0)
    planes = u_ref.shape[1]
    half = planes // 2
    pitch = OUTER_PITCH

    def pieces(main, low, high):
        row = OUTER_ROW
        return [
            (low, 0, 2, row, 2),
            (main, 0, 8, row + 4, 2),
            (main, 8, 2, row + 20, 2),
            (main, planes - 10, 2, row + 1, 2),
            (main, planes - 8, 8, row + 5, 2),
            (high, 0, 2, row + 21, 2),
        ]

    @pl.when(m == 0)
    def _():
        _fill(
            ce_ref,
            pitch,
            pieces(lambda r, c: c_ref[r, c], lambda r, c: clo_ref[0, r, c], lambda r, c: chi_ref[0, r, c]),
        )

    _fill(
        e_ref,
        pitch,
        pieces(lambda r, c: u_ref[0, r, c], lambda r, c: lo_ref[0, r, c], lambda r, c: hi_ref[0, r, c]),
    )
    out = out_ref.reshape(DEPTH * half, LANES)

    def put(v, i, value):
        out[pl.ds(pl.multiple_of(v * half + 8 * i, 8), 8), :] = value

    tops = _two_steps(
        m, e_ref, ce_ref, u1_ref, ex_ref, ey_ref, surf_ref, pitch,
        (OUTER_ROW, 3, 2), (OUTER_ROW + 4, 2, 2), True, put,
    )
    for i in range(2):
        surf_ref[0, pl.ds(8 * i, 8), :] = tops[i]


def _forecast_call(body, name, pitch, operands, specs, ex, ey, members, planes, blocks, halves):
    scratch = pltpu.VMEM(((DEPTH + 1) * pitch, LANES), jnp.float32)
    return pl.pallas_call(
        body,
        grid=(members,),
        in_specs=specs
        + [
            pl.BlockSpec((1, STEPS, pitch, LANES), lambda m: (m, 0, 0, 0)),
            pl.BlockSpec((1, STEPS, DEPTH, LANES), lambda m: (m, 0, 0, 0)),
        ],
        out_specs=[
            pl.BlockSpec((blocks, 1, halves, planes // 2, LANES), lambda m: (0, m, 0, 0, 0)),
            pl.BlockSpec((1, planes // 2, LANES), lambda m: (m, 0, 0)),
        ],
        out_shape=[
            jax.ShapeDtypeStruct((blocks, members, halves, planes // 2, LANES), jnp.float32),
            jax.ShapeDtypeStruct((members, planes // 2, LANES), jnp.float32),
        ],
        scratch_shapes=[scratch, scratch, scratch],
        compiler_params=pltpu.CompilerParams(
            dimension_semantics=("arbitrary",), vmem_limit_bytes=28 << 20
        ),
        cost_estimate=pl.CostEstimate(flops=100_000_000, bytes_accessed=7_000_000, transcendentals=0),
        name=name,
    )(*operands, ex, ey)


def forecast_inner(u, cond, ex, ey, blocks):
    members, planes, columns = u.shape
    specs = [
        pl.BlockSpec((1, planes, columns), lambda m: (m, 0, 0)),
        pl.BlockSpec((planes, columns), lambda m: (0, 0)),
    ]
    return _forecast_call(
        _inner_body, "inner", INNER_PITCH, (u, cond), specs, ex, ey, members, planes, blocks, columns // blocks // LANES
    )


def forecast_outer(u, cond, low, high, ex, ey, blocks):
    members, planes, columns = u.shape
    edge = lambda at: pl.BlockSpec((1, 2, columns), at)
    specs = [
        pl.BlockSpec((1, planes, columns), lambda m: (m, 0, 0)),
        pl.BlockSpec((planes, columns), lambda m: (0, 0)),
        edge(lambda m: (m, 0, 0)),
        edge(lambda m: (m, 0, 0)),
        edge(lambda m: (members, 0, 0)),
        edge(lambda m: (members, 0, 0)),
    ]
    operands = (u, cond, low, high, low, high)
    return _forecast_call(
        _outer_body, "outer", OUTER_PITCH, operands, specs, ex, ey, members, planes, blocks, columns // blocks // LANES
    )


def _nt(a, b):
    return lax.dot_general(
        a, b, (((1,), (1,)), ((), ())), precision=lax.Precision.HIGHEST, preferred_element_type=jnp.float32
    )


def _cell_sums_body(pc_ref, obs_ref, var_ref, out_ref):
    planes = pc_ref.shape[0]
    cell = lax.broadcasted_iota(jnp.int32, (planes, LANES), 1)
    weight = 1.0 / var_ref[...]
    value = weight * obs_ref[...]
    pc = pc_ref[...]
    wsum = jnp.zeros((planes, LANES), jnp.float32)
    rsum = jnp.zeros((planes, LANES), jnp.float32)
    for j in range(pc.shape[1]):
        hit = pc[:, j : j + 1] == cell
        wsum = wsum + jnp.where(hit, weight[:, j : j + 1], 0.0)
        rsum = rsum + jnp.where(hit, value[:, j : j + 1], 0.0)
    tiles = [8 * i for i in range(planes // 8)]
    inner, outer = tiles[1:-1], [tiles[0], tiles[-1]]
    for part, (one, two) in enumerate((inner, outer)):
        out_ref[part] = (
            wsum[one : one + 8]
            + _roll(rsum[one : one + 8], 64, 1)
            + _roll(wsum[two : two + 8], 32, 1)
            + _roll(rsum[two : two + 8], 96, 1)
        )


def cell_sums(pixel_cell, observed, obs_var):
    return pl.pallas_call(
        _cell_sums_body,
        out_shape=jax.ShapeDtypeStruct((2, 8, LANES), jnp.float32),
        cost_estimate=pl.CostEstimate(flops=400_000, bytes_accessed=100_000, transcendentals=0),
        name="cell_sums",
    )(pixel_cell, observed, obs_var)


def _gram_body(members, planes, seen_ref, out_ref, s_ref):
    sources = seen_ref.shape[0]
    count = sources * members
    group = lax.broadcasted_iota(jnp.int32, (8, LANES), 1) // 4
    sums = [jnp.zeros((8, LANES), jnp.float32) for _ in range(4)]
    for i in range(sources):
        row = seen_ref[i, pl.ds(members * planes, 8), :]
        for g in range(4):
            sums[g] = jnp.where(group == (i + 8 * g) % sources, row, sums[g])
        s_ref[pl.ds(i * members * planes, members * planes), :] = seen_ref[i, pl.ds(0, members * planes), :]
    w_one, w_two, r_one, r_two = (
        _roll(sums[g], (LANES - 32 * g) % LANES, 1) if g else sums[g] for g in range(4)
    )
    wsums = [w_one, w_two]
    rsums = [r_one, r_two]
    gram = jnp.zeros((count, count), jnp.float32)
    proj = jnp.zeros((8, count), jnp.float32)
    for x in range(planes):
        s = s_ref[pl.ds(x, count, stride=planes), :]
        wsum = wsums[x // 8][x % 8 : x % 8 + 1]
        rsum = rsums[x // 8][x % 8 : x % 8 + 1]
        mean = jnp.sum(s, axis=0, keepdims=True) * (1.0 / count)
        anom = s - mean
        gram = gram + _nt(anom * wsum, anom)
        proj = proj + _nt(jnp.broadcast_to(rsum - wsum * mean, (8, LANES)), anom)
    out_ref[pl.ds(0, count), :] = gram
    out_ref[pl.ds(count, 8), :] = proj


def gram_part(seen, members, planes):
    count = seen.shape[0] * members
    return pl.pallas_call(
        functools.partial(_gram_body, members, planes),
        out_shape=jax.ShapeDtypeStruct((count + 8, count), jnp.float32),
        scratch_shapes=[pltpu.VMEM((count * planes, LANES), jnp.float32)],
        cost_estimate=pl.CostEstimate(flops=80_000_000, bytes_accessed=1_700_000, transcendentals=0),
        name="gram",
    )(seen)


GROUP = 4


def _mix_body(p0_ref, p1_ref, p2_ref, p3_ref, hi_ref, lo_ref, a_ref):
    count = hi_ref.shape[0]

    def total(rows):
        return (p0_ref[rows, :] + p1_ref[rows, :]) + (p2_ref[rows, :] + p3_ref[rows, :])

    proj = total(pl.ds(count, 8))
    ntile = count // 8
    sub = lax.broadcasted_iota(jnp.int32, (8, LANES), 0)
    lane = lax.broadcasted_iota(jnp.int32, (8, LANES), 1)
    a, inv, diag = [], [], []
    for i in range(ntile):
        eye = (lane == sub + 8 * i).astype(jnp.float32)
        a.append(eye + total(pl.ds(8 * i, 8)) * (1.0 / (count - 1)))
        inv.append(eye)
        diag.append(jnp.ones((8, LANES), jnp.float32))

    def row_of(tile, r):
        return jnp.broadcast_to(tile[r : r + 1, :], (8, LANES))

    for j0 in range(0, count, GROUP):
        base = j0 // 8
        cols = [
            {i: jnp.broadcast_to(a[i][:, j0 + t : j0 + t + 1], (8, LANES)) for i in range(base, ntile)}
            for t in range(GROUP)
        ]
        r0 = j0 % 8
        arow = [row_of(a[base], r0 + t) for t in range(GROUP)]
        irow = [row_of(inv[base], r0 + t) for t in range(GROUP)]
        for t in range(GROUP):
            pivot = row_of(cols[t][base], r0 + t)
            recip = 1.0 / pivot
            diag[base] = jnp.where(sub == r0 + t, pivot, diag[base])
            for s in range(t + 1, GROUP):
                factor = row_of(cols[t][base], r0 + s) * recip
                for i in range(base, ntile):
                    cols[s][i] = cols[s][i] - factor * cols[t][i]
                arow[s] = arow[s] - factor * arow[t]
                irow[s] = irow[s] - factor * irow[t]
            arow[t] = arow[t] * recip
            irow[t] = irow[t] * recip
            cols[t][base] = jnp.where(sub > r0 + t, cols[t][base], 0.0)
        for i in range(base, ntile):
            for t in range(GROUP):
                a[i] = a[i] - cols[t][i] * arow[t]
                inv[i] = inv[i] - cols[t][i] * irow[t]
    for i in range(ntile):
        a_ref[pl.ds(8 * i, 8), :] = inv[i] / jnp.sqrt(diag[i])
    linv = a_ref[...]
    middle = _nt(proj, linv)
    wmean = lax.dot_general(
        middle, linv, (((1,), (0,)), ((), ())), precision=lax.Precision.HIGHEST, preferred_element_type=jnp.float32
    ) * (1.0 / (count - 1))
    mix = linv + wmean[0:1]
    mix = mix + (1.0 - jnp.sum(mix, axis=1, keepdims=True)) * (1.0 / count)
    hi = mix.astype(jnp.bfloat16)
    hi_ref[...] = hi
    lo_ref[...] = (mix - hi.astype(jnp.float32)).astype(jnp.bfloat16)


def mix_matrices(parts):
    count = parts[0].shape[1]
    shape = jax.ShapeDtypeStruct((count, count), jnp.bfloat16)
    return pl.pallas_call(
        _mix_body,
        out_shape=[shape, shape],
        scratch_shapes=[pltpu.VMEM((count, LANES), jnp.float32)],
        cost_estimate=pl.CostEstimate(flops=200_000_000, bytes_accessed=600_000, transcendentals=0),
        name="mix",
    )(*parts)


def _transform_body(f_ref, hi_ref, lo_ref, out_ref):
    count = hi_ref.shape[0]
    hi = hi_ref[...]
    lo = lo_ref[...]
    src = f_ref.reshape(count * 8, LANES)
    dst = out_ref.reshape(count * 8, LANES)
    for x in range(8):
        rows = pl.ds(x, count, stride=8)
        f = src[rows, :]
        fhi = f.astype(jnp.bfloat16)
        flo = (f - fhi.astype(jnp.float32)).astype(jnp.bfloat16)
        out = jnp.dot(hi, fhi, preferred_element_type=jnp.float32)
        out = out + jnp.dot(hi, flo, preferred_element_type=jnp.float32)
        out = out + jnp.dot(lo, fhi, preferred_element_type=jnp.float32)
        dst[rows, :] = out


def _transform_more(f_ref, hi_ref, lo_ref, _, out_ref):
    _transform_body(f_ref, hi_ref, lo_ref, out_ref)


def transform(block, hi, lo, onto=None):
    count, halves, planes, _ = block.shape
    first = 0 if onto is None else planes // 8
    mat = pl.BlockSpec((count, count), lambda x, c: (0, 0))
    in_specs = [pl.BlockSpec((count, 1, 8, LANES), lambda x, c: (0, c, x, 0)), mat, mat]
    operands = (block, hi, lo)
    if onto is not None:
        in_specs.append(pl.BlockSpec(memory_space=pl.ANY))
        operands += (onto,)
    return pl.pallas_call(
        _transform_body if onto is None else _transform_more,
        grid=(planes // 8, halves),
        in_specs=in_specs,
        out_specs=pl.BlockSpec((count, 1, 8, LANES), lambda x, c: (0, c, x + first, 0)),
        out_shape=jax.ShapeDtypeStruct((count, halves, 2 * planes, LANES), jnp.float32),
        input_output_aliases={} if onto is None else {3: 0},
        compiler_params=pltpu.CompilerParams(
            dimension_semantics=("arbitrary", "arbitrary"), vmem_limit_bytes=24 << 20
        ),
        cost_estimate=pl.CostEstimate(flops=450_000_000, bytes_accessed=4_300_000, transcendentals=0),
        name="transform",
    )(*operands)


def _place_body(in_ref, out_ref):
    group, _, halves, planes, _ = in_ref.shape
    inner = planes // 2
    order = list(range(inner, inner + 8, 8)) + list(range(0, inner, 8)) + list(range(inner + 8, planes, 8))
    for s in range(group):
        for h in range(halves):
            cols = pl.ds((s * halves + h) * LANES, LANES)
            for x, row in enumerate(order):
                out_ref[0, pl.ds(8 * x, 8), cols] = in_ref[s, 0, h, pl.ds(row, 8), :]


def place(back):
    blocks, members, halves, planes, _ = back.shape
    group = 8
    return pl.pallas_call(
        _place_body,
        grid=(members, blocks // group),
        in_specs=[pl.BlockSpec((group, 1, halves, planes, LANES), lambda m, b: (b, m, 0, 0, 0))],
        out_specs=pl.BlockSpec((1, planes, group * halves * LANES), lambda m, b: (m, 0, b)),
        out_shape=jax.ShapeDtypeStruct((members, planes, blocks * halves * LANES), jnp.float32),
        compiler_params=pltpu.CompilerParams(dimension_semantics=("arbitrary", "arbitrary")),
        cost_estimate=pl.CostEstimate(flops=0, bytes_accessed=8_400_000, transcendentals=0),
        name="place",
    )(back)


def heat_in_x(laser_x, xs):
    dx = (xs[None, None, :] - laser_x[:, :, None]).astype(jnp.float32)
    ex = (step_dt * laser_power) * jnp.exp(-(dx * dx) / beam_spot_width)
    return jnp.broadcast_to(ex[..., None], ex.shape + (LANES,))


def heat_in_y(laser_y):
    lane = jnp.arange(LANES, dtype=jnp.int32)
    ys = jnp.arange(DEPTH, dtype=jnp.int32)[:, None] + (lane // DEPTH * DEPTH)[None, :]
    dy = (ys - laser_y[:, :, None, None]).astype(jnp.float32)
    return jnp.where(lane % DEPTH == DEPTH - 1, jnp.exp(-(dy * dy) / beam_spot_width), 0.0)


def inner_planes(first):
    return first + jnp.arange(INNER_PITCH, dtype=jnp.int32)


def outer_planes(first, planes):
    row = jnp.arange(OUTER_PITCH, dtype=jnp.int32) - OUTER_ROW
    return first + row // 2 - 2 + (row % 2) * (planes - 8)


def per_device(initial_heat_matrix, conductivity, laser_x, laser_y, pixel_cell, observed, obs_var):
    members, planes, columns = initial_heat_matrix.shape
    blocks = 1
    for axis in MA:
        blocks *= lax.axis_size(axis)
    slabs = lax.axis_size("sa")
    first = lax.axis_index("sa") * planes
    u = initial_heat_matrix
    forward = [(i, i + 1) for i in range(slabs - 1)]
    backward = [(b, a) for a, b in forward]
    top = jnp.concatenate([u[:, planes - 2 :], conductivity[None, planes - 2 :]], axis=0)
    bottom = jnp.concatenate([u[:, :2], conductivity[None, :2]], axis=0)
    low = lax.ppermute(top, "sa", forward)
    high = lax.ppermute(bottom, "sa", backward)
    ey = heat_in_y(laser_y)
    sent_in, surf_in = forecast_inner(u, conductivity, heat_in_x(laser_x, inner_planes(first)), ey, blocks)
    held_in = lax.all_to_all(sent_in, MA, 0, 0, tiled=True)
    ex = heat_in_x(laser_x, outer_planes(first, planes))
    sent_out, surf_out = forecast_outer(u, conductivity, low, high, ex, ey, blocks)

    sums = cell_sums(pixel_cell, observed, obs_var)
    rows = jnp.concatenate([jnp.stack([surf_in, surf_out]).reshape(2, members * planes // 2, LANES), sums], axis=1)
    rows = jnp.broadcast_to(rows[None], (blocks // 2,) + rows.shape).reshape((blocks,) + rows.shape[1:])
    rows, held_in = lax.optimization_barrier((rows, held_in))
    seen = lax.all_to_all(rows, MA, 0, 0, tiled=True)
    part = gram_part(seen, members, planes // 2)
    part = part + lax.ppermute(part, "ma_2", [(0, 1), (1, 0)])
    parts = [part] + [
        lax.ppermute(part, "sa", [(i, (i + s) % slabs) for i in range(slabs)]) for s in range(1, slabs)
    ]
    hi, lo = mix_matrices(parts)

    held_out = lax.all_to_all(sent_out, MA, 0, 0, tiled=True)
    shape = (blocks * members,) + held_in.shape[2:]
    done = transform(held_in.reshape(shape), hi, lo)
    done = transform(held_out.reshape(shape), hi, lo, done)
    back = lax.all_to_all(done.reshape((blocks, members) + done.shape[1:]), MA, 0, 0, tiled=True)
    return place(back)


def solution(mesh):
    torus = Mesh(mesh.devices.reshape(4, 4, 2, mesh.shape["sa"]), ("ma_0", "ma_1", "ma_2", "sa"))
    in_specs = (
        P(MA, "sa", None),
        P("sa", None),
        P(MA, None),
        P(MA, None),
        P("sa", MA),
        P("sa", MA),
        P("sa", MA),
    )
    out_specs = P(MA, "sa", None)
    return jax.shard_map(
        per_device, mesh=torus, in_specs=in_specs, out_specs=out_specs, check_vma=False
    )
```

time: 214 us -> 208 us (0.972)
  waiting for transfers between devices: 30 us -> 13.4 us
  Pallas kernels: 46.6 us -> 59.2 us
  local copies, waits for them, and re-layouts: 27.5 us -> 20.1 us
  blocking collectives: 81.7 us -> 86.5 us
  other arithmetic: 1.44 us -> 4.62 us
  starting transfers between devices: 25.3 us -> 22.7 us
    all_to_all x2, waiting for transfers between devices: 26.4 us -> 0.01 us  [the longest x1 0.01 us: per_device(): held_in = lax.all_to_all(sent_in, MA, 0, 0, tiled=True)]
    pallas_call x4 -> x7, Pallas kernels: 38.6 us -> 51.2 us  [the longest x2 28.1 us: _forecast_call(): pl.pallas_call(body, grid=(members,), in_specs=specs + [pl.BlockSpec((1,...]
    ppermute x1, waiting for transfers between devices: 0.01 us -> 7.83 us  [per_device(): high = lax.ppermute(bottom, 'sa', backward)]
    reshape x1 -> x0, local copies, waits for them, and re-layouts: 6.41 us -> none  [per_device(): return back.transpose(1, 3, 0, 2, 4).reshape(members, planes, columns)]
    unnamed x28 -> x46, local copies, waits for them, and re-layouts: 11.2 us -> 17.4 us
    transpose x1 -> x0, local copies, waits for them, and re-layouts: 5.18 us -> none  [per_device(): return back.transpose(1, 3, 0, 2, 4).reshape(members, planes, columns)]
    all_to_all x2, blocking collectives: 81.7 us -> 86.5 us  [the longest x1 59.3 us: per_device(): lax.all_to_all(done.reshape((blocks, members) + done.shape[1:]), MA, 0, 0...]
    ppermute x3, starting transfers between devices: 6.02 us -> 2.65 us  [per_device(): lax.ppermute(part, 'sa', [(i, (i + s) % slabs) for i in range(slabs)])]
  transfers between devices with their start and end apart: 8 -> 8, of which waited for: 4 -> 5; matrix products, arithmetic and copies ran while one was open for 3% -> 4% of each run, Pallas kernels for 19% -> 16%
where the time goes in v3:
time: 208 us; the launch traced here: 207 us
  blocking collectives  86.5 us (42%)
  Pallas kernels  59.2 us (28%)
  starting transfers between devices  22.7 us (11%)
  local copies, waits for them, and re-layouts  20.1 us (10%)
  waiting for transfers between devices  13.4 us (6%)
  other arithmetic  4.62 us (2%)
    all_to_all x1, blocking collectives, per_device(): lax.all_to_all(done.reshape((blocks, members) + done.shape[1:]), MA, 0, 0...  59.3 us
    pallas_call x2, Pallas kernels, _forecast_call(): pl.pallas_call(body, grid=(members,), in_specs=specs + [pl.BlockSpec((1,...  28.1 us
    all_to_all x1, blocking collectives, per_device(): seen = lax.all_to_all(rows, MA, 0, 0, tiled=True)  27.2 us
    unnamed x46, local copies, waits for them, and re-layouts  17.4 us
    pallas_call x1, Pallas kernels, place(): pl.pallas_call(_place_body, grid=(members, blocks // group), in_specs=[pl...  10.1 us
    all_to_all x1, starting transfers between devices, per_device(): held_in = lax.all_to_all(sent_in, MA, 0, 0, tiled=True)  9.74 us
    pallas_call x1, Pallas kernels, mix_matrices(): pl.pallas_call(_mix_body, out_shape=[shape, shape], scratch_shapes=[pltpu...  7.98 us
    ppermute x1, waiting for transfers between devices, per_device(): high = lax.ppermute(bottom, 'sa', backward)  7.83 us
  transfers between devices with their start and end apart: 8, of which 5 were waited for; matrix products, arithmetic and copies ran while one was open for 4% of the time, Pallas kernels for 16%

profile of v3, /device:TPU:1, one launch (start us, length us, event | category | flops | bytes accessed | tf_op | source)
XLA Modules:
  0.0 206.8 jit_solution(16402178554831834566)
XLA Ops:
  0.0 0.8 copy.16
  0.8 0.8 exponential_multiply_fusion
  1.6 0.1 exponential_select_fusion.ey_ref
  1.7 0.1 broadcast_in_dim.23.ex_ref
  1.8 0.0 copy-start.2
  1.8 2.2 %copy-done.2 = f32[4,32,8192]{2,1,0:T(8,128)S(1)} copy-done((f32[4,32,8192]{2,1,0:T(8,128)S(1)}, f32[4,32,8192]{2,1,0:T(8,128)}, u32[]{:S(2)}) %copy-start.2) | copy-done | bytes 4194328
  4.0 1.2 copy-done.4
  5.2 13.0 %inner.1 = (f32[32,4,2,16,128]{4,3,2,1,0:T(8,128)S(1)}, f32[4,16,128]{2,1,0:T(8,128)S(1)}) custom-call(f32[4,32,8192]{2,1,0:T(8,128)S(1)} %copy-done.2, f32[32,8192]{1,0:T(8,128)S(1)} %copy-done.4, f32[4,2,32,128]{3,2,1,0:T(8,128)S(1)} %broadcast_in_dim.23.ex_ref, f32[4,2,64,128]{3,2,1,0:T(8,128)S(1)} %exponential_select_fusion.ey_ref), custom_call_target="tpu_custom_call" | custom-call | flops 100000000 | bytes 7000000 | tf_op jit(solution)/shard_map/inner/pallas_call | solution.py:239
  18.2 1.3 copy-done.7
  19.6 9.7 %all-to-all-start.1 = ((f32[32,4,2,16,128]{4,3,2,1,0:T(8,128)}), f32[32,4,2,16,128]{4,3,2,1,0:T(8,128)S(1)}, u32[]{:S(2)}, u32[]{:S(2)}) async-start(f32[32,4,2,16,128]{4,3,2,1,0:T(8,128)} %copy-done.7), calls=%async_computation.1 | async-start | bytes 4194304 | tf_op jit(solution)/shard_map/all_to_all | solution.py:554
  29.4 2.4 %fusion.4 = (f32[4,2,8192]{2,1,0:T(2,128)}, f32[4,2,8192]{2,1,0:T(2,128)S(1)}) fusion(f32[4,32,8192]{2,1,0:T(8,128)} %u_ref.3), kind=kLoop, calls=%fused_computation.24 | loop fusion | bytes 1048576 | tf_op jit(solution)/shard_map/slice | solution.py:549
  31.8 0.9 pad_maximum_fusion
  32.7 3.8 %collective-permute-start = (f32[5,2,8192]{2,1,0:T(2,128)}, f32[5,2,8192]{2,1,0:T(2,128)}, u32[]{:S(2)}, u32[]{:S(2)}) collective-permute-start(f32[5,2,8192]{2,1,0:T(2,128)} %pad_maximum_fusion), channel_id=1, source_target_pairs={{0,1},{1,2},{2,3},{4,5},{5,6},{6,7},{8,9},{9,10},{10,11},{12,13},{... | collective-permute-start | bytes 983048 | tf_op jit(solution)/shard_map/ppermute | solution.py:550
  36.5 0.7 copy.18.pc_ref
  37.2 0.7 copy.19.obs_ref
  37.9 0.7 copy.20.var_ref
  38.6 1.8 pad_maximum_fusion.1
  40.4 1.3 collective-permute-start.1
  41.7 1.7 cell_sums.1
  43.4 0.1 exponential_multiply_fusion.1
  43.5 7.8 %collective-permute-done.1.hi_ref.chi_ref = f32[5,2,8192]{2,1,0:T(2,128)} collective-permute-done((f32[5,2,8192]{2,1,0:T(2,128)}, f32[5,2,8192]{2,1,0:T(2,128)}, u32[]{:S(2)}, u32[]{:S(2)}) %collective-permute-start.1) | collective-permute-done | bytes 327712 | tf_op jit(solution)/shard_map/ppermute | solution.py:551
  51.4 0.1 broadcast_in_dim.20.ex_ref
  51.5 2.2 %copy-done.3 = f32[4,32,8192]{2,1,0:T(8,128)S(1)} copy-done((f32[4,32,8192]{2,1,0:T(8,128)S(1)}, f32[4,32,8192]{2,1,0:T(8,128)}, u32[]{:S(2)}) %copy-start.3) | copy-done | bytes 4194328
  53.7 15.1 %outer.1 = (f32[32,4,2,16,128]{4,3,2,1,0:T(8,128)S(1)}, f32[4,16,128]{2,1,0:T(8,128)S(1)}) custom-call(f32[4,32,8192]{2,1,0:T(8,128)S(1)} %copy-done.3, f32[32,8192]{1,0:T(8,128)S(1)} %copy-done.5, f32[5,2,8192]{2,1,0:T(2,128)} %collective-permute-done.lo_ref.clo_ref, f32[5,2,8192]{2,1,0:T(2,128)} %collective-permute-done.1.hi_ref.chi_ref, ...), custom_call_target="tpu_custom_call" | custom-call | flops 100000000 | bytes 7000000 | tf_op jit(solution)/shard_map/outer/pallas_call | solution.py:239
  68.8 1.3 copy-done.6
  70.2 0.1 broadcast_in_dim.24
  70.2 27.2 %all_to_all.20.seen_ref = f32[32,72,128]{2,1,0:T(8,128)} all-to-all(f32[32,72,128]{2,1,0:T(8,128)S(1)} %bitcast.14), channel_id=1, replica_groups=mesh['ma_0'=4,'ma_1'=4,'ma_2'=2,'sa'=4] {'ma_0','ma_1','ma_2'}, dimensions={0} | all-to-all | bytes 2359296 | tf_op jit(solution)/shard_map/all_to_all | solution.py:562
  97.5 4.7 %all-to-all-start = ((f32[32,4,2,16,128]{4,3,2,1,0:T(8,128)}), f32[32,4,2,16,128]{4,3,2,1,0:T(8,128)}, u32[]{:S(2)}, u32[]{:S(2)}) async-start(f32[32,4,2,16,128]{4,3,2,1,0:T(8,128)} %copy-done.6), calls=%async_computation | async-start | bytes 4194304 | tf_op jit(solution)/shard_map/all_to_all | solution.py:570
  102.2 5.6 %gram.1 = f32[136,128]{1,0:T(8,128)} custom-call(f32[32,72,128]{2,1,0:T(8,128)} %all_to_all.20.seen_ref), custom_call_target="tpu_custom_call" | custom-call | flops 80000000 | bytes 1700000 | tf_op jit(solution)/shard_map/gram/pallas_call | solution.py:361
  107.8 0.4 collective-permute-start.2
  108.3 1.1 collective-permute-done.2
  109.4 0.9 add.93.p0_ref
  110.3 0.1 collective-permute-start.5
  110.4 2.3 %collective-permute-start.4 = (f32[136,128]{1,0:T(8,128)S(1)}, f32[136,128]{1,0:T(8,128)S(1)}, u32[]{:S(2)}, u32[]{:S(2)}) collective-permute-start(f32[136,128]{1,0:T(8,128)S(1)} %add.93.p0_ref), channel_id=1, source_target_pairs={{0,2},{1,3},{2,0},{3,1},{4,6},{5,7},{6,4},{7,5},{8,10},{9,11},{10,... | collective-permute-start | bytes 208904 | tf_op jit(solution)/shard_map/ppermute | solution.py:566
  112.7 0.3 collective-permute-start.3
  113.0 1.0 collective-permute-done.5.p3_ref
  113.9 1.6 collective-permute-done.4.p2_ref
  115.5 1.9 collective-permute-done.3.p1_ref
  117.4 0.6 copy-done.20
  118.1 8.0 %mix.1 = (bf16[128,128]{1,0:T(8,128)(2,1)}, bf16[128,128]{1,0:T(8,128)(2,1)}) custom-call(f32[136,128]{1,0:T(8,128)} %copy-done.12, f32[136,128]{1,0:T(8,128)} %copy-done.20, f32[136,128]{1,0:T(8,128)} %copy-done.19, f32[136,128]{1,0:T(8,128)} %copy-done.18), custom_call_target="tpu_custom_call" | custom-call | flops 200000000 | bytes 600000 | tf_op jit(solution)/shard_map/mix/pallas_call | solution.py:436
  126.1 0.8 copy-done.8
  126.8 0.8 copy-done.10
  127.6 2.1 %transform.2._ = f32[128,2,32,128]{3,2,1,0:T(8,128)S(1)} custom-call(f32[128,2,16,128]{3,2,1,0:T(8,128)S(1)} %bitcast.11, bf16[128,128]{1,0:T(8,128)(2,1)S(1)} %copy-done.8, bf16[128,128]{1,0:T(8,128)(2,1)S(1)} %copy-done.10), custom_call_target="tpu_custom_call" | custom-call | flops 450000000 | bytes 4300000 | tf_op jit(solution)/shard_map/transform/pallas_call | solution.py:475
  129.7 2.0 copy-done
  131.7 2.2 %copy-done.1 = f32[128,2,32,128]{3,2,1,0:T(8,128)S(1)} copy-done((f32[128,2,32,128]{3,2,1,0:T(8,128)S(1)}, f32[128,2,32,128]{3,2,1,0:T(8,128)}, u32[]{:S(2)}) %copy-start.1) | copy-done | bytes 4194328
  133.9 3.5 %transform.3 = f32[128,2,32,128]{3,2,1,0:T(8,128)S(1)} custom-call(f32[128,2,16,128]{3,2,1,0:T(8,128)} %bitcast.2.f_ref, bf16[128,128]{1,0:T(8,128)(2,1)S(1)} %copy-done.9, bf16[128,128]{1,0:T(8,128)(2,1)S(1)} %copy-done.11, f32[128,2,32,128]{3,2,1,0:T(8,128)S(1)} %copy-done.1), custom_call_target="tpu_custom_call", output_to_operand_aliasing={{}: (3, {})} | custom-call | flops 450000000 | bytes 4300000 | tf_op jit(solution)/shard_map/transform/pallas_call | solution.py:475
  137.4 59.3 %all_to_all.21.in_ref = f32[32,4,2,32,128]{4,3,2,1,0:T(8,128)} all-to-all(f32[32,4,2,32,128]{4,3,2,1,0:T(8,128)S(1)} %bitcast.10), channel_id=1, replica_groups=mesh['ma_0'=4,'ma_1'=4,'ma_2'=2,'sa'=4] {'ma_0','ma_1','ma_2'}, dimensions={0} | all-to-all | bytes 8388608 | tf_op jit(solution)/shard_map/all_to_all | solution.py:574
  196.7 10.1 %place.1 = f32[4,32,8192]{2,1,0:T(8,128)} custom-call(f32[32,4,2,32,128]{4,3,2,1,0:T(8,128)} %all_to_all.21.in_ref), custom_call_target="tpu_custom_call" | custom-call | bytes 8400000 | tf_op jit(solution)/shard_map/place/pallas_call | solution.py:504
  (43 shorter events, 0.2 us)
Async XLA Ops:
  1.8 2.2 %copy-start.2 = (f32[4,32,8192]{2,1,0:T(8,128)S(1)}, f32[4,32,8192]{2,1,0:T(8,128)}, u32[]{:S(2)}) copy-start(f32[4,32,8192]{2,1,0:T(8,128)} %u_ref.3) | copy-start | bytes 12582916
  4.0 1.2 copy-start.4
  5.2 24.1 %copy-start.5 = (f32[32,8192]{1,0:T(8,128)S(1)}, f32[32,8192]{1,0:T(8,128)}, u32[]{:S(2)}) copy-start(f32[32,8192]{1,0:T(8,128)} %c_ref.3) | copy-start | bytes 3145732
  18.2 1.3 copy-start.7
  19.6 17.0 %copy-start.14 = (s32[32,16]{0,1:T(8,128)S(1)}, s32[32,16]{0,1:T(8,128)}, u32[]{:S(2)}) copy-start(s32[32,16]{0,1:T(8,128)} %param.11) | copy-start | bytes 6148
  19.6 17.6 %copy-start.15 = (f32[32,16]{0,1:T(8,128)S(1)}, f32[32,16]{0,1:T(8,128)}, u32[]{:S(2)}) copy-start(f32[32,16]{0,1:T(8,128)} %param.12) | copy-start | bytes 6148
  19.6 18.3 %copy-start.16 = (f32[32,16]{0,1:T(8,128)S(1)}, f32[32,16]{0,1:T(8,128)}, u32[]{:S(2)}) copy-start(f32[32,16]{0,1:T(8,128)} %param.13) | copy-start | bytes 6148
  19.6 23.9 %copy-start.17 = (s32[4,2]{0,1:T(2,128)S(1)}, s32[4,2]{0,1:T(2,128)}, u32[]{:S(2)}) copy-start(s32[4,2]{0,1:T(2,128)} %param.9) | copy-start | bytes 100
  19.6 50.6 %all-to-all-start.1 = ((f32[32,4,2,16,128]{4,3,2,1,0:T(8,128)}), f32[32,4,2,16,128]{4,3,2,1,0:T(8,128)S(1)}, u32[]{:S(2)}, u32[]{:S(2)}) async-start(f32[32,4,2,16,128]{4,3,2,1,0:T(8,128)} %copy-done.7), calls=%async_computation.1 | async-start | bytes 4194304 | tf_op jit(solution)/shard_map/all_to_all | solution.py:554
  32.7 10.8 %collective-permute-start = (f32[5,2,8192]{2,1,0:T(2,128)}, f32[5,2,8192]{2,1,0:T(2,128)}, u32[]{:S(2)}, u32[]{:S(2)}) collective-permute-start(f32[5,2,8192]{2,1,0:T(2,128)} %pad_maximum_fusion), channel_id=1, source_target_pairs={{0,1},{1,2},{2,3},{4,5},{5,6},{6,7},{8,9},{9,10},{10,11},{12,13},{... | collective-permute-start | bytes 983048 | tf_op jit(solution)/shard_map/ppermute | solution.py:550
  40.4 11.0 %collective-permute-start.1 = (f32[5,2,8192]{2,1,0:T(2,128)}, f32[5,2,8192]{2,1,0:T(2,128)}, u32[]{:S(2)}, u32[]{:S(2)}) collective-permute-start(f32[5,2,8192]{2,1,0:T(2,128)} %pad_maximum_fusion.1), channel_id=1, source_target_pairs={{1,0},{2,1},{3,2},{5,4},{6,5},{7,6},{9,8},{10,9},{11,10},{13,12},{... | collective-permute-start | bytes 983048 | tf_op jit(solution)/shard_map/ppermute | solution.py:551
  43.4 26.7 %copy-start.13 = (f32[2,8,128]{2,1,0:T(8,128)S(1)}, f32[2,8,128]{2,1,0:T(8,128)}, u32[]{:S(2)}) copy-start(f32[2,8,128]{2,1,0:T(8,128)} %cell_sums.1) | copy-start | bytes 24580
  51.5 2.2 %copy-start.3 = (f32[4,32,8192]{2,1,0:T(8,128)S(1)}, f32[4,32,8192]{2,1,0:T(8,128)}, u32[]{:S(2)}) copy-start(f32[4,32,8192]{2,1,0:T(8,128)} %u_ref.3) | copy-start | bytes 12582916
  68.8 1.3 copy-start.6
  97.5 34.2 %all-to-all-start = ((f32[32,4,2,16,128]{4,3,2,1,0:T(8,128)}), f32[32,4,2,16,128]{4,3,2,1,0:T(8,128)}, u32[]{:S(2)}, u32[]{:S(2)}) async-start(f32[32,4,2,16,128]{4,3,2,1,0:T(8,128)} %copy-done.6), calls=%async_computation | async-start | bytes 4194304 | tf_op jit(solution)/shard_map/all_to_all | solution.py:570
  107.8 1.5 collective-permute-start.2
  110.3 7.1 %copy-start.12 = (f32[136,128]{1,0:T(8,128)}, f32[136,128]{1,0:T(8,128)S(1)}, u32[]{:S(2)}) copy-start(f32[136,128]{1,0:T(8,128)S(1)} %add.93.p0_ref) | copy-start | bytes 208900
  110.3 3.6 %collective-permute-start.5 = (f32[136,128]{1,0:T(8,128)S(1)}, f32[136,128]{1,0:T(8,128)S(1)}, u32[]{:S(2)}, u32[]{:S(2)}) collective-permute-start(f32[136,128]{1,0:T(8,128)S(1)} %add.93.p0_ref), channel_id=1, source_target_pairs={{0,3},{1,0},{2,1},{3,2},{4,7},{5,4},{6,5},{7,6},{8,11},{9,8},{10,9... | collective-permute-start | bytes 208904 | tf_op jit(solution)/shard_map/ppermute | solution.py:566
  110.4 5.1 %collective-permute-start.4 = (f32[136,128]{1,0:T(8,128)S(1)}, f32[136,128]{1,0:T(8,128)S(1)}, u32[]{:S(2)}, u32[]{:S(2)}) collective-permute-start(f32[136,128]{1,0:T(8,128)S(1)} %add.93.p0_ref), channel_id=1, source_target_pairs={{0,2},{1,3},{2,0},{3,1},{4,6},{5,7},{6,4},{7,5},{8,10},{9,11},{10,... | collective-permute-start | bytes 208904 | tf_op jit(solution)/shard_map/ppermute | solution.py:566
  112.7 4.8 %collective-permute-start.3 = (f32[136,128]{1,0:T(8,128)S(1)}, f32[136,128]{1,0:T(8,128)S(1)}, u32[]{:S(2)}, u32[]{:S(2)}) collective-permute-start(f32[136,128]{1,0:T(8,128)S(1)} %add.93.p0_ref), channel_id=1, source_target_pairs={{0,1},{1,2},{2,3},{3,0},{4,5},{5,6},{6,7},{7,4},{8,9},{9,10},{10,1... | collective-permute-start | bytes 208904 | tf_op jit(solution)/shard_map/ppermute | solution.py:566
  113.9 3.5 %copy-start.18 = (f32[136,128]{1,0:T(8,128)}, f32[136,128]{1,0:T(8,128)S(1)}, u32[]{:S(2)}) copy-start(f32[136,128]{1,0:T(8,128)S(1)} %collective-permute-done.5.p3_ref) | copy-start | bytes 208900
  115.5 1.9 copy-start.19
  117.4 0.6 copy-start.20
  126.1 0.8 copy-start.8
  126.8 0.8 copy-start.10
  127.6 4.1 %copy-start.9 = (bf16[128,128]{1,0:T(8,128)(2,1)S(1)}, bf16[128,128]{1,0:T(8,128)(2,1)}, u32[]{:S(2)}) copy-start(bf16[128,128]{1,0:T(8,128)(2,1)} %get-tuple-element.18.hi_ref) | copy-start | bytes 98308
  127.6 4.1 %copy-start.11 = (bf16[128,128]{1,0:T(8,128)(2,1)S(1)}, bf16[128,128]{1,0:T(8,128)(2,1)}, u32[]{:S(2)}) copy-start(bf16[128,128]{1,0:T(8,128)(2,1)} %get-tuple-element.19.lo_ref) | copy-start | bytes 98308
  129.7 2.0 copy-start
  131.7 2.2 %copy-start.1 = (f32[128,2,32,128]{3,2,1,0:T(8,128)S(1)}, f32[128,2,32,128]{3,2,1,0:T(8,128)}, u32[]{:S(2)}) copy-start(f32[128,2,32,128]{3,2,1,0:T(8,128)} %copy-done) | copy-start | bytes 12582916

commit v4 on v3

--- a/solution.py
+++ b/solution.py
@@ -11,6 +11,7 @@
 DEPTH = 64
 STEPS = 2
 LANES = 128
+VMEM_BYTES = 60 << 20
 MA = ("ma_0", "ma_1", "ma_2")
 MA_SA = ("ma_0", "ma_1", "ma_2", "sa")
 
@@ -254,7 +255,7 @@
         ],
         scratch_shapes=[scratch, scratch, scratch],
         compiler_params=pltpu.CompilerParams(
-            dimension_semantics=("arbitrary",), vmem_limit_bytes=28 << 20
+            dimension_semantics=("arbitrary",), vmem_limit_bytes=VMEM_BYTES
         ),
         cost_estimate=pl.CostEstimate(flops=100_000_000, bytes_accessed=7_000_000, transcendentals=0),
         name=name,
@@ -323,6 +324,7 @@
         _cell_sums_body,
         out_shape=jax.ShapeDtypeStruct((2, 8, LANES), jnp.float32),
         cost_estimate=pl.CostEstimate(flops=400_000, bytes_accessed=100_000, transcendentals=0),
+        compiler_params=pltpu.CompilerParams(vmem_limit_bytes=VMEM_BYTES),
         name="cell_sums",
     )(pixel_cell, observed, obs_var)
 
@@ -363,6 +365,7 @@
         out_shape=jax.ShapeDtypeStruct((count + 8, count), jnp.float32),
         scratch_shapes=[pltpu.VMEM((count * planes, LANES), jnp.float32)],
         cost_estimate=pl.CostEstimate(flops=80_000_000, bytes_accessed=1_700_000, transcendentals=0),
+        compiler_params=pltpu.CompilerParams(vmem_limit_bytes=VMEM_BYTES),
         name="gram",
     )(seen)
 
@@ -438,6 +441,7 @@
         out_shape=[shape, shape],
         scratch_shapes=[pltpu.VMEM((count, LANES), jnp.float32)],
         cost_estimate=pl.CostEstimate(flops=200_000_000, bytes_accessed=600_000, transcendentals=0),
+        compiler_params=pltpu.CompilerParams(vmem_limit_bytes=VMEM_BYTES),
         name="mix",
     )(*parts)
 
@@ -465,52 +469,29 @@
 
 def transform(block, hi, lo, onto=None):
     count, halves, planes, _ = block.shape
-    first = 0 if onto is None else planes // 8
+    tiles = planes // 8
     mat = pl.BlockSpec((count, count), lambda x, c: (0, 0))
     in_specs = [pl.BlockSpec((count, 1, 8, LANES), lambda x, c: (0, c, x, 0)), mat, mat]
     operands = (block, hi, lo)
-    if onto is not None:
+    if onto is None:
+        out_map = lambda x, c: (0, x + 1, c)
+    else:
+        out_map = lambda x, c: (0, x * (tiles + 1), c)
         in_specs.append(pl.BlockSpec(memory_space=pl.ANY))
         operands += (onto,)
     return pl.pallas_call(
         _transform_body if onto is None else _transform_more,
-        grid=(planes // 8, halves),
+        grid=(tiles, halves),
         in_specs=in_specs,
-        out_specs=pl.BlockSpec((count, 1, 8, LANES), lambda x, c: (0, c, x + first, 0)),
-        out_shape=jax.ShapeDtypeStruct((count, halves, 2 * planes, LANES), jnp.float32),
+        out_specs=pl.BlockSpec((count, 8, LANES), out_map),
+        out_shape=jax.ShapeDtypeStruct((count, 2 * planes, halves * LANES), jnp.float32),
         input_output_aliases={} if onto is None else {3: 0},
         compiler_params=pltpu.CompilerParams(
-            dimension_semantics=("arbitrary", "arbitrary"), vmem_limit_bytes=24 << 20
+            dimension_semantics=("arbitrary", "arbitrary"), vmem_limit_bytes=VMEM_BYTES
         ),
         cost_estimate=pl.CostEstimate(flops=450_000_000, bytes_accessed=4_300_000, transcendentals=0),
         name="transform",
     )(*operands)
-
-
-def _place_body(in_ref, out_ref):
-    group, _, halves, planes, _ = in_ref.shape
-    inner = planes // 2
-    order = list(range(inner, inner + 8, 8)) + list(range(0, inner, 8)) + list(range(inner + 8, planes, 8))
-    for s in range(group):
-        for h in range(halves):
-            cols = pl.ds((s * halves + h) * LANES, LANES)
-            for x, row in enumerate(order):
-                out_ref[0, pl.ds(8 * x, 8), cols] = in_ref[s, 0, h, pl.ds(row, 8), :]
-
-
-def place(back):
-    blocks, members, halves, planes, _ = back.shape
-    group = 8
-    return pl.pallas_call(
-        _place_body,
-        grid=(members, blocks // group),
-        in_specs=[pl.BlockSpec((group, 1, halves, planes, LANES), lambda m, b: (b, m, 0, 0, 0))],
-        out_specs=pl.BlockSpec((1, planes, group * halves * LANES), lambda m, b: (m, 0, b)),
-        out_shape=jax.ShapeDtypeStruct((members, planes, blocks * halves * LANES), jnp.float32),
-        compiler_params=pltpu.CompilerParams(dimension_semantics=("arbitrary", "arbitrary")),
-        cost_estimate=pl.CostEstimate(flops=0, bytes_accessed=8_400_000, transcendentals=0),
-        name="place",
-    )(back)
 
 
 def heat_in_x(laser_x, xs):
@@ -551,6 +532,7 @@
     high = lax.ppermute(bottom, "sa", backward)
     ey = heat_in_y(laser_y)
     sent_in, surf_in = forecast_inner(u, conductivity, heat_in_x(laser_x, inner_planes(first)), ey, blocks)
+    sent_in, low, high = lax.optimization_barrier((sent_in, low, high))
     held_in = lax.all_to_all(sent_in, MA, 0, 0, tiled=True)
     ex = heat_in_x(laser_x, outer_planes(first, planes))
     sent_out, surf_out = forecast_outer(u, conductivity, low, high, ex, ey, blocks)
@@ -572,7 +554,7 @@
     done = transform(held_in.reshape(shape), hi, lo)
     done = transform(held_out.reshape(shape), hi, lo, done)
     back = lax.all_to_all(done.reshape((blocks, members) + done.shape[1:]), MA, 0, 0, tiled=True)
-    return place(back)
+    return back.transpose(1, 2, 0, 3).reshape(members, planes, columns)
 
 
 def solution(mesh):

time: 208 us -> 190 us (0.913)
  local copies, waits for them, and re-layouts: 20.1 us -> 10.4 us
  blocking collectives: 86.5 us -> 81.9 us
  Pallas kernels: 59.2 us -> 56.4 us
    unnamed x46 -> x30, local copies, waits for them, and re-layouts: 17.4 us -> 3.45 us
    pallas_call x1 -> x0, Pallas kernels: 10.1 us -> none  [place(): pl.pallas_call(_place_body, grid=(members, blocks // group), in_specs=[pl...]
    ppermute x1, waiting for transfers between devices: 7.83 us -> 0.01 us  [per_device(): high = lax.ppermute(bottom, 'sa', backward)]
    all_to_all x1, waiting for transfers between devices: 0.01 us -> 6.14 us  [per_device(): held_in = lax.all_to_all(sent_in, MA, 0, 0, tiled=True)]
    all_to_all x1, blocking collectives: 27.2 us -> 23.3 us  [per_device(): seen = lax.all_to_all(rows, MA, 0, 0, tiled=True)]
    pallas_call x2, Pallas kernels: 28.1 us -> 32.1 us  [_forecast_call(): pl.pallas_call(body, grid=(members,), in_specs=specs + [pl.BlockSpec((1,...]
    pallas_call x2, Pallas kernels: 5.59 us -> 8.94 us  [transform(): pl.pallas_call(_transform_body if onto is None else _transform_more, grid...]
    reshape x0 -> x1, local copies, waits for them, and re-layouts: none -> 2.51 us  [per_device(): return back.transpose(1, 2, 0, 3).reshape(members, planes, columns)]
  transfers between devices with their start and end apart: 8 -> 8, of which waited for: 5 -> 5; matrix products, arithmetic and copies ran while one was open for 4% -> 4% of each run, Pallas kernels for 16% -> 27%
where the time goes in v4:
time: 190 us
  blocking collectives  81.9 us (43%)
  Pallas kernels  56.4 us (30%)
  starting transfers between devices  24.3 us (13%)
  waiting for transfers between devices  12.8 us (7%)
  local copies, waits for them, and re-layouts  10.4 us (5%)
  other arithmetic  3.67 us (2%)
    all_to_all x1, blocking collectives, per_device(): lax.all_to_all(done.reshape((blocks, members) + done.shape[1:]), MA, 0, 0...  58.6 us
    pallas_call x2, Pallas kernels, _forecast_call(): pl.pallas_call(body, grid=(members,), in_specs=specs + [pl.BlockSpec((1,...  32.1 us
    all_to_all x1, blocking collectives, per_device(): seen = lax.all_to_all(rows, MA, 0, 0, tiled=True)  23.3 us
    all_to_all x1, starting transfers between devices, per_device(): held_in = lax.all_to_all(sent_in, MA, 0, 0, tiled=True)  9.07 us
    pallas_call x2, Pallas kernels, transform(): pl.pallas_call(_transform_body if onto is None else _transform_more, grid...  8.94 us
    pallas_call x1, Pallas kernels, mix_matrices(): pl.pallas_call(_mix_body, out_shape=[shape, shape], scratch_shapes=[pltpu...  7.97 us
    all_to_all x1, waiting for transfers between devices, per_device(): held_in = lax.all_to_all(sent_in, MA, 0, 0, tiled=True)  6.14 us
    pallas_call x1, Pallas kernels, gram_part(): pl.pallas_call(functools.partial(_gram_body, members, planes), out_shape=...  5.64 us
  transfers between devices with their start and end apart: 8, of which 5 were waited for; matrix products, arithmetic and copies ran while one was open for 4% of the time, Pallas kernels for 27%

profile of v4, /device:TPU:1, one launch (start us, length us, event | category | flops | bytes accessed | tf_op | source)
XLA Modules:
  0.0 189.6 jit_solution(13855014634522011003)
XLA Ops:
  0.0 1.1 slice_bitcast_fusion
  1.1 1.7 fusion.4
  2.8 0.2 pad_maximum_fusion
  3.0 4.0 %collective-permute-start = (f32[5,2,8192]{2,1,0:T(2,128)S(1)}, f32[5,2,8192]{2,1,0:T(2,128)S(1)}, u32[]{:S(2)}, u32[]{:S(2)}) collective-permute-start(f32[5,2,8192]{2,1,0:T(2,128)S(1)} %pad_maximum_fusion), channel_id=1, source_target_pairs={{0,1},{1,2},{2,3},{4,5},{5,6},{6,7},{8,9},{9,10},{10,11},{12,13},{... | collective-permute-start | bytes 983048 | tf_op jit(solution)/shard_map/ppermute | solution.py:531
  6.9 0.2 pad_maximum_fusion.1
  7.1 1.3 collective-permute-start.1
  8.4 0.8 copy.17
  9.2 0.8 exponential_multiply_fusion.1
  10.0 0.8 exponential_select_fusion.ey_ref
  10.8 0.7 broadcast_in_dim.18.ex_ref
  11.6 15.4 %inner.1 = (f32[32,4,2,16,128]{4,3,2,1,0:T(8,128)}, f32[4,16,128]{2,1,0:T(8,128)}) custom-call(f32[4,32,8192]{2,1,0:T(8,128)} %u_ref.3, f32[32,8192]{1,0:T(8,128)} %c_ref.3, f32[4,2,32,128]{3,2,1,0:T(8,128)} %broadcast_in_dim.18.ex_ref, f32[4,2,64,128]{3,2,1,0:T(8,128)} %exponential_select_fusion.ey_ref), custom_call_target="tpu_custom_call" | custom-call | flops 100000000 | bytes 7000000 | tf_op jit(solution)/shard_map/inner/pallas_call | solution.py:240
  27.0 0.0 collective-permute-done.lo_ref.clo_ref
  27.0 0.0 copy-start.1
  27.0 0.0 collective-permute-done.1.hi_ref.chi_ref
  27.0 0.0 copy-start.2
  27.0 9.1 %all-to-all-start.1 = ((f32[32,4,2,16,128]{4,3,2,1,0:T(8,128)}), f32[32,4,2,16,128]{4,3,2,1,0:T(8,128)S(1)}, u32[]{:S(2)}, u32[]{:S(2)}) async-start(f32[32,4,2,16,128]{4,3,2,1,0:T(8,128)} %get-tuple-element.22), calls=%async_computation.1 | async-start | bytes 4194304 | tf_op jit(solution)/shard_map/all_to_all | solution.py:536
  36.1 0.7 copy.19.pc_ref
  36.8 0.7 copy.20.obs_ref
  37.4 0.7 copy.21.var_ref
  38.1 1.7 cell_sums.1
  39.8 0.0 copy-done.9
  39.8 0.1 exponential_multiply_fusion
  39.9 0.8 broadcast_in_dim.23.ex_ref
  40.7 16.7 %outer.1 = (f32[32,4,2,16,128]{4,3,2,1,0:T(8,128)}, f32[4,16,128]{2,1,0:T(8,128)}) custom-call(f32[4,32,8192]{2,1,0:T(8,128)} %u_ref.3, f32[32,8192]{1,0:T(8,128)} %c_ref.3, f32[5,2,8192]{2,1,0:T(2,128)} %copy-done.1, f32[5,2,8192]{2,1,0:T(2,128)} %copy-done.2, f32[5,2,8192]{2,1,0:T(2,128)} %copy-done.1, f32[5,2,8192]{2,1,0:T(2,128)} %copy-done.2, ...), custom_call_target="tpu_custom_call" | custom-call | flops 100000000 | bytes 7000000 | tf_op jit(solution)/shard_map/outer/pallas_call | solution.py:240
  57.5 0.8 pad_maximum_fusion.2
  58.2 6.1 %all-to-all-done.1 = f32[32,4,2,16,128]{4,3,2,1,0:T(8,128)S(1)} async-done(((f32[32,4,2,16,128]{4,3,2,1,0:T(8,128)}), f32[32,4,2,16,128]{4,3,2,1,0:T(8,128)S(1)}, u32[]{:S(2)}, u32[]{:S(2)}) %all-to-all-start.1) | async-done | bytes 2097184 | tf_op jit(solution)/shard_map/all_to_all | solution.py:536
  64.4 0.1 broadcast_in_dim.24
  64.4 23.3 %all_to_all.20.seen_ref = f32[32,72,128]{2,1,0:T(8,128)} all-to-all(f32[32,72,128]{2,1,0:T(8,128)S(1)} %bitcast.16), channel_id=1, replica_groups=mesh['ma_0'=4,'ma_1'=4,'ma_2'=2,'sa'=4] {'ma_0','ma_1','ma_2'}, dimensions={0} | all-to-all | bytes 2359296 | tf_op jit(solution)/shard_map/all_to_all | solution.py:544
  87.7 4.7 %all-to-all-start = ((f32[32,4,2,16,128]{4,3,2,1,0:T(8,128)}), f32[32,4,2,16,128]{4,3,2,1,0:T(8,128)}, u32[]{:S(2)}, u32[]{:S(2)}) async-start(f32[32,4,2,16,128]{4,3,2,1,0:T(8,128)} %get-tuple-element.19), calls=%async_computation | async-start | bytes 4194304 | tf_op jit(solution)/shard_map/all_to_all | solution.py:552
  92.4 5.6 %gram.1 = f32[136,128]{1,0:T(8,128)} custom-call(f32[32,72,128]{2,1,0:T(8,128)} %all_to_all.20.seen_ref), custom_call_target="tpu_custom_call" | custom-call | flops 80000000 | bytes 1700000 | tf_op jit(solution)/shard_map/gram/pallas_call | solution.py:363
  98.1 0.4 collective-permute-start.2
  98.5 1.1 collective-permute-done.2
  99.6 0.9 add.93.p0_ref
  100.5 0.0 copy-start.3
  100.5 3.7 %collective-permute-start.5 = (f32[136,128]{1,0:T(8,128)S(1)}, f32[136,128]{1,0:T(8,128)S(1)}, u32[]{:S(2)}, u32[]{:S(2)}) collective-permute-start(f32[136,128]{1,0:T(8,128)S(1)} %add.93.p0_ref), channel_id=1, source_target_pairs={{0,3},{1,0},{2,1},{3,2},{4,7},{5,4},{6,5},{7,6},{8,11},{9,8},{10,9... | collective-permute-start | bytes 208904 | tf_op jit(solution)/shard_map/ppermute | solution.py:548
  104.2 0.5 collective-permute-start.4
  104.7 0.6 collective-permute-start.3
  105.3 0.3 collective-permute-done.5.p3_ref
  105.6 3.7 %collective-permute-done.4.p2_ref = f32[136,128]{1,0:T(8,128)S(1)} collective-permute-done((f32[136,128]{1,0:T(8,128)S(1)}, f32[136,128]{1,0:T(8,128)S(1)}, u32[]{:S(2)}, u32[]{:S(2)}) %collective-permute-start.4) | collective-permute-done | bytes 69664 | tf_op jit(solution)/shard_map/ppermute | solution.py:548
  109.3 1.6 collective-permute-done.3.p1_ref
  110.9 0.0 copy-done.10
  110.9 0.6 copy-done.12
  111.5 8.0 %mix.1 = (bf16[128,128]{1,0:T(8,128)(2,1)}, bf16[128,128]{1,0:T(8,128)(2,1)}) custom-call(f32[136,128]{1,0:T(8,128)} %copy-done.3, f32[136,128]{1,0:T(8,128)} %copy-done.12, f32[136,128]{1,0:T(8,128)} %copy-done.11, f32[136,128]{1,0:T(8,128)} %copy-done.10), custom_call_target="tpu_custom_call" | custom-call | flops 200000000 | bytes 600000 | tf_op jit(solution)/shard_map/mix/pallas_call | solution.py:439
  119.5 4.5 %transform.2._ = f32[128,32,256]{2,1,0:T(8,128)} custom-call(f32[128,2,16,128]{3,2,1,0:T(8,128)} %bitcast.15, bf16[128,128]{1,0:T(8,128)(2,1)} %get-tuple-element.24.hi_ref, bf16[128,128]{1,0:T(8,128)(2,1)} %get-tuple-element.25.lo_ref), custom_call_target="tpu_custom_call" | custom-call | flops 450000000 | bytes 4300000 | tf_op jit(solution)/shard_map/transform/pallas_call | solution.py:482
  123.9 0.0 all-to-all-done
  124.0 4.5 %transform.3 = f32[128,32,256]{2,1,0:T(8,128)} custom-call(f32[128,2,16,128]{3,2,1,0:T(8,128)} %bitcast.2.f_ref, bf16[128,128]{1,0:T(8,128)(2,1)} %get-tuple-element.24.hi_ref, bf16[128,128]{1,0:T(8,128)(2,1)} %get-tuple-element.25.lo_ref, f32[128,32,256]{2,1,0:T(8,128)} %transform.2._), custom_call_target="tpu_custom_call", output_to_operand_aliasing={{}: (3, {})} | custom-call | flops 450000000 | bytes 4300000 | tf_op jit(solution)/shard_map/transform/pallas_call | solution.py:482
  128.4 58.6 %all_to_all.21 = f32[32,4,32,256]{3,2,1,0:T(8,128)S(1)} all-to-all(f32[32,4,32,256]{3,2,1,0:T(8,128)} %bitcast.13), channel_id=1, replica_groups=mesh['ma_0'=4,'ma_1'=4,'ma_2'=2,'sa'=4] {'ma_0','ma_1','ma_2'}, dimensions={0} | all-to-all | bytes 8388608 | tf_op jit(solution)/shard_map/all_to_all | solution.py:556
  187.0 2.5 %copy.23 = f32[32,4,4,8,256]{4,3,0,2,1:T(8,128)} copy(f32[32,4,4,8,256]{4,3,2,1,0:T(8,128)S(1)} %bitcast.14) | data formatting | bytes 8388608 | tf_op jit(solution)/shard_map/reshape | solution.py:557
  (27 shorter events, 0.1 us)
Async XLA Ops:
  3.0 24.0 %collective-permute-start = (f32[5,2,8192]{2,1,0:T(2,128)S(1)}, f32[5,2,8192]{2,1,0:T(2,128)S(1)}, u32[]{:S(2)}, u32[]{:S(2)}) collective-permute-start(f32[5,2,8192]{2,1,0:T(2,128)S(1)} %pad_maximum_fusion), channel_id=1, source_target_pairs={{0,1},{1,2},{2,3},{4,5},{5,6},{6,7},{8,9},{9,10},{10,11},{12,13},{... | collective-permute-start | bytes 983048 | tf_op jit(solution)/shard_map/ppermute | solution.py:531
  7.1 19.9 %collective-permute-start.1 = (f32[5,2,8192]{2,1,0:T(2,128)S(1)}, f32[5,2,8192]{2,1,0:T(2,128)S(1)}, u32[]{:S(2)}, u32[]{:S(2)}) collective-permute-start(f32[5,2,8192]{2,1,0:T(2,128)S(1)} %pad_maximum_fusion.1), channel_id=1, source_target_pairs={{1,0},{2,1},{3,2},{5,4},{6,5},{7,6},{9,8},{10,9},{11,10},{13,12},{... | collective-permute-start | bytes 983048 | tf_op jit(solution)/shard_map/ppermute | solution.py:532
  11.6 24.5 %copy-start.6 = (s32[32,16]{0,1:T(8,128)S(1)}, s32[32,16]{0,1:T(8,128)}, u32[]{:S(2)}) copy-start(s32[32,16]{0,1:T(8,128)} %param.11) | copy-start | bytes 6148
  11.6 25.2 %copy-start.7 = (f32[32,16]{0,1:T(8,128)S(1)}, f32[32,16]{0,1:T(8,128)}, u32[]{:S(2)}) copy-start(f32[32,16]{0,1:T(8,128)} %param.12) | copy-start | bytes 6148
  11.6 25.9 %copy-start.8 = (f32[32,16]{0,1:T(8,128)S(1)}, f32[32,16]{0,1:T(8,128)}, u32[]{:S(2)}) copy-start(f32[32,16]{0,1:T(8,128)} %param.13) | copy-start | bytes 6148
  11.6 28.3 %copy-start.9 = (s32[4,2]{0,1:T(2,128)S(1)}, s32[4,2]{0,1:T(2,128)}, u32[]{:S(2)}) copy-start(s32[4,2]{0,1:T(2,128)} %param.9) | copy-start | bytes 100
  27.0 13.7 %copy-start.1 = (f32[5,2,8192]{2,1,0:T(2,128)}, f32[5,2,8192]{2,1,0:T(2,128)S(1)}, u32[]{:S(2)}) copy-start(f32[5,2,8192]{2,1,0:T(2,128)S(1)} %collective-permute-done.lo_ref.clo_ref) | copy-start | bytes 983044
  27.0 13.7 %copy-start.2 = (f32[5,2,8192]{2,1,0:T(2,128)}, f32[5,2,8192]{2,1,0:T(2,128)S(1)}, u32[]{:S(2)}) copy-start(f32[5,2,8192]{2,1,0:T(2,128)S(1)} %collective-permute-done.1.hi_ref.chi_ref) | copy-start | bytes 983044
  27.0 37.4 %all-to-all-start.1 = ((f32[32,4,2,16,128]{4,3,2,1,0:T(8,128)}), f32[32,4,2,16,128]{4,3,2,1,0:T(8,128)S(1)}, u32[]{:S(2)}, u32[]{:S(2)}) async-start(f32[32,4,2,16,128]{4,3,2,1,0:T(8,128)} %get-tuple-element.22), calls=%async_computation.1 | async-start | bytes 4194304 | tf_op jit(solution)/shard_map/all_to_all | solution.py:536
  36.1 21.4 %copy-start.5 = (f32[4,16,128]{2,1,0:T(8,128)S(1)}, f32[4,16,128]{2,1,0:T(8,128)}, u32[]{:S(2)}) copy-start(f32[4,16,128]{2,1,0:T(8,128)} %get-tuple-element.20) | copy-start | bytes 98308
  39.8 17.6 %copy-start.4 = (f32[2,8,128]{2,1,0:T(8,128)S(1)}, f32[2,8,128]{2,1,0:T(8,128)}, u32[]{:S(2)}) copy-start(f32[2,8,128]{2,1,0:T(8,128)} %cell_sums.1) | copy-start | bytes 24580
  64.4 33.7 %copy-start = (f32[32,4,2,16,128]{4,3,2,1,0:T(8,128)}, f32[32,4,2,16,128]{4,3,2,1,0:T(8,128)S(1)}, u32[]{:S(2)}) copy-start(f32[32,4,2,16,128]{4,3,2,1,0:T(8,128)S(1)} %all-to-all-done.1) | copy-start | bytes 6291460
  87.7 36.3 %all-to-all-start = ((f32[32,4,2,16,128]{4,3,2,1,0:T(8,128)}), f32[32,4,2,16,128]{4,3,2,1,0:T(8,128)}, u32[]{:S(2)}, u32[]{:S(2)}) async-start(f32[32,4,2,16,128]{4,3,2,1,0:T(8,128)} %get-tuple-element.19), calls=%async_computation | async-start | bytes 4194304 | tf_op jit(solution)/shard_map/all_to_all | solution.py:552
  98.1 1.5 collective-permute-start.2
  100.5 10.4 %copy-start.3 = (f32[136,128]{1,0:T(8,128)}, f32[136,128]{1,0:T(8,128)S(1)}, u32[]{:S(2)}) copy-start(f32[136,128]{1,0:T(8,128)S(1)} %add.93.p0_ref) | copy-start | bytes 208900
  100.5 5.1 %collective-permute-start.5 = (f32[136,128]{1,0:T(8,128)S(1)}, f32[136,128]{1,0:T(8,128)S(1)}, u32[]{:S(2)}, u32[]{:S(2)}) collective-permute-start(f32[136,128]{1,0:T(8,128)S(1)} %add.93.p0_ref), channel_id=1, source_target_pairs={{0,3},{1,0},{2,1},{3,2},{4,7},{5,4},{6,5},{7,6},{8,11},{9,8},{10,9... | collective-permute-start | bytes 208904 | tf_op jit(solution)/shard_map/ppermute | solution.py:548
  104.2 5.1 %collective-permute-start.4 = (f32[136,128]{1,0:T(8,128)S(1)}, f32[136,128]{1,0:T(8,128)S(1)}, u32[]{:S(2)}, u32[]{:S(2)}) collective-permute-start(f32[136,128]{1,0:T(8,128)S(1)} %add.93.p0_ref), channel_id=1, source_target_pairs={{0,2},{1,3},{2,0},{3,1},{4,6},{5,7},{6,4},{7,5},{8,10},{9,11},{10,... | collective-permute-start | bytes 208904 | tf_op jit(solution)/shard_map/ppermute | solution.py:548
  104.7 6.1 %collective-permute-start.3 = (f32[136,128]{1,0:T(8,128)S(1)}, f32[136,128]{1,0:T(8,128)S(1)}, u32[]{:S(2)}, u32[]{:S(2)}) collective-permute-start(f32[136,128]{1,0:T(8,128)S(1)} %add.93.p0_ref), channel_id=1, source_target_pairs={{0,1},{1,2},{2,3},{3,0},{4,5},{5,6},{6,7},{7,4},{8,9},{9,10},{10,1... | collective-permute-start | bytes 208904 | tf_op jit(solution)/shard_map/ppermute | solution.py:548
  105.6 5.3 %copy-start.10 = (f32[136,128]{1,0:T(8,128)}, f32[136,128]{1,0:T(8,128)S(1)}, u32[]{:S(2)}) copy-start(f32[136,128]{1,0:T(8,128)S(1)} %collective-permute-done.5.p3_ref) | copy-start | bytes 208900
  109.3 1.6 copy-start.11
  110.9 0.6 copy-start.12

commit v5 on v4

--- a/solution.py
+++ b/solution.py
@@ -131,12 +131,25 @@
     _close(ref, pitch)
 
 
-def _two_steps(m, e_ref, ce_ref, u1_ref, ex_ref, ey_ref, surf_ref, pitch, step1, step2, edged, put):
+def _two_steps(m, members, laser_ref, e_ref, ce_ref, u1_ref, ey_ref, pitch, plane_at, step1, step2, edged, put):
+    sub = lax.broadcasted_iota(jnp.int32, (8, LANES), 0)
+    lane = lax.broadcasted_iota(jnp.int32, (8, LANES), 1)
+    last_layer = (lane & (DEPTH - 1)) == DEPTH - 1
+    for t in range(STEPS):
+        for g in range(0, DEPTH, 8):
+            y = sub + g + jnp.where(lane < DEPTH, 0, DEPTH)
+            dy = (y - laser_ref[members + m, t]).astype(jnp.float32)
+            ey_ref[t, pl.ds(g, 8), :] = jnp.where(last_layer, jnp.exp(-(dy * dy) / beam_spot_width), 0.0)
+
     def ey_row(t):
-        return lambda y: ey_ref[0, t, pl.ds(y, 1), :]
+        return lambda y: ey_ref[t, pl.ds(y, 1), :]
 
     def factors(t, base, tiles):
-        return [ex_ref[0, t, pl.ds(base + i, 8, stride=tiles), :] for i in range(tiles)]
+        found = []
+        for i in range(tiles):
+            dx = (plane_at(base + i + tiles * sub) - laser_ref[m, t]).astype(jnp.float32)
+            found.append((step_dt * laser_power) * jnp.exp(-(dx * dx) / beam_spot_width))
+        return found
 
     base, tiles, apart = step1
 
@@ -166,7 +179,7 @@
 OUTER_ROW = 8
 
 
-def _inner_body(u_ref, c_ref, ex_ref, ey_ref, out_ref, surf_ref, e_ref, ce_ref, u1_ref):
+def _inner_body(laser_ref, u_ref, c_ref, out_ref, surf_ref, e_ref, ce_ref, u1_ref, ey_ref):
     m = pl.program_id(0)
     planes = u_ref.shape[1]
     half = planes // 2
@@ -183,7 +196,8 @@
         out[pl.ds(v * half + i, 8, stride=2), :] = value
 
     tops = _two_steps(
-        m, e_ref, ce_ref, u1_ref, ex_ref, ey_ref, surf_ref, pitch, (4, 3, 1), (8, 2, 1), False, put
+        m, pl.num_programs(0), laser_ref, e_ref, ce_ref, u1_ref, ey_ref, pitch,
+        lambda row: laser_ref[laser_ref.shape[0] - 1, 0] + row, (4, 3, 1), (8, 2, 1), False, put,
     )
     surf = surf_ref.reshape(half, LANES)
     for i in range(2):
@@ -191,7 +205,8 @@
 
 
 def _outer_body(
-    u_ref, c_ref, lo_ref, hi_ref, clo_ref, chi_ref, ex_ref, ey_ref, out_ref, surf_ref, e_ref, ce_ref, u1_ref
+    laser_ref, u_ref, c_ref, lo_ref, hi_ref, clo_ref, chi_ref, out_ref, surf_ref, e_ref, ce_ref, u1_ref,
+    ey_ref,
 ):
     m = pl.program_id(0)
     planes = u_ref.shape[1]
@@ -227,24 +242,25 @@
     def put(v, i, value):
         out[pl.ds(pl.multiple_of(v * half + 8 * i, 8), 8), :] = value
 
+    def plane_at(row):
+        return laser_ref[laser_ref.shape[0] - 1, 0] + ((row - OUTER_ROW) >> 1) - 2 + (row & 1) * (planes - 8)
+
     tops = _two_steps(
-        m, e_ref, ce_ref, u1_ref, ex_ref, ey_ref, surf_ref, pitch,
+        m, pl.num_programs(0), laser_ref, e_ref, ce_ref, u1_ref, ey_ref, pitch, plane_at,
         (OUTER_ROW, 3, 2), (OUTER_ROW + 4, 2, 2), True, put,
     )
     for i in range(2):
         surf_ref[0, pl.ds(8 * i, 8), :] = tops[i]
 
 
-def _forecast_call(body, name, pitch, operands, specs, ex, ey, members, planes, blocks, halves):
+def _forecast_call(body, name, pitch, lasers, operands, specs, shape, blocks):
+    members, planes, columns = shape
+    halves = columns // blocks // LANES
     scratch = pltpu.VMEM(((DEPTH + 1) * pitch, LANES), jnp.float32)
     return pl.pallas_call(
         body,
         grid=(members,),
-        in_specs=specs
-        + [
-            pl.BlockSpec((1, STEPS, pitch, LANES), lambda m: (m, 0, 0, 0)),
-            pl.BlockSpec((1, STEPS, DEPTH, LANES), lambda m: (m, 0, 0, 0)),
-        ],
+        in_specs=[pl.BlockSpec(memory_space=pltpu.SMEM)] + specs,
         out_specs=[
             pl.BlockSpec((blocks, 1, halves, planes // 2, LANES), lambda m: (0, m, 0, 0, 0)),
             pl.BlockSpec((1, planes // 2, LANES), lambda m: (m, 0, 0)),
@@ -253,27 +269,25 @@
             jax.ShapeDtypeStruct((blocks, members, halves, planes // 2, LANES), jnp.float32),
             jax.ShapeDtypeStruct((members, planes // 2, LANES), jnp.float32),
         ],
-        scratch_shapes=[scratch, scratch, scratch],
+        scratch_shapes=[scratch, scratch, scratch, pltpu.VMEM((STEPS, DEPTH, LANES), jnp.float32)],
         compiler_params=pltpu.CompilerParams(
             dimension_semantics=("arbitrary",), vmem_limit_bytes=VMEM_BYTES
         ),
         cost_estimate=pl.CostEstimate(flops=100_000_000, bytes_accessed=7_000_000, transcendentals=0),
         name=name,
-    )(*operands, ex, ey)
-
-
-def forecast_inner(u, cond, ex, ey, blocks):
+    )(lasers, *operands)
+
+
+def forecast_inner(lasers, u, cond, blocks):
     members, planes, columns = u.shape
     specs = [
         pl.BlockSpec((1, planes, columns), lambda m: (m, 0, 0)),
         pl.BlockSpec((planes, columns), lambda m: (0, 0)),
     ]
-    return _forecast_call(
-        _inner_body, "inner", INNER_PITCH, (u, cond), specs, ex, ey, members, planes, blocks, columns // blocks // LANES
-    )
-
-
-def forecast_outer(u, cond, low, high, ex, ey, blocks):
+    return _forecast_call(_inner_body, "inner", INNER_PITCH, lasers, (u, cond), specs, u.shape, blocks)
+
+
+def forecast_outer(lasers, u, cond, low, high, blocks):
     members, planes, columns = u.shape
     edge = lambda at: pl.BlockSpec((1, 2, columns), at)
     specs = [
@@ -285,9 +299,7 @@
         edge(lambda m: (members, 0, 0)),
     ]
     operands = (u, cond, low, high, low, high)
-    return _forecast_call(
-        _outer_body, "outer", OUTER_PITCH, operands, specs, ex, ey, members, planes, blocks, columns // blocks // LANES
-    )
+    return _forecast_call(_outer_body, "outer", OUTER_PITCH, lasers, operands, specs, u.shape, blocks)
 
 
 def _nt(a, b):
@@ -344,18 +356,20 @@
     )
     wsums = [w_one, w_two]
     rsums = [r_one, r_two]
-    gram = jnp.zeros((count, count), jnp.float32)
-    proj = jnp.zeros((8, count), jnp.float32)
-    for x in range(planes):
-        s = s_ref[pl.ds(x, count, stride=planes), :]
-        wsum = wsums[x // 8][x % 8 : x % 8 + 1]
-        rsum = rsums[x // 8][x % 8 : x % 8 + 1]
-        mean = jnp.sum(s, axis=0, keepdims=True) * (1.0 / count)
-        anom = s - mean
-        gram = gram + _nt(anom * wsum, anom)
-        proj = proj + _nt(jnp.broadcast_to(rsum - wsum * mean, (8, LANES)), anom)
-    out_ref[pl.ds(0, count), :] = gram
-    out_ref[pl.ds(count, 8), :] = proj
+    both = jnp.zeros((count + 8, count), jnp.float32)
+    for x0 in range(0, planes, 2):
+        left, right = [], []
+        for x in (x0, x0 + 1):
+            s = s_ref[pl.ds(x, count, stride=planes), :]
+            wsum = wsums[x // 8][x % 8 : x % 8 + 1]
+            rsum = rsums[x // 8][x % 8 : x % 8 + 1]
+            mean = jnp.sum(s, axis=0, keepdims=True) * (1.0 / count)
+            anom = s - mean
+            q = jnp.broadcast_to(rsum - wsum * mean, (8, LANES))
+            left.append(jnp.concatenate([anom * wsum, q], axis=0))
+            right.append(anom)
+        both = both + _nt(jnp.concatenate(left, axis=1), jnp.concatenate(right, axis=1))
+    out_ref[...] = both
 
 
 def gram_part(seen, members, planes):
@@ -370,7 +384,7 @@
     )(seen)
 
 
-GROUP = 4
+GROUP = 8
 
 
 def _mix_body(p0_ref, p1_ref, p2_ref, p3_ref, hi_ref, lo_ref, a_ref):
@@ -452,15 +466,15 @@
     lo = lo_ref[...]
     src = f_ref.reshape(count * 8, LANES)
     dst = out_ref.reshape(count * 8, LANES)
-    for x in range(8):
-        rows = pl.ds(x, count, stride=8)
-        f = src[rows, :]
+    wide = jnp.concatenate([hi, hi], axis=1)
+    for x in range(0, 8, 2):
+        f = jnp.concatenate([src[pl.ds(x + i, count, stride=8), :] for i in range(2)], axis=1)
         fhi = f.astype(jnp.bfloat16)
         flo = (f - fhi.astype(jnp.float32)).astype(jnp.bfloat16)
-        out = jnp.dot(hi, fhi, preferred_element_type=jnp.float32)
-        out = out + jnp.dot(hi, flo, preferred_element_type=jnp.float32)
+        out = jnp.dot(wide, jnp.concatenate([fhi, flo], axis=0), preferred_element_type=jnp.float32)
         out = out + jnp.dot(lo, fhi, preferred_element_type=jnp.float32)
-        dst[rows, :] = out
+        for i in range(2):
+            dst[pl.ds(x + i, count, stride=8), :] = out[:, i * LANES : (i + 1) * LANES]
 
 
 def _transform_more(f_ref, hi_ref, lo_ref, _, out_ref):
@@ -494,28 +508,6 @@
     )(*operands)
 
 
-def heat_in_x(laser_x, xs):
-    dx = (xs[None, None, :] - laser_x[:, :, None]).astype(jnp.float32)
-    ex = (step_dt * laser_power) * jnp.exp(-(dx * dx) / beam_spot_width)
-    return jnp.broadcast_to(ex[..., None], ex.shape + (LANES,))
-
-
-def heat_in_y(laser_y):
-    lane = jnp.arange(LANES, dtype=jnp.int32)
-    ys = jnp.arange(DEPTH, dtype=jnp.int32)[:, None] + (lane // DEPTH * DEPTH)[None, :]
-    dy = (ys - laser_y[:, :, None, None]).astype(jnp.float32)
-    return jnp.where(lane % DEPTH == DEPTH - 1, jnp.exp(-(dy * dy) / beam_spot_width), 0.0)
-
-
-def inner_planes(first):
-    return first + jnp.arange(INNER_PITCH, dtype=jnp.int32)
-
-
-def outer_planes(first, planes):
-    row = jnp.arange(OUTER_PITCH, dtype=jnp.int32) - OUTER_ROW
-    return first + row // 2 - 2 + (row % 2) * (planes - 8)
-
-
 def per_device(initial_heat_matrix, conductivity, laser_x, laser_y, pixel_cell, observed, obs_var):
     members, planes, columns = initial_heat_matrix.shape
     blocks = 1
@@ -530,12 +522,11 @@
     bottom = jnp.concatenate([u[:, :2], conductivity[None, :2]], axis=0)
     low = lax.ppermute(top, "sa", forward)
     high = lax.ppermute(bottom, "sa", backward)
-    ey = heat_in_y(laser_y)
-    sent_in, surf_in = forecast_inner(u, conductivity, heat_in_x(laser_x, inner_planes(first)), ey, blocks)
+    lasers = jnp.concatenate([laser_x, laser_y, jnp.broadcast_to(first, (1, STEPS))], axis=0)
+    sent_in, surf_in = forecast_inner(lasers, u, conductivity, blocks)
     sent_in, low, high = lax.optimization_barrier((sent_in, low, high))
     held_in = lax.all_to_all(sent_in, MA, 0, 0, tiled=True)
-    ex = heat_in_x(laser_x, outer_planes(first, planes))
-    sent_out, surf_out = forecast_outer(u, conductivity, low, high, ex, ey, blocks)
+    sent_out, surf_out = forecast_outer(lasers, u, conductivity, low, high, blocks)
 
     sums = cell_sums(pixel_cell, observed, obs_var)
     rows = jnp.concatenate([jnp.stack([surf_in, surf_out]).reshape(2, members * planes // 2, LANES), sums], axis=1)

time: 190 us -> 185 us (0.974)
  Pallas kernels: 56.4 us -> 52.4 us
    pallas_call x1, Pallas kernels: 5.64 us -> 3.32 us  [gram_part(): pl.pallas_call(functools.partial(_gram_body, members, planes), out_shape=...]
  transfers between devices with their start and end apart: 8 -> 8, of which waited for: 5 -> 6; matrix products, arithmetic and copies ran while one was open for 4% -> 3% of each run, Pallas kernels for 27% -> 26%
where the time goes in v5:
time: 185 us; the launch traced here: 184 us
  blocking collectives  81 us (44%)
  Pallas kernels  52.4 us (28%)
  starting transfers between devices  24.3 us (13%)
  waiting for transfers between devices  14.5 us (8%)
  local copies, waits for them, and re-layouts  8.83 us (5%)
  other arithmetic  2.74 us (1%)
    all_to_all x1, blocking collectives, per_device(): lax.all_to_all(done.reshape((blocks, members) + done.shape[1:]), MA, 0, 0...  57.7 us
    pallas_call x2, Pallas kernels, _forecast_call(): pl.pallas_call(body, grid=(members,), in_specs=[pl.BlockSpec(memory_space...  32.2 us
    all_to_all x1, blocking collectives, per_device(): seen = lax.all_to_all(rows, MA, 0, 0, tiled=True)  23.2 us
    all_to_all x1, starting transfers between devices, per_device(): held_in = lax.all_to_all(sent_in, MA, 0, 0, tiled=True)  9.07 us
    pallas_call x2, Pallas kernels, transform(): pl.pallas_call(_transform_body if onto is None else _transform_more, grid...  8.81 us
    all_to_all x1, waiting for transfers between devices, per_device(): held_in = lax.all_to_all(sent_in, MA, 0, 0, tiled=True)  6.89 us
    pallas_call x1, Pallas kernels, mix_matrices(): pl.pallas_call(_mix_body, out_shape=[shape, shape], scratch_shapes=[pltpu...  6.35 us
    ppermute x3, waiting for transfers between devices, per_device(): lax.ppermute(part, 'sa', [(i, (i + s) % slabs) for i in range(slabs)])  5.53 us
  transfers between devices with their start and end apart: 8, of which 6 were waited for; matrix products, arithmetic and copies ran while one was open for 3% of the time, Pallas kernels for 26%

profile of v5, /device:TPU:1, one launch (start us, length us, event | category | flops | bytes accessed | tf_op | source)
XLA Modules:
  0.0 183.9 jit_solution(14885282263345605139)
XLA Ops:
  0.0 1.1 slice_bitcast_fusion
  1.1 1.7 fusion
  2.8 0.2 pad_maximum_fusion
  3.0 4.0 %collective-permute-start = (f32[5,2,8192]{2,1,0:T(2,128)S(1)}, f32[5,2,8192]{2,1,0:T(2,128)S(1)}, u32[]{:S(2)}, u32[]{:S(2)}) collective-permute-start(f32[5,2,8192]{2,1,0:T(2,128)S(1)} %pad_maximum_fusion), channel_id=1, source_target_pairs={{0,1},{1,2},{2,3},{4,5},{5,6},{6,7},{8,9},{9,10},{10,11},{12,13},{... | collective-permute-start | bytes 983048 | tf_op jit(solution)/shard_map/ppermute | solution.py:523
  6.9 0.2 pad_maximum_fusion.1
  7.1 1.3 collective-permute-start.1
  8.4 0.1 pad.9.clone
  8.5 0.8 add_add_fusion
  9.3 0.7 copy.16.laser_ref
  9.9 15.3 %inner.1 = (f32[32,4,2,16,128]{4,3,2,1,0:T(8,128)}, f32[4,16,128]{2,1,0:T(8,128)}) custom-call(s32[9,2]{1,0:T(8,128)} %copy.16.laser_ref, f32[4,32,8192]{2,1,0:T(8,128)} %u_ref.3, f32[32,8192]{1,0:T(8,128)} %c_ref.3), custom_call_target="tpu_custom_call" | custom-call | flops 100000000 | bytes 7000000 | tf_op jit(solution)/shard_map/inner/pallas_call | solution.py:260
  25.3 0.0 collective-permute-done.lo_ref.clo_ref
  25.3 0.0 collective-permute-done.1.hi_ref.chi_ref
  25.3 0.0 copy-start.2
  25.3 9.1 %all-to-all-start.1 = ((f32[32,4,2,16,128]{4,3,2,1,0:T(8,128)}), f32[32,4,2,16,128]{4,3,2,1,0:T(8,128)S(1)}, u32[]{:S(2)}, u32[]{:S(2)}) async-start(f32[32,4,2,16,128]{4,3,2,1,0:T(8,128)} %get-tuple-element.22), calls=%async_computation.1 | async-start | bytes 4194304 | tf_op jit(solution)/shard_map/all_to_all | solution.py:528
  34.4 0.0 copy-done.6
  34.4 0.0 copy-start.5
  34.4 0.7 copy.17.pc_ref
  35.1 0.0 copy-done.7
  35.1 0.7 copy.18.obs_ref
  35.8 0.0 copy-done.8
  35.8 0.7 copy.19.var_ref
  36.4 1.7 cell_sums.1
  38.2 16.9 %outer.1 = (f32[32,4,2,16,128]{4,3,2,1,0:T(8,128)}, f32[4,16,128]{2,1,0:T(8,128)}) custom-call(s32[9,2]{1,0:T(8,128)} %copy.16.laser_ref, f32[4,32,8192]{2,1,0:T(8,128)} %u_ref.3, f32[32,8192]{1,0:T(8,128)} %c_ref.3, f32[5,2,8192]{2,1,0:T(2,128)} %copy-done.1, f32[5,2,8192]{2,1,0:T(2,128)} %copy-done.2, f32[5,2,8192]{2,1,0:T(2,128)} %copy-done.1, ...), custom_call_target="tpu_custom_call" | custom-call | flops 100000000 | bytes 7000000 | tf_op jit(solution)/shard_map/outer/pallas_call | solution.py:260
  55.0 0.0 copy-done.4
  55.0 0.8 pad_maximum_fusion.2
  55.8 6.9 %all-to-all-done.1 = f32[32,4,2,16,128]{4,3,2,1,0:T(8,128)S(1)} async-done(((f32[32,4,2,16,128]{4,3,2,1,0:T(8,128)}), f32[32,4,2,16,128]{4,3,2,1,0:T(8,128)S(1)}, u32[]{:S(2)}, u32[]{:S(2)}) %all-to-all-start.1) | async-done | bytes 2097184 | tf_op jit(solution)/shard_map/all_to_all | solution.py:528
  62.7 0.1 broadcast_in_dim.18
  62.8 23.2 %all_to_all.20.seen_ref = f32[32,72,128]{2,1,0:T(8,128)} all-to-all(f32[32,72,128]{2,1,0:T(8,128)S(1)} %bitcast.17), channel_id=1, replica_groups=mesh['ma_0'=4,'ma_1'=4,'ma_2'=2,'sa'=4] {'ma_0','ma_1','ma_2'}, dimensions={0} | all-to-all | bytes 2359296 | tf_op jit(solution)/shard_map/all_to_all | solution.py:535
  86.0 4.8 %all-to-all-start = ((f32[32,4,2,16,128]{4,3,2,1,0:T(8,128)}), f32[32,4,2,16,128]{4,3,2,1,0:T(8,128)}, u32[]{:S(2)}, u32[]{:S(2)}) async-start(f32[32,4,2,16,128]{4,3,2,1,0:T(8,128)} %get-tuple-element.19), calls=%async_computation | async-start | bytes 4194304 | tf_op jit(solution)/shard_map/all_to_all | solution.py:543
  90.8 3.3 %gram.1 = f32[136,128]{1,0:T(8,128)} custom-call(f32[32,72,128]{2,1,0:T(8,128)} %all_to_all.20.seen_ref), custom_call_target="tpu_custom_call" | custom-call | flops 80000000 | bytes 1700000 | tf_op jit(solution)/shard_map/gram/pallas_call | solution.py:377
  94.1 0.4 collective-permute-start.2
  94.5 1.1 collective-permute-done.2
  95.6 0.9 add.3.p0_ref
  96.5 0.0 copy-start.3
  96.6 3.7 %collective-permute-start.5 = (f32[136,128]{1,0:T(8,128)S(1)}, f32[136,128]{1,0:T(8,128)S(1)}, u32[]{:S(2)}, u32[]{:S(2)}) collective-permute-start(f32[136,128]{1,0:T(8,128)S(1)} %add.3.p0_ref), channel_id=1, source_target_pairs={{0,3},{1,0},{2,1},{3,2},{4,7},{5,4},{6,5},{7,6},{8,11},{9,8},{10,9... | collective-permute-start | bytes 208904 | tf_op jit(solution)/shard_map/ppermute | solution.py:539
  100.3 0.5 collective-permute-start.4
  100.8 0.6 collective-permute-start.3
  101.4 0.3 collective-permute-done.5.p3_ref
  101.6 3.7 %collective-permute-done.4.p2_ref = f32[136,128]{1,0:T(8,128)S(1)} collective-permute-done((f32[136,128]{1,0:T(8,128)S(1)}, f32[136,128]{1,0:T(8,128)S(1)}, u32[]{:S(2)}, u32[]{:S(2)}) %collective-permute-start.4) | collective-permute-done | bytes 69664 | tf_op jit(solution)/shard_map/ppermute | solution.py:539
  105.3 1.6 collective-permute-done.3.p1_ref
  106.9 0.0 copy-done.3
  106.9 0.6 copy-done.11
  107.5 6.4 %mix.1 = (bf16[128,128]{1,0:T(8,128)(2,1)}, bf16[128,128]{1,0:T(8,128)(2,1)}) custom-call(f32[136,128]{1,0:T(8,128)} %copy-done.3, f32[136,128]{1,0:T(8,128)} %copy-done.11, f32[136,128]{1,0:T(8,128)} %copy-done.10, f32[136,128]{1,0:T(8,128)} %copy-done.9), custom_call_target="tpu_custom_call" | custom-call | flops 200000000 | bytes 600000 | tf_op jit(solution)/shard_map/mix/pallas_call | solution.py:453
  113.9 4.4 %transform.2._ = f32[128,32,256]{2,1,0:T(8,128)} custom-call(f32[128,2,16,128]{3,2,1,0:T(8,128)} %bitcast.16, bf16[128,128]{1,0:T(8,128)(2,1)} %get-tuple-element.24.hi_ref, bf16[128,128]{1,0:T(8,128)(2,1)} %get-tuple-element.25.lo_ref), custom_call_target="tpu_custom_call" | custom-call | flops 450000000 | bytes 4300000 | tf_op jit(solution)/shard_map/transform/pallas_call | solution.py:496
  118.3 0.9 all-to-all-done
  119.2 4.4 %transform.3 = f32[128,32,256]{2,1,0:T(8,128)} custom-call(f32[128,2,16,128]{3,2,1,0:T(8,128)} %bitcast.2.f_ref, bf16[128,128]{1,0:T(8,128)(2,1)} %get-tuple-element.24.hi_ref, bf16[128,128]{1,0:T(8,128)(2,1)} %get-tuple-element.25.lo_ref, f32[128,32,256]{2,1,0:T(8,128)} %transform.2._), custom_call_target="tpu_custom_call", output_to_operand_aliasing={{}: (3, {})} | custom-call | flops 450000000 | bytes 4300000 | tf_op jit(solution)/shard_map/transform/pallas_call | solution.py:496
  123.6 57.7 %all_to_all.21 = f32[32,4,32,256]{3,2,1,0:T(8,128)S(1)} all-to-all(f32[32,4,32,256]{3,2,1,0:T(8,128)} %bitcast.14), channel_id=1, replica_groups=mesh['ma_0'=4,'ma_1'=4,'ma_2'=2,'sa'=4] {'ma_0','ma_1','ma_2'}, dimensions={0} | all-to-all | bytes 8388608 | tf_op jit(solution)/shard_map/all_to_all | solution.py:547
  181.4 2.5 %copy.21 = f32[32,4,4,8,256]{4,3,0,2,1:T(8,128)} copy(f32[32,4,4,8,256]{4,3,2,1,0:T(8,128)S(1)} %bitcast.15) | data formatting | bytes 8388608 | tf_op jit(solution)/shard_map/reshape | solution.py:548
  (15 shorter events, 0.0 us)
Async XLA Ops:
  3.0 22.3 %collective-permute-start = (f32[5,2,8192]{2,1,0:T(2,128)S(1)}, f32[5,2,8192]{2,1,0:T(2,128)S(1)}, u32[]{:S(2)}, u32[]{:S(2)}) collective-permute-start(f32[5,2,8192]{2,1,0:T(2,128)S(1)} %pad_maximum_fusion), channel_id=1, source_target_pairs={{0,1},{1,2},{2,3},{4,5},{5,6},{6,7},{8,9},{9,10},{10,11},{12,13},{... | collective-permute-start | bytes 983048 | tf_op jit(solution)/shard_map/ppermute | solution.py:523
  7.1 18.2 %collective-permute-start.1 = (f32[5,2,8192]{2,1,0:T(2,128)S(1)}, f32[5,2,8192]{2,1,0:T(2,128)S(1)}, u32[]{:S(2)}, u32[]{:S(2)}) collective-permute-start(f32[5,2,8192]{2,1,0:T(2,128)S(1)} %pad_maximum_fusion.1), channel_id=1, source_target_pairs={{1,0},{2,1},{3,2},{5,4},{6,5},{7,6},{9,8},{10,9},{11,10},{13,12},{... | collective-permute-start | bytes 983048 | tf_op jit(solution)/shard_map/ppermute | solution.py:524
  9.9 24.5 %copy-start.6 = (s32[32,16]{0,1:T(8,128)S(1)}, s32[32,16]{0,1:T(8,128)}, u32[]{:S(2)}) copy-start(s32[32,16]{0,1:T(8,128)} %param.11) | copy-start | bytes 6148
  9.9 25.1 %copy-start.7 = (f32[32,16]{0,1:T(8,128)S(1)}, f32[32,16]{0,1:T(8,128)}, u32[]{:S(2)}) copy-start(f32[32,16]{0,1:T(8,128)} %param.12) | copy-start | bytes 6148
  9.9 25.8 %copy-start.8 = (f32[32,16]{0,1:T(8,128)S(1)}, f32[32,16]{0,1:T(8,128)}, u32[]{:S(2)}) copy-start(f32[32,16]{0,1:T(8,128)} %param.13) | copy-start | bytes 6148
  25.3 12.9 %copy-start.1 = (f32[5,2,8192]{2,1,0:T(2,128)}, f32[5,2,8192]{2,1,0:T(2,128)S(1)}, u32[]{:S(2)}) copy-start(f32[5,2,8192]{2,1,0:T(2,128)S(1)} %collective-permute-done.lo_ref.clo_ref) | copy-start | bytes 983044
  25.3 12.8 %copy-start.2 = (f32[5,2,8192]{2,1,0:T(2,128)}, f32[5,2,8192]{2,1,0:T(2,128)S(1)}, u32[]{:S(2)}) copy-start(f32[5,2,8192]{2,1,0:T(2,128)S(1)} %collective-permute-done.1.hi_ref.chi_ref) | copy-start | bytes 983044
  25.3 37.4 %all-to-all-start.1 = ((f32[32,4,2,16,128]{4,3,2,1,0:T(8,128)}), f32[32,4,2,16,128]{4,3,2,1,0:T(8,128)S(1)}, u32[]{:S(2)}, u32[]{:S(2)}) async-start(f32[32,4,2,16,128]{4,3,2,1,0:T(8,128)} %get-tuple-element.22), calls=%async_computation.1 | async-start | bytes 4194304 | tf_op jit(solution)/shard_map/all_to_all | solution.py:528
  34.4 20.6 %copy-start.5 = (f32[4,16,128]{2,1,0:T(8,128)S(1)}, f32[4,16,128]{2,1,0:T(8,128)}, u32[]{:S(2)}) copy-start(f32[4,16,128]{2,1,0:T(8,128)} %get-tuple-element.20) | copy-start | bytes 98308
  38.1 16.9 %copy-start.4 = (f32[2,8,128]{2,1,0:T(8,128)S(1)}, f32[2,8,128]{2,1,0:T(8,128)}, u32[]{:S(2)}) copy-start(f32[2,8,128]{2,1,0:T(8,128)} %cell_sums.1) | copy-start | bytes 24580
  62.7 31.4 %copy-start = (f32[32,4,2,16,128]{4,3,2,1,0:T(8,128)}, f32[32,4,2,16,128]{4,3,2,1,0:T(8,128)S(1)}, u32[]{:S(2)}) copy-start(f32[32,4,2,16,128]{4,3,2,1,0:T(8,128)S(1)} %all-to-all-done.1) | copy-start | bytes 6291460
  86.0 33.2 %all-to-all-start = ((f32[32,4,2,16,128]{4,3,2,1,0:T(8,128)}), f32[32,4,2,16,128]{4,3,2,1,0:T(8,128)}, u32[]{:S(2)}, u32[]{:S(2)}) async-start(f32[32,4,2,16,128]{4,3,2,1,0:T(8,128)} %get-tuple-element.19), calls=%async_computation | async-start | bytes 4194304 | tf_op jit(solution)/shard_map/all_to_all | solution.py:543
  94.1 1.5 collective-permute-start.2
  96.5 10.4 %copy-start.3 = (f32[136,128]{1,0:T(8,128)}, f32[136,128]{1,0:T(8,128)S(1)}, u32[]{:S(2)}) copy-start(f32[136,128]{1,0:T(8,128)S(1)} %add.3.p0_ref) | copy-start | bytes 208900
  96.6 5.1 %collective-permute-start.5 = (f32[136,128]{1,0:T(8,128)S(1)}, f32[136,128]{1,0:T(8,128)S(1)}, u32[]{:S(2)}, u32[]{:S(2)}) collective-permute-start(f32[136,128]{1,0:T(8,128)S(1)} %add.3.p0_ref), channel_id=1, source_target_pairs={{0,3},{1,0},{2,1},{3,2},{4,7},{5,4},{6,5},{7,6},{8,11},{9,8},{10,9... | collective-permute-start | bytes 208904 | tf_op jit(solution)/shard_map/ppermute | solution.py:539
  100.3 5.1 %collective-permute-start.4 = (f32[136,128]{1,0:T(8,128)S(1)}, f32[136,128]{1,0:T(8,128)S(1)}, u32[]{:S(2)}, u32[]{:S(2)}) collective-permute-start(f32[136,128]{1,0:T(8,128)S(1)} %add.3.p0_ref), channel_id=1, source_target_pairs={{0,2},{1,3},{2,0},{3,1},{4,6},{5,7},{6,4},{7,5},{8,10},{9,11},{10,... | collective-permute-start | bytes 208904 | tf_op jit(solution)/shard_map/ppermute | solution.py:539
  100.8 6.1 %collective-permute-start.3 = (f32[136,128]{1,0:T(8,128)S(1)}, f32[136,128]{1,0:T(8,128)S(1)}, u32[]{:S(2)}, u32[]{:S(2)}) collective-permute-start(f32[136,128]{1,0:T(8,128)S(1)} %add.3.p0_ref), channel_id=1, source_target_pairs={{0,1},{1,2},{2,3},{3,0},{4,5},{5,6},{6,7},{7,4},{8,9},{9,10},{10,1... | collective-permute-start | bytes 208904 | tf_op jit(solution)/shard_map/ppermute | solution.py:539
  101.6 5.3 %copy-start.9 = (f32[136,128]{1,0:T(8,128)}, f32[136,128]{1,0:T(8,128)S(1)}, u32[]{:S(2)}) copy-start(f32[136,128]{1,0:T(8,128)S(1)} %collective-permute-done.5.p3_ref) | copy-start | bytes 208900
  105.3 1.6 copy-start.10
  106.9 0.6 copy-start.11

commit v6 on v5

--- a/solution.py
+++ b/solution.py
@@ -179,7 +179,9 @@
 OUTER_ROW = 8
 
 
-def _inner_body(laser_ref, u_ref, c_ref, out_ref, surf_ref, e_ref, ce_ref, u1_ref, ey_ref):
+def _inner_body(
+    laser_ref, u_ref, c_ref, out_ref, surf_ref, bottom_ref, top_ref, e_ref, ce_ref, u1_ref, ey_ref
+):
     m = pl.program_id(0)
     planes = u_ref.shape[1]
     half = planes // 2
@@ -188,7 +190,11 @@
     @pl.when(m == 0)
     def _():
         _fill(ce_ref, pitch, [(lambda r, c: c_ref[r, c], 8 * i, 8, 8 * i, 1) for i in range(planes // 8)])
-
+        bottom_ref[bottom_ref.shape[0] - 1] = c_ref[pl.ds(0, 2), :]
+        top_ref[top_ref.shape[0] - 1] = c_ref[pl.ds(planes - 2, 2), :]
+
+    bottom_ref[m] = u_ref[0, pl.ds(0, 2), :]
+    top_ref[m] = u_ref[0, pl.ds(planes - 2, 2), :]
     _fill(e_ref, pitch, [(lambda r, c: u_ref[0, r, c], 8 * i, 8, 8 * i, 1) for i in range(planes // 8)])
     out = out_ref.reshape(DEPTH * half, LANES)
 
@@ -253,10 +259,12 @@
         surf_ref[0, pl.ds(8 * i, 8), :] = tops[i]
 
 
-def _forecast_call(body, name, pitch, lasers, operands, specs, shape, blocks):
+def _forecast_call(body, name, pitch, lasers, operands, specs, shape, blocks, edges=False):
     members, planes, columns = shape
     halves = columns // blocks // LANES
     scratch = pltpu.VMEM(((DEPTH + 1) * pitch, LANES), jnp.float32)
+    edge_spec = [pl.BlockSpec((members + 1, 2, columns), lambda m: (0, 0, 0))] * 2 if edges else []
+    edge_shape = [jax.ShapeDtypeStruct((members + 1, 2, columns), jnp.float32)] * 2 if edges else []
     return pl.pallas_call(
         body,
         grid=(members,),
@@ -264,11 +272,13 @@
         out_specs=[
             pl.BlockSpec((blocks, 1, halves, planes // 2, LANES), lambda m: (0, m, 0, 0, 0)),
             pl.BlockSpec((1, planes // 2, LANES), lambda m: (m, 0, 0)),
-        ],
+        ]
+        + edge_spec,
         out_shape=[
             jax.ShapeDtypeStruct((blocks, members, halves, planes // 2, LANES), jnp.float32),
             jax.ShapeDtypeStruct((members, planes // 2, LANES), jnp.float32),
-        ],
+        ]
+        + edge_shape,
         scratch_shapes=[scratch, scratch, scratch, pltpu.VMEM((STEPS, DEPTH, LANES), jnp.float32)],
         compiler_params=pltpu.CompilerParams(
             dimension_semantics=("arbitrary",), vmem_limit_bytes=VMEM_BYTES
@@ -284,7 +294,7 @@
         pl.BlockSpec((1, planes, columns), lambda m: (m, 0, 0)),
         pl.BlockSpec((planes, columns), lambda m: (0, 0)),
     ]
-    return _forecast_call(_inner_body, "inner", INNER_PITCH, lasers, (u, cond), specs, u.shape, blocks)
+    return _forecast_call(_inner_body, "inner", INNER_PITCH, lasers, (u, cond), specs, u.shape, blocks, True)
 
 
 def forecast_outer(lasers, u, cond, low, high, blocks):
@@ -518,13 +528,10 @@
     u = initial_heat_matrix
     forward = [(i, i + 1) for i in range(slabs - 1)]
     backward = [(b, a) for a, b in forward]
-    top = jnp.concatenate([u[:, planes - 2 :], conductivity[None, planes - 2 :]], axis=0)
-    bottom = jnp.concatenate([u[:, :2], conductivity[None, :2]], axis=0)
+    lasers = jnp.concatenate([laser_x, laser_y, jnp.broadcast_to(first, (1, STEPS))], axis=0)
+    sent_in, surf_in, bottom, top = forecast_inner(lasers, u, conductivity, blocks)
     low = lax.ppermute(top, "sa", forward)
     high = lax.ppermute(bottom, "sa", backward)
-    lasers = jnp.concatenate([laser_x, laser_y, jnp.broadcast_to(first, (1, STEPS))], axis=0)
-    sent_in, surf_in = forecast_inner(lasers, u, conductivity, blocks)
-    sent_in, low, high = lax.optimization_barrier((sent_in, low, high))
     held_in = lax.all_to_all(sent_in, MA, 0, 0, tiled=True)
     sent_out, surf_out = forecast_outer(lasers, u, conductivity, low, high, blocks)
 

time: 185 us -> 183 us (0.989)
  blocking collectives: 81 us -> 83.2 us
  local copies, waits for them, and re-layouts: 8.83 us -> 6.78 us
    all_to_all x1, waiting for transfers between devices: 6.89 us -> 0.01 us  [per_device(): held_in = lax.all_to_all(sent_in, MA, 0, 0, tiled=True)]
    all_to_all x1, blocking collectives: 23.2 us -> 27.2 us  [per_device(): seen = lax.all_to_all(rows, MA, 0, 0, tiled=True)]
    ppermute x1, waiting for transfers between devices: 0.01 us -> 3.82 us  [per_device(): high = lax.ppermute(bottom, 'sa', backward)]
    all_to_all x1, waiting for transfers between devices: 0.91 us -> 3.42 us  [per_device(): held_out = lax.all_to_all(sent_out, MA, 0, 0, tiled=True)]
  transfers between devices with their start and end apart: 8 -> 8, of which waited for: 6 -> 7; matrix products, arithmetic and copies ran while one was open for 3% -> 2% of each run, Pallas kernels for 26% -> 18%
where the time goes in v6:
time: 183 us
  blocking collectives  83.2 us (45%)
  Pallas kernels  52.7 us (29%)
  starting transfers between devices  22.7 us (12%)
  waiting for transfers between devices  14.6 us (8%)
  local copies, waits for them, and re-layouts  6.78 us (4%)
  other arithmetic  2.43 us (1%)
    all_to_all x1, blocking collectives, per_device(): lax.all_to_all(done.reshape((blocks, members) + done.shape[1:]), MA, 0, 0...  55.9 us
    pallas_call x2, Pallas kernels, _forecast_call(): pl.pallas_call(body, grid=(members,), in_specs=[pl.BlockSpec(memory_space...  32.5 us
    all_to_all x1, blocking collectives, per_device(): seen = lax.all_to_all(rows, MA, 0, 0, tiled=True)  27.2 us
    all_to_all x1, starting transfers between devices, per_device(): held_in = lax.all_to_all(sent_in, MA, 0, 0, tiled=True)  9.75 us
    pallas_call x2, Pallas kernels, transform(): pl.pallas_call(_transform_body if onto is None else _transform_more, grid...  8.82 us
    pallas_call x1, Pallas kernels, mix_matrices(): pl.pallas_call(_mix_body, out_shape=[shape, shape], scratch_shapes=[pltpu...  6.35 us
    all_to_all x1, starting transfers between devices, per_device(): held_out = lax.all_to_all(sent_out, MA, 0, 0, tiled=True)  4.75 us
    ppermute x3, waiting for transfers between devices, per_device(): lax.ppermute(part, 'sa', [(i, (i + s) % slabs) for i in range(slabs)])  4.46 us
  transfers between devices with their start and end apart: 8, of which 7 were waited for; matrix products, arithmetic and copies ran while one was open for 2% of the time, Pallas kernels for 18%

profile of v6, /device:TPU:1, one launch (start us, length us, event | category | flops | bytes accessed | tf_op | source)
XLA Modules:
  0.0 182.5 jit_solution(2660945548758662025)
XLA Ops:
  0.0 0.1 pad.5.clone
  0.1 0.8 add_add_fusion
  0.8 0.7 copy.16.laser_ref
  1.5 15.6 %inner.1 = (f32[32,4,2,16,128]{4,3,2,1,0:T(8,128)}, f32[4,16,128]{2,1,0:T(8,128)}, f32[5,2,8192]{2,1,0:T(2,128)}, f32[5,2,8192]{2,1,0:T(2,128)}) custom-call(s32[9,2]{1,0:T(8,128)} %copy.16.laser_ref, f32[4,32,8192]{2,1,0:T(8,128)} %u_ref.3, f32[32,8192]{1,0:T(8,128)} %c_ref.3), custom_call_target="tpu_custom_call" | custom-call | flops 100000000 | bytes 7000000 | tf_op jit(solution)/shard_map/inner/pallas_call | solution.py:268
  17.2 0.0 copy-start.10
  17.2 0.0 copy-start.9
  17.2 0.0 copy-start.6
  17.2 0.0 copy-start.7
  17.2 0.0 copy-start.8
  17.2 9.7 %all-to-all-start.1 = ((f32[32,4,2,16,128]{4,3,2,1,0:T(8,128)}), f32[32,4,2,16,128]{4,3,2,1,0:T(8,128)S(1)}, u32[]{:S(2)}, u32[]{:S(2)}) async-start(f32[32,4,2,16,128]{4,3,2,1,0:T(8,128)} %get-tuple-element.20), calls=%async_computation.1 | async-start | bytes 4194304 | tf_op jit(solution)/shard_map/all_to_all | solution.py:535
  27.0 0.0 copy-done.10
  27.0 3.1 %collective-permute-start = (f32[5,2,8192]{2,1,0:T(2,128)S(1)}, f32[5,2,8192]{2,1,0:T(2,128)S(1)}, u32[]{:S(2)}, u32[]{:S(2)}) collective-permute-start(f32[5,2,8192]{2,1,0:T(2,128)S(1)} %copy-done.10), channel_id=1, source_target_pairs={{0,1},{1,2},{2,3},{4,5},{5,6},{6,7},{8,9},{9,10},{10,11},{12,13},{... | collective-permute-start | bytes 983048 | tf_op jit(solution)/shard_map/ppermute | solution.py:533
  30.1 0.0 copy-done.9
  30.1 1.3 collective-permute-start.1
  31.4 0.0 copy-done.6
  31.5 0.7 copy.17.pc_ref
  32.1 0.0 copy-done.7
  32.1 0.7 copy.18.obs_ref
  32.8 0.7 copy.19.var_ref
  33.5 1.7 cell_sums.1
  35.2 1.8 collective-permute-done.lo_ref.clo_ref
  37.0 3.8 %collective-permute-done.1.hi_ref.chi_ref = f32[5,2,8192]{2,1,0:T(2,128)S(1)} collective-permute-done((f32[5,2,8192]{2,1,0:T(2,128)S(1)}, f32[5,2,8192]{2,1,0:T(2,128)S(1)}, u32[]{:S(2)}, u32[]{:S(2)}) %collective-permute-start.1) | collective-permute-done | bytes 327712 | tf_op jit(solution)/shard_map/ppermute | solution.py:534
  40.8 0.7 copy-done.2
  41.5 16.8 %outer.1 = (f32[32,4,2,16,128]{4,3,2,1,0:T(8,128)}, f32[4,16,128]{2,1,0:T(8,128)}) custom-call(s32[9,2]{1,0:T(8,128)} %copy.16.laser_ref, f32[4,32,8192]{2,1,0:T(8,128)} %u_ref.3, f32[32,8192]{1,0:T(8,128)} %c_ref.3, f32[5,2,8192]{2,1,0:T(2,128)} %copy-done.1, f32[5,2,8192]{2,1,0:T(2,128)} %copy-done.2, f32[5,2,8192]{2,1,0:T(2,128)} %copy-done.1, ...), custom_call_target="tpu_custom_call" | custom-call | flops 100000000 | bytes 7000000 | tf_op jit(solution)/shard_map/outer/pallas_call | solution.py:268
  58.4 0.8 pad_maximum_fusion
  59.2 0.0 all-to-all-done.1
  59.2 0.1 broadcast_in_dim.10
  59.3 27.2 %all_to_all.20.seen_ref = f32[32,72,128]{2,1,0:T(8,128)} all-to-all(f32[32,72,128]{2,1,0:T(8,128)S(1)} %bitcast.13), channel_id=1, replica_groups=mesh['ma_0'=4,'ma_1'=4,'ma_2'=2,'sa'=4] {'ma_0','ma_1','ma_2'}, dimensions={0} | all-to-all | bytes 2359296 | tf_op jit(solution)/shard_map/all_to_all | solution.py:542
  86.5 4.8 %all-to-all-start = ((f32[32,4,2,16,128]{4,3,2,1,0:T(8,128)}), f32[32,4,2,16,128]{4,3,2,1,0:T(8,128)}, u32[]{:S(2)}, u32[]{:S(2)}) async-start(f32[32,4,2,16,128]{4,3,2,1,0:T(8,128)} %get-tuple-element.17), calls=%async_computation | async-start | bytes 4194304 | tf_op jit(solution)/shard_map/all_to_all | solution.py:550
  91.3 3.3 %gram.1 = f32[136,128]{1,0:T(8,128)} custom-call(f32[32,72,128]{2,1,0:T(8,128)} %all_to_all.20.seen_ref), custom_call_target="tpu_custom_call" | custom-call | flops 80000000 | bytes 1700000 | tf_op jit(solution)/shard_map/gram/pallas_call | solution.py:387
  94.6 0.4 collective-permute-start.2
  95.0 1.1 collective-permute-done.2
  96.1 0.9 add.3.p0_ref
  97.0 0.0 copy-start.3
  97.0 0.6 collective-permute-start.5
  97.6 2.5 %collective-permute-start.4 = (f32[136,128]{1,0:T(8,128)S(1)}, f32[136,128]{1,0:T(8,128)S(1)}, u32[]{:S(2)}, u32[]{:S(2)}) collective-permute-start(f32[136,128]{1,0:T(8,128)S(1)} %add.3.p0_ref), channel_id=1, source_target_pairs={{0,2},{1,3},{2,0},{3,1},{4,6},{5,7},{6,4},{7,5},{8,10},{9,11},{10,... | collective-permute-start | bytes 208904 | tf_op jit(solution)/shard_map/ppermute | solution.py:546
  100.1 0.3 collective-permute-start.3
  100.4 0.3 collective-permute-done.5.p3_ref
  100.7 2.0 %collective-permute-done.4.p2_ref = f32[136,128]{1,0:T(8,128)S(1)} collective-permute-done((f32[136,128]{1,0:T(8,128)S(1)}, f32[136,128]{1,0:T(8,128)S(1)}, u32[]{:S(2)}, u32[]{:S(2)}) %collective-permute-start.4) | collective-permute-done | bytes 69664 | tf_op jit(solution)/shard_map/ppermute | solution.py:546
  102.7 2.2 %collective-permute-done.3.p1_ref = f32[136,128]{1,0:T(8,128)S(1)} collective-permute-done((f32[136,128]{1,0:T(8,128)S(1)}, f32[136,128]{1,0:T(8,128)S(1)}, u32[]{:S(2)}, u32[]{:S(2)}) %collective-permute-start.3) | collective-permute-done | bytes 69664 | tf_op jit(solution)/shard_map/ppermute | solution.py:546
  104.9 0.0 copy-done.11
  104.9 0.6 copy-done.13
  105.5 6.4 %mix.1 = (bf16[128,128]{1,0:T(8,128)(2,1)}, bf16[128,128]{1,0:T(8,128)(2,1)}) custom-call(f32[136,128]{1,0:T(8,128)} %copy-done.3, f32[136,128]{1,0:T(8,128)} %copy-done.13, f32[136,128]{1,0:T(8,128)} %copy-done.12, f32[136,128]{1,0:T(8,128)} %copy-done.11), custom_call_target="tpu_custom_call" | custom-call | flops 200000000 | bytes 600000 | tf_op jit(solution)/shard_map/mix/pallas_call | solution.py:463
  111.9 4.4 %transform.2._ = f32[128,32,256]{2,1,0:T(8,128)} custom-call(f32[128,2,16,128]{3,2,1,0:T(8,128)} %bitcast.12, bf16[128,128]{1,0:T(8,128)(2,1)} %get-tuple-element.22.hi_ref, bf16[128,128]{1,0:T(8,128)(2,1)} %get-tuple-element.23.lo_ref), custom_call_target="tpu_custom_call" | custom-call | flops 450000000 | bytes 4300000 | tf_op jit(solution)/shard_map/transform/pallas_call | solution.py:506
  116.3 3.4 %all-to-all-done = f32[32,4,2,16,128]{4,3,2,1,0:T(8,128)} async-done(((f32[32,4,2,16,128]{4,3,2,1,0:T(8,128)}), f32[32,4,2,16,128]{4,3,2,1,0:T(8,128)}, u32[]{:S(2)}, u32[]{:S(2)}) %all-to-all-start) | async-done | bytes 2097184 | tf_op jit(solution)/shard_map/all_to_all | solution.py:550
  119.7 4.4 %transform.3 = f32[128,32,256]{2,1,0:T(8,128)} custom-call(f32[128,2,16,128]{3,2,1,0:T(8,128)} %bitcast.f_ref, bf16[128,128]{1,0:T(8,128)(2,1)} %get-tuple-element.22.hi_ref, bf16[128,128]{1,0:T(8,128)(2,1)} %get-tuple-element.23.lo_ref, f32[128,32,256]{2,1,0:T(8,128)} %transform.2._), custom_call_target="tpu_custom_call", output_to_operand_aliasing={{}: (3, {})} | custom-call | flops 450000000 | bytes 4300000 | tf_op jit(solution)/shard_map/transform/pallas_call | solution.py:506
  124.1 55.9 %all_to_all.21 = f32[32,4,32,256]{3,2,1,0:T(8,128)S(1)} all-to-all(f32[32,4,32,256]{3,2,1,0:T(8,128)} %bitcast.10), channel_id=1, replica_groups=mesh['ma_0'=4,'ma_1'=4,'ma_2'=2,'sa'=4] {'ma_0','ma_1','ma_2'}, dimensions={0} | all-to-all | bytes 8388608 | tf_op jit(solution)/shard_map/all_to_all | solution.py:554
  180.0 2.5 %copy.21 = f32[32,4,4,8,256]{4,3,0,2,1:T(8,128)} copy(f32[32,4,4,8,256]{4,3,2,1,0:T(8,128)S(1)} %bitcast.11) | data formatting | bytes 8388608 | tf_op jit(solution)/shard_map/reshape | solution.py:555
  (15 shorter events, 0.0 us)
Async XLA Ops:
  17.2 9.8 %copy-start.10 = (f32[5,2,8192]{2,1,0:T(2,128)S(1)}, f32[5,2,8192]{2,1,0:T(2,128)}, u32[]{:S(2)}) copy-start(f32[5,2,8192]{2,1,0:T(2,128)} %get-tuple-element.15) | copy-start | bytes 983044
  17.2 13.0 %copy-start.9 = (f32[5,2,8192]{2,1,0:T(2,128)S(1)}, f32[5,2,8192]{2,1,0:T(2,128)}, u32[]{:S(2)}) copy-start(f32[5,2,8192]{2,1,0:T(2,128)} %get-tuple-element.16) | copy-start | bytes 983044
  17.2 14.3 %copy-start.6 = (s32[32,16]{0,1:T(8,128)S(1)}, s32[32,16]{0,1:T(8,128)}, u32[]{:S(2)}) copy-start(s32[32,16]{0,1:T(8,128)} %param.11) | copy-start | bytes 6148
  17.2 14.9 %copy-start.7 = (f32[32,16]{0,1:T(8,128)S(1)}, f32[32,16]{0,1:T(8,128)}, u32[]{:S(2)}) copy-start(f32[32,16]{0,1:T(8,128)} %param.12) | copy-start | bytes 6148
  17.2 15.6 %copy-start.8 = (f32[32,16]{0,1:T(8,128)S(1)}, f32[32,16]{0,1:T(8,128)}, u32[]{:S(2)}) copy-start(f32[32,16]{0,1:T(8,128)} %param.13) | copy-start | bytes 6148
  17.2 41.9 %all-to-all-start.1 = ((f32[32,4,2,16,128]{4,3,2,1,0:T(8,128)}), f32[32,4,2,16,128]{4,3,2,1,0:T(8,128)S(1)}, u32[]{:S(2)}, u32[]{:S(2)}) async-start(f32[32,4,2,16,128]{4,3,2,1,0:T(8,128)} %get-tuple-element.20), calls=%async_computation.1 | async-start | bytes 4194304 | tf_op jit(solution)/shard_map/all_to_all | solution.py:535
  27.0 10.0 %collective-permute-start = (f32[5,2,8192]{2,1,0:T(2,128)S(1)}, f32[5,2,8192]{2,1,0:T(2,128)S(1)}, u32[]{:S(2)}, u32[]{:S(2)}) collective-permute-start(f32[5,2,8192]{2,1,0:T(2,128)S(1)} %copy-done.10), channel_id=1, source_target_pairs={{0,1},{1,2},{2,3},{4,5},{5,6},{6,7},{8,9},{9,10},{10,11},{12,13},{... | collective-permute-start | bytes 983048 | tf_op jit(solution)/shard_map/ppermute | solution.py:533
  30.1 10.7 %collective-permute-start.1 = (f32[5,2,8192]{2,1,0:T(2,128)S(1)}, f32[5,2,8192]{2,1,0:T(2,128)S(1)}, u32[]{:S(2)}, u32[]{:S(2)}) collective-permute-start(f32[5,2,8192]{2,1,0:T(2,128)S(1)} %copy-done.9), channel_id=1, source_target_pairs={{1,0},{2,1},{3,2},{5,4},{6,5},{7,6},{9,8},{10,9},{11,10},{13,12},{... | collective-permute-start | bytes 983048 | tf_op jit(solution)/shard_map/ppermute | solution.py:534
  35.2 23.2 %copy-start.4 = (f32[2,8,128]{2,1,0:T(8,128)S(1)}, f32[2,8,128]{2,1,0:T(8,128)}, u32[]{:S(2)}) copy-start(f32[2,8,128]{2,1,0:T(8,128)} %cell_sums.1) | copy-start | bytes 24580
  35.2 23.2 %copy-start.5 = (f32[4,16,128]{2,1,0:T(8,128)S(1)}, f32[4,16,128]{2,1,0:T(8,128)}, u32[]{:S(2)}) copy-start(f32[4,16,128]{2,1,0:T(8,128)} %get-tuple-element.18) | copy-start | bytes 98308
  37.0 3.8 %copy-start.1 = (f32[5,2,8192]{2,1,0:T(2,128)}, f32[5,2,8192]{2,1,0:T(2,128)S(1)}, u32[]{:S(2)}) copy-start(f32[5,2,8192]{2,1,0:T(2,128)S(1)} %collective-permute-done.lo_ref.clo_ref) | copy-start | bytes 983044
  40.8 0.7 copy-start.2
  59.2 27.3 %copy-start = (f32[32,4,2,16,128]{4,3,2,1,0:T(8,128)}, f32[32,4,2,16,128]{4,3,2,1,0:T(8,128)S(1)}, u32[]{:S(2)}) copy-start(f32[32,4,2,16,128]{4,3,2,1,0:T(8,128)S(1)} %all-to-all-done.1) | copy-start | bytes 6291460
  86.5 33.2 %all-to-all-start = ((f32[32,4,2,16,128]{4,3,2,1,0:T(8,128)}), f32[32,4,2,16,128]{4,3,2,1,0:T(8,128)}, u32[]{:S(2)}, u32[]{:S(2)}) async-start(f32[32,4,2,16,128]{4,3,2,1,0:T(8,128)} %get-tuple-element.17), calls=%async_computation | async-start | bytes 4194304 | tf_op jit(solution)/shard_map/all_to_all | solution.py:550
  94.6 1.5 collective-permute-start.2
  97.0 7.8 %copy-start.3 = (f32[136,128]{1,0:T(8,128)}, f32[136,128]{1,0:T(8,128)S(1)}, u32[]{:S(2)}) copy-start(f32[136,128]{1,0:T(8,128)S(1)} %add.3.p0_ref) | copy-start | bytes 208900
  97.0 3.6 %collective-permute-start.5 = (f32[136,128]{1,0:T(8,128)S(1)}, f32[136,128]{1,0:T(8,128)S(1)}, u32[]{:S(2)}, u32[]{:S(2)}) collective-permute-start(f32[136,128]{1,0:T(8,128)S(1)} %add.3.p0_ref), channel_id=1, source_target_pairs={{0,3},{1,0},{2,1},{3,2},{4,7},{5,4},{6,5},{7,6},{8,11},{9,8},{10,9... | collective-permute-start | bytes 208904 | tf_op jit(solution)/shard_map/ppermute | solution.py:546
  97.6 5.1 %collective-permute-start.4 = (f32[136,128]{1,0:T(8,128)S(1)}, f32[136,128]{1,0:T(8,128)S(1)}, u32[]{:S(2)}, u32[]{:S(2)}) collective-permute-start(f32[136,128]{1,0:T(8,128)S(1)} %add.3.p0_ref), channel_id=1, source_target_pairs={{0,2},{1,3},{2,0},{3,1},{4,6},{5,7},{6,4},{7,5},{8,10},{9,11},{10,... | collective-permute-start | bytes 208904 | tf_op jit(solution)/shard_map/ppermute | solution.py:546
  100.1 4.8 %collective-permute-start.3 = (f32[136,128]{1,0:T(8,128)S(1)}, f32[136,128]{1,0:T(8,128)S(1)}, u32[]{:S(2)}, u32[]{:S(2)}) collective-permute-start(f32[136,128]{1,0:T(8,128)S(1)} %add.3.p0_ref), channel_id=1, source_target_pairs={{0,1},{1,2},{2,3},{3,0},{4,5},{5,6},{6,7},{7,4},{8,9},{9,10},{10,1... | collective-permute-start | bytes 208904 | tf_op jit(solution)/shard_map/ppermute | solution.py:546
  100.7 4.2 %copy-start.11 = (f32[136,128]{1,0:T(8,128)}, f32[136,128]{1,0:T(8,128)S(1)}, u32[]{:S(2)}) copy-start(f32[136,128]{1,0:T(8,128)S(1)} %collective-permute-done.5.p3_ref) | copy-start | bytes 208900
  102.7 2.2 %copy-start.12 = (f32[136,128]{1,0:T(8,128)}, f32[136,128]{1,0:T(8,128)S(1)}, u32[]{:S(2)}) copy-start(f32[136,128]{1,0:T(8,128)S(1)} %collective-permute-done.4.p2_ref) | copy-start | bytes 208900
  104.9 0.6 copy-start.13

commit v7 on v6

--- a/solution.py
+++ b/solution.py
@@ -180,7 +180,7 @@
 
 
 def _inner_body(
-    laser_ref, u_ref, c_ref, out_ref, surf_ref, bottom_ref, top_ref, e_ref, ce_ref, u1_ref, ey_ref
+    laser_ref, u_ref, c_ref, out_ref, bottom_ref, top_ref, e_ref, ce_ref, u1_ref, ey_ref, rows_ref
 ):
     m = pl.program_id(0)
     planes = u_ref.shape[1]
@@ -196,18 +196,22 @@
     bottom_ref[m] = u_ref[0, pl.ds(0, 2), :]
     top_ref[m] = u_ref[0, pl.ds(planes - 2, 2), :]
     _fill(e_ref, pitch, [(lambda r, c: u_ref[0, r, c], 8 * i, 8, 8 * i, 1) for i in range(planes // 8)])
-    out = out_ref.reshape(DEPTH * half, LANES)
+    blocks, _, rows, _ = out_ref.shape
+    halves = DEPTH // blocks
+    out = out_ref.reshape(blocks * rows, LANES)
 
     def put(v, i, value):
-        out[pl.ds(v * half + i, 8, stride=2), :] = value
+        row = v * half + lax.div(v, halves) * (rows - halves * half)
+        out[pl.ds(row + i, 8, stride=2), :] = value
 
     tops = _two_steps(
         m, pl.num_programs(0), laser_ref, e_ref, ce_ref, u1_ref, ey_ref, pitch,
         lambda row: laser_ref[laser_ref.shape[0] - 1, 0] + row, (4, 3, 1), (8, 2, 1), False, put,
     )
-    surf = surf_ref.reshape(half, LANES)
     for i in range(2):
-        surf[pl.ds(i, 8, stride=2), :] = tops[i]
+        rows_ref[pl.ds(i, 8, stride=2), :] = tops[i]
+    for d in range(blocks):
+        out_ref[d, 0, pl.ds(halves * half, 8), :] = rows_ref[pl.ds(8 * (d % 2), 8), :]
 
 
 def _outer_body(
@@ -259,27 +263,15 @@
         surf_ref[0, pl.ds(8 * i, 8), :] = tops[i]
 
 
-def _forecast_call(body, name, pitch, lasers, operands, specs, shape, blocks, edges=False):
-    members, planes, columns = shape
-    halves = columns // blocks // LANES
+def _forecast_call(body, name, pitch, lasers, operands, specs, out_specs, out_shape, more_scratch):
     scratch = pltpu.VMEM(((DEPTH + 1) * pitch, LANES), jnp.float32)
-    edge_spec = [pl.BlockSpec((members + 1, 2, columns), lambda m: (0, 0, 0))] * 2 if edges else []
-    edge_shape = [jax.ShapeDtypeStruct((members + 1, 2, columns), jnp.float32)] * 2 if edges else []
     return pl.pallas_call(
         body,
-        grid=(members,),
+        grid=(operands[0].shape[0],),
         in_specs=[pl.BlockSpec(memory_space=pltpu.SMEM)] + specs,
-        out_specs=[
-            pl.BlockSpec((blocks, 1, halves, planes // 2, LANES), lambda m: (0, m, 0, 0, 0)),
-            pl.BlockSpec((1, planes // 2, LANES), lambda m: (m, 0, 0)),
-        ]
-        + edge_spec,
-        out_shape=[
-            jax.ShapeDtypeStruct((blocks, members, halves, planes // 2, LANES), jnp.float32),
-            jax.ShapeDtypeStruct((members, planes // 2, LANES), jnp.float32),
-        ]
-        + edge_shape,
-        scratch_shapes=[scratch, scratch, scratch, pltpu.VMEM((STEPS, DEPTH, LANES), jnp.float32)],
+        out_specs=out_specs,
+        out_shape=[jax.ShapeDtypeStruct(shape, jnp.float32) for shape in out_shape],
+        scratch_shapes=[scratch, scratch, scratch, pltpu.VMEM((STEPS, DEPTH, LANES), jnp.float32)] + more_scratch,
         compiler_params=pltpu.CompilerParams(
             dimension_semantics=("arbitrary",), vmem_limit_bytes=VMEM_BYTES
         ),
@@ -290,15 +282,26 @@
 
 def forecast_inner(lasers, u, cond, blocks):
     members, planes, columns = u.shape
+    rows = columns // blocks // LANES * (planes // 2) + 8
+    edge = (members + 1, 2, columns)
     specs = [
         pl.BlockSpec((1, planes, columns), lambda m: (m, 0, 0)),
         pl.BlockSpec((planes, columns), lambda m: (0, 0)),
     ]
-    return _forecast_call(_inner_body, "inner", INNER_PITCH, lasers, (u, cond), specs, u.shape, blocks, True)
+    out_specs = [
+        pl.BlockSpec((blocks, 1, rows, LANES), lambda m: (0, m, 0, 0)),
+        pl.BlockSpec(edge, lambda m: (0, 0, 0)),
+        pl.BlockSpec(edge, lambda m: (0, 0, 0)),
+    ]
+    return _forecast_call(
+        _inner_body, "inner", INNER_PITCH, lasers, (u, cond), specs, out_specs,
+        [(blocks, members, rows, LANES), edge, edge], [pltpu.VMEM((planes // 2, LANES), jnp.float32)],
+    )
 
 
 def forecast_outer(lasers, u, cond, low, high, blocks):
     members, planes, columns = u.shape
+    halves = columns // blocks // LANES
     edge = lambda at: pl.BlockSpec((1, 2, columns), at)
     specs = [
         pl.BlockSpec((1, planes, columns), lambda m: (m, 0, 0)),
@@ -308,8 +311,14 @@
         edge(lambda m: (members, 0, 0)),
         edge(lambda m: (members, 0, 0)),
     ]
-    operands = (u, cond, low, high, low, high)
-    return _forecast_call(_outer_body, "outer", OUTER_PITCH, lasers, operands, specs, u.shape, blocks)
+    out_specs = [
+        pl.BlockSpec((blocks, 1, halves, planes // 2, LANES), lambda m: (0, m, 0, 0, 0)),
+        pl.BlockSpec((1, planes // 2, LANES), lambda m: (m, 0, 0)),
+    ]
+    return _forecast_call(
+        _outer_body, "outer", OUTER_PITCH, lasers, (u, cond, low, high, low, high), specs, out_specs,
+        [(blocks, members, halves, planes // 2, LANES), (members, planes // 2, LANES)], [],
+    )
 
 
 def _nt(a, b):
@@ -331,8 +340,7 @@
         wsum = wsum + jnp.where(hit, weight[:, j : j + 1], 0.0)
         rsum = rsum + jnp.where(hit, value[:, j : j + 1], 0.0)
     tiles = [8 * i for i in range(planes // 8)]
-    inner, outer = tiles[1:-1], [tiles[0], tiles[-1]]
-    for part, (one, two) in enumerate((inner, outer)):
+    for part, (one, two) in enumerate(((tiles[1], tiles[0]), (tiles[-2], tiles[-1]))):
         out_ref[part] = (
             wsum[one : one + 8]
             + _roll(rsum[one : one + 8], 64, 1)
@@ -351,28 +359,27 @@
     )(pixel_cell, observed, obs_var)
 
 
-def _gram_body(members, planes, seen_ref, out_ref, s_ref):
+def _gram_body(members, inner_ref, seen_ref, out_ref, s_ref):
     sources = seen_ref.shape[0]
     count = sources * members
+    outer = members * 8
     group = lax.broadcasted_iota(jnp.int32, (8, LANES), 1) // 4
     sums = [jnp.zeros((8, LANES), jnp.float32) for _ in range(4)]
     for i in range(sources):
-        row = seen_ref[i, pl.ds(members * planes, 8), :]
+        row = seen_ref[i, pl.ds(outer, 8), :]
         for g in range(4):
             sums[g] = jnp.where(group == (i + 8 * g) % sources, row, sums[g])
-        s_ref[pl.ds(i * members * planes, members * planes), :] = seen_ref[i, pl.ds(0, members * planes), :]
-    w_one, w_two, r_one, r_two = (
+        s_ref[pl.ds(i * outer, outer), :] = seen_ref[i, pl.ds(0, outer), :]
+    w_in, w_out, r_in, r_out = (
         _roll(sums[g], (LANES - 32 * g) % LANES, 1) if g else sums[g] for g in range(4)
     )
-    wsums = [w_one, w_two]
-    rsums = [r_one, r_two]
     both = jnp.zeros((count + 8, count), jnp.float32)
-    for x0 in range(0, planes, 2):
+    for x in range(8):
         left, right = [], []
-        for x in (x0, x0 + 1):
-            s = s_ref[pl.ds(x, count, stride=planes), :]
-            wsum = wsums[x // 8][x % 8 : x % 8 + 1]
-            rsum = rsums[x // 8][x % 8 : x % 8 + 1]
+        for cells, wsums, rsums in ((inner_ref.reshape(count * 8, LANES), w_in, r_in), (s_ref, w_out, r_out)):
+            s = cells[pl.ds(x, count, stride=8), :]
+            wsum = wsums[x : x + 1]
+            rsum = rsums[x : x + 1]
             mean = jnp.sum(s, axis=0, keepdims=True) * (1.0 / count)
             anom = s - mean
             q = jnp.broadcast_to(rsum - wsum * mean, (8, LANES))
@@ -382,16 +389,23 @@
     out_ref[...] = both
 
 
-def gram_part(seen, members, planes):
-    count = seen.shape[0] * members
+def gram_part(inner, seen, members):
+    count, rows, _ = inner.shape
+    last = rows // 8 - 1
     return pl.pallas_call(
-        functools.partial(_gram_body, members, planes),
+        functools.partial(_gram_body, members),
+        grid=(1,),
+        in_specs=[
+            pl.BlockSpec((count, 8, LANES), lambda i: (0, last, 0)),
+            pl.BlockSpec(seen.shape, lambda i: (0, 0, 0)),
+        ],
+        out_specs=pl.BlockSpec((count + 8, count), lambda i: (0, 0)),
         out_shape=jax.ShapeDtypeStruct((count + 8, count), jnp.float32),
-        scratch_shapes=[pltpu.VMEM((count * planes, LANES), jnp.float32)],
+        scratch_shapes=[pltpu.VMEM((count * 8, LANES), jnp.float32)],
         cost_estimate=pl.CostEstimate(flops=80_000_000, bytes_accessed=1_700_000, transcendentals=0),
         compiler_params=pltpu.CompilerParams(vmem_limit_bytes=VMEM_BYTES),
         name="gram",
-    )(seen)
+    )(inner, seen)
 
 
 GROUP = 8
@@ -491,11 +505,12 @@
     _transform_body(f_ref, hi_ref, lo_ref, out_ref)
 
 
-def transform(block, hi, lo, onto=None):
-    count, halves, planes, _ = block.shape
+def transform(block, planes, hi, lo, onto=None):
+    count = block.shape[0]
     tiles = planes // 8
+    halves = 2
     mat = pl.BlockSpec((count, count), lambda x, c: (0, 0))
-    in_specs = [pl.BlockSpec((count, 1, 8, LANES), lambda x, c: (0, c, x, 0)), mat, mat]
+    in_specs = [pl.BlockSpec((count, 8, LANES), lambda x, c: (0, c * tiles + x, 0)), mat, mat]
     operands = (block, hi, lo)
     if onto is None:
         out_map = lambda x, c: (0, x + 1, c)
@@ -529,18 +544,20 @@
     forward = [(i, i + 1) for i in range(slabs - 1)]
     backward = [(b, a) for a, b in forward]
     lasers = jnp.concatenate([laser_x, laser_y, jnp.broadcast_to(first, (1, STEPS))], axis=0)
-    sent_in, surf_in, bottom, top = forecast_inner(lasers, u, conductivity, blocks)
+    sent_in, bottom, top = forecast_inner(lasers, u, conductivity, blocks)
     low = lax.ppermute(top, "sa", forward)
     high = lax.ppermute(bottom, "sa", backward)
     held_in = lax.all_to_all(sent_in, MA, 0, 0, tiled=True)
     sent_out, surf_out = forecast_outer(lasers, u, conductivity, low, high, blocks)
 
     sums = cell_sums(pixel_cell, observed, obs_var)
-    rows = jnp.concatenate([jnp.stack([surf_in, surf_out]).reshape(2, members * planes // 2, LANES), sums], axis=1)
+    surf = surf_out.reshape(members, 2, planes // 4, LANES).transpose(1, 0, 2, 3)
+    rows = jnp.concatenate([surf.reshape(2, members * planes // 4, LANES), sums], axis=1)
     rows = jnp.broadcast_to(rows[None], (blocks // 2,) + rows.shape).reshape((blocks,) + rows.shape[1:])
     rows, held_in = lax.optimization_barrier((rows, held_in))
     seen = lax.all_to_all(rows, MA, 0, 0, tiled=True)
-    part = gram_part(seen, members, planes // 2)
+    inner = held_in.reshape((blocks * members,) + held_in.shape[2:])
+    part = gram_part(inner, seen, members)
     part = part + lax.ppermute(part, "ma_2", [(0, 1), (1, 0)])
     parts = [part] + [
         lax.ppermute(part, "sa", [(i, (i + s) % slabs) for i in range(slabs)]) for s in range(1, slabs)
@@ -548,9 +565,8 @@
     hi, lo = mix_matrices(parts)
 
     held_out = lax.all_to_all(sent_out, MA, 0, 0, tiled=True)
-    shape = (blocks * members,) + held_in.shape[2:]
-    done = transform(held_in.reshape(shape), hi, lo)
-    done = transform(held_out.reshape(shape), hi, lo, done)
+    done = transform(inner, planes // 2, hi, lo)
+    done = transform(held_out.reshape(blocks * members, -1, LANES), planes // 2, hi, lo, done)
     back = lax.all_to_all(done.reshape((blocks, members) + done.shape[1:]), MA, 0, 0, tiled=True)
     return back.transpose(1, 2, 0, 3).reshape(members, planes, columns)
 

time: 183 us -> 177 us (0.967)
  blocking collectives: 83.2 us -> 75.5 us
  waiting for transfers between devices: 14.6 us -> 16.5 us
    all_to_all x1, blocking collectives: 27.2 us -> 19.7 us  [per_device(): seen = lax.all_to_all(rows, MA, 0, 0, tiled=True)]
  transfers between devices with their start and end apart: 8 -> 8, of which waited for: 7 -> 8; matrix products, arithmetic and copies ran while one was open for 2% -> 2% of each run, Pallas kernels for 18% -> 18%
where the time goes in v7:
time: 177 us; the launch traced here: 176 us
  blocking collectives  75.5 us (43%)
  Pallas kernels  52.6 us (30%)
  starting transfers between devices  22 us (12%)
  waiting for transfers between devices  16.5 us (9%)
  local copies, waits for them, and re-layouts  7.45 us (4%)
    all_to_all x1, blocking collectives, per_device(): lax.all_to_all(done.reshape((blocks, members) + done.shape[1:]), MA, 0, 0...  55.8 us
    pallas_call x2, Pallas kernels, _forecast_call(): pl.pallas_call(body, grid=(operands[0].shape[0],), in_specs=[pl.BlockSpec...  32.6 us
    all_to_all x1, blocking collectives, per_device(): seen = lax.all_to_all(rows, MA, 0, 0, tiled=True)  19.7 us
    all_to_all x1, starting transfers between devices, per_device(): held_in = lax.all_to_all(sent_in, MA, 0, 0, tiled=True)  9.6 us
    pallas_call x2, Pallas kernels, transform(): pl.pallas_call(_transform_body if onto is None else _transform_more, grid...  8.81 us
    pallas_call x1, Pallas kernels, mix_matrices(): pl.pallas_call(_mix_body, out_shape=[shape, shape], scratch_shapes=[pltpu...  6.35 us
    all_to_all x1, starting transfers between devices, per_device(): held_out = lax.all_to_all(sent_out, MA, 0, 0, tiled=True)  4.55 us
    ppermute x3, waiting for transfers between devices, per_device(): lax.ppermute(part, 'sa', [(i, (i + s) % slabs) for i in range(slabs)])  4.45 us
  transfers between devices with their start and end apart: 8, of which 8 were waited for; matrix products, arithmetic and copies ran while one was open for 2% of the time, Pallas kernels for 18%

profile of v7, /device:TPU:1, one launch (start us, length us, event | category | flops | bytes accessed | tf_op | source)
XLA Modules:
  0.0 175.8 jit_solution(9010508412033853963)
XLA Ops:
  0.0 0.1 pad.4.clone
  0.1 0.8 add_add_fusion
  0.8 0.7 copy.23.laser_ref
  1.5 0.0 copy-start.5
  1.5 15.8 %inner.1 = (f32[32,4,40,128]{3,2,1,0:T(8,128)}, f32[5,2,8192]{2,1,0:T(2,128)}, f32[5,2,8192]{2,1,0:T(2,128)}) custom-call(s32[9,2]{1,0:T(8,128)} %copy.23.laser_ref, f32[4,32,8192]{2,1,0:T(8,128)} %u_ref.3, f32[32,8192]{1,0:T(8,128)} %c_ref.3), custom_call_target="tpu_custom_call" | custom-call | flops 100000000 | bytes 7000000 | tf_op jit(solution)/shard_map/inner/pallas_call | solution.py:268
  17.3 9.6 %all-to-all-start.1 = ((f32[32,4,40,128]{3,2,1,0:T(8,128)}), f32[32,4,40,128]{3,2,1,0:T(8,128)S(1)}, u32[]{:S(2)}, u32[]{:S(2)}) async-start(f32[32,4,40,128]{3,2,1,0:T(8,128)} %get-tuple-element.18), calls=%async_computation.1 | async-start | bytes 5242880 | tf_op jit(solution)/shard_map/all_to_all | solution.py:550
  26.9 3.1 %collective-permute-start = (f32[5,2,8192]{2,1,0:T(2,128)}, f32[5,2,8192]{2,1,0:T(2,128)S(1)}, u32[]{:S(2)}, u32[]{:S(2)}) collective-permute-start(f32[5,2,8192]{2,1,0:T(2,128)} %get-tuple-element.14), channel_id=1, source_target_pairs={{0,1},{1,2},{2,3},{4,5},{5,6},{6,7},{8,9},{9,10},{10,11},{12,13},{... | collective-permute-start | bytes 983048 | tf_op jit(solution)/shard_map/ppermute | solution.py:548
  30.1 1.3 collective-permute-start.1
  31.4 0.0 copy-done.5
  31.4 0.7 copy.25.pc_ref
  32.1 0.0 copy-done.6
  32.1 0.7 copy.26.obs_ref
  32.7 0.0 copy-done.7
  32.7 0.7 copy.27.var_ref
  33.4 1.7 cell_sums.1
  35.1 2.1 %collective-permute-done.lo_ref.clo_ref = f32[5,2,8192]{2,1,0:T(2,128)S(1)} collective-permute-done((f32[5,2,8192]{2,1,0:T(2,128)}, f32[5,2,8192]{2,1,0:T(2,128)S(1)}, u32[]{:S(2)}, u32[]{:S(2)}) %collective-permute-start) | collective-permute-done | bytes 327712 | tf_op jit(solution)/shard_map/ppermute | solution.py:548
  37.2 3.7 %collective-permute-done.1.hi_ref.chi_ref = f32[5,2,8192]{2,1,0:T(2,128)S(1)} collective-permute-done((f32[5,2,8192]{2,1,0:T(2,128)}, f32[5,2,8192]{2,1,0:T(2,128)S(1)}, u32[]{:S(2)}, u32[]{:S(2)}) %collective-permute-start.1) | collective-permute-done | bytes 327712 | tf_op jit(solution)/shard_map/ppermute | solution.py:549
  40.9 0.0 copy-done.1
  40.9 0.7 copy-done.2
  41.7 16.8 %outer.1 = (f32[32,4,2,16,128]{4,3,2,1,0:T(8,128)}, f32[4,16,128]{2,1,0:T(8,128)}) custom-call(s32[9,2]{1,0:T(8,128)} %copy.23.laser_ref, f32[4,32,8192]{2,1,0:T(8,128)} %u_ref.3, f32[32,8192]{1,0:T(8,128)} %c_ref.3, f32[5,2,8192]{2,1,0:T(2,128)} %copy-done.1, f32[5,2,8192]{2,1,0:T(2,128)} %copy-done.2, f32[5,2,8192]{2,1,0:T(2,128)} %copy-done.1, ...), custom_call_target="tpu_custom_call" | custom-call | flops 100000000 | bytes 7000000 | tf_op jit(solution)/shard_map/outer/pallas_call | solution.py:268
  58.5 0.8 copy_bitcast_fusion
  59.2 0.0 copy-done.4
  59.2 1.6 all-to-all-done.1
  60.9 19.7 %all_to_all.20.seen_ref = f32[32,40,128]{2,1,0:T(8,128)} all-to-all(f32[32,40,128]{2,1,0:T(8,128)S(1)} %bitcast.19), channel_id=1, replica_groups=mesh['ma_0'=4,'ma_1'=4,'ma_2'=2,'sa'=4] {'ma_0','ma_1','ma_2'}, dimensions={0} | all-to-all | bytes 1310720 | tf_op jit(solution)/shard_map/all_to_all | solution.py:558
  80.5 4.5 %all-to-all-start = ((f32[32,4,2,16,128]{4,3,2,1,0:T(8,128)}), f32[32,4,2,16,128]{4,3,2,1,0:T(8,128)}, u32[]{:S(2)}, u32[]{:S(2)}) async-start(f32[32,4,2,16,128]{4,3,2,1,0:T(8,128)} %get-tuple-element.16), calls=%async_computation | async-start | bytes 4194304 | tf_op jit(solution)/shard_map/all_to_all | solution.py:567
  85.1 0.0 copy-done
  85.1 3.2 %gram.1 = f32[136,128]{1,0:T(8,128)} custom-call(f32[128,40,128]{2,1,0:T(8,128)} %bitcast.16, f32[32,40,128]{2,1,0:T(8,128)} %all_to_all.20.seen_ref), custom_call_target="tpu_custom_call" | custom-call | flops 80000000 | bytes 1700000 | tf_op jit(solution)/shard_map/gram/pallas_call | solution.py:395
  88.3 0.0 collective-permute-start.2
  88.3 1.4 collective-permute-done.2
  89.7 0.9 add.3.p0_ref
  90.6 0.0 copy-start.3
  90.7 0.7 collective-permute-start.5
  91.3 2.4 %collective-permute-start.4 = (f32[136,128]{1,0:T(8,128)S(1)}, f32[136,128]{1,0:T(8,128)S(1)}, u32[]{:S(2)}, u32[]{:S(2)}) collective-permute-start(f32[136,128]{1,0:T(8,128)S(1)} %add.3.p0_ref), channel_id=1, source_target_pairs={{0,2},{1,3},{2,0},{3,1},{4,6},{5,7},{6,4},{7,5},{8,10},{9,11},{10,... | collective-permute-start | bytes 208904 | tf_op jit(solution)/shard_map/ppermute | solution.py:563
  93.7 0.3 collective-permute-start.3
  94.0 0.4 collective-permute-done.5.p3_ref
  94.5 1.9 %collective-permute-done.4.p2_ref = f32[136,128]{1,0:T(8,128)S(1)} collective-permute-done((f32[136,128]{1,0:T(8,128)S(1)}, f32[136,128]{1,0:T(8,128)S(1)}, u32[]{:S(2)}, u32[]{:S(2)}) %collective-permute-start.4) | collective-permute-done | bytes 69664 | tf_op jit(solution)/shard_map/ppermute | solution.py:563
  96.4 2.1 %collective-permute-done.3.p1_ref = f32[136,128]{1,0:T(8,128)S(1)} collective-permute-done((f32[136,128]{1,0:T(8,128)S(1)}, f32[136,128]{1,0:T(8,128)S(1)}, u32[]{:S(2)}, u32[]{:S(2)}) %collective-permute-start.3) | collective-permute-done | bytes 69664 | tf_op jit(solution)/shard_map/ppermute | solution.py:563
  98.5 0.0 copy-done.3
  98.5 0.0 copy-done.8
  98.5 0.0 copy-done.9
  98.5 0.0 copy-start.10
  98.5 0.6 copy-done.10
  99.1 6.4 %mix.1 = (bf16[128,128]{1,0:T(8,128)(2,1)}, bf16[128,128]{1,0:T(8,128)(2,1)}) custom-call(f32[136,128]{1,0:T(8,128)} %copy-done.3, f32[136,128]{1,0:T(8,128)} %copy-done.10, f32[136,128]{1,0:T(8,128)} %copy-done.9, f32[136,128]{1,0:T(8,128)} %copy-done.8), custom_call_target="tpu_custom_call" | custom-call | flops 200000000 | bytes 600000 | tf_op jit(solution)/shard_map/mix/pallas_call | solution.py:477
  105.5 4.4 %transform.2._ = f32[128,32,256]{2,1,0:T(8,128)} custom-call(f32[128,40,128]{2,1,0:T(8,128)} %bitcast.17, bf16[128,128]{1,0:T(8,128)(2,1)} %get-tuple-element.21.hi_ref, bf16[128,128]{1,0:T(8,128)(2,1)} %get-tuple-element.22.lo_ref), custom_call_target="tpu_custom_call" | custom-call | flops 450000000 | bytes 4300000 | tf_op jit(solution)/shard_map/transform/pallas_call | solution.py:521
  109.9 3.3 %all-to-all-done = f32[32,4,2,16,128]{4,3,2,1,0:T(8,128)} async-done(((f32[32,4,2,16,128]{4,3,2,1,0:T(8,128)}), f32[32,4,2,16,128]{4,3,2,1,0:T(8,128)}, u32[]{:S(2)}, u32[]{:S(2)}) %all-to-all-start) | async-done | bytes 2097184 | tf_op jit(solution)/shard_map/all_to_all | solution.py:567
  113.2 4.4 %transform.3 = f32[128,32,256]{2,1,0:T(8,128)} custom-call(f32[128,32,128]{2,1,0:T(8,128)} %bitcast.f_ref, bf16[128,128]{1,0:T(8,128)(2,1)} %get-tuple-element.21.hi_ref, bf16[128,128]{1,0:T(8,128)(2,1)} %get-tuple-element.22.lo_ref, f32[128,32,256]{2,1,0:T(8,128)} %transform.2._), custom_call_target="tpu_custom_call", output_to_operand_aliasing={{}: (3, {})} | custom-call | flops 450000000 | bytes 4300000 | tf_op jit(solution)/shard_map/transform/pallas_call | solution.py:521
  117.6 55.8 %all_to_all.21 = f32[32,4,32,256]{3,2,1,0:T(8,128)S(1)} all-to-all(f32[32,4,32,256]{3,2,1,0:T(8,128)} %bitcast.15), channel_id=1, replica_groups=mesh['ma_0'=4,'ma_1'=4,'ma_2'=2,'sa'=4] {'ma_0','ma_1','ma_2'}, dimensions={0} | all-to-all | bytes 8388608 | tf_op jit(solution)/shard_map/all_to_all | solution.py:570
  173.3 2.5 %copy.29 = f32[32,4,4,8,256]{4,3,0,2,1:T(8,128)} copy(f32[32,4,4,8,256]{4,3,2,1,0:T(8,128)S(1)} %bitcast.18) | data formatting | bytes 8388608 | tf_op jit(solution)/shard_map/reshape | solution.py:571
  (10 shorter events, 0.1 us)
Async XLA Ops:
  1.5 29.8 %copy-start.5 = (s32[32,16]{0,1:T(8,128)S(1)}, s32[32,16]{0,1:T(8,128)}, u32[]{:S(2)}) copy-start(s32[32,16]{0,1:T(8,128)} %param.11) | copy-start | bytes 6148
  1.5 30.5 %copy-start.6 = (f32[32,16]{0,1:T(8,128)S(1)}, f32[32,16]{0,1:T(8,128)}, u32[]{:S(2)}) copy-start(f32[32,16]{0,1:T(8,128)} %param.12) | copy-start | bytes 6148
  1.5 31.2 %copy-start.7 = (f32[32,16]{0,1:T(8,128)S(1)}, f32[32,16]{0,1:T(8,128)}, u32[]{:S(2)}) copy-start(f32[32,16]{0,1:T(8,128)} %param.13) | copy-start | bytes 6148
  17.3 43.5 %all-to-all-start.1 = ((f32[32,4,40,128]{3,2,1,0:T(8,128)}), f32[32,4,40,128]{3,2,1,0:T(8,128)S(1)}, u32[]{:S(2)}, u32[]{:S(2)}) async-start(f32[32,4,40,128]{3,2,1,0:T(8,128)} %get-tuple-element.18), calls=%async_computation.1 | async-start | bytes 5242880 | tf_op jit(solution)/shard_map/all_to_all | solution.py:550
  26.9 10.3 %collective-permute-start = (f32[5,2,8192]{2,1,0:T(2,128)}, f32[5,2,8192]{2,1,0:T(2,128)S(1)}, u32[]{:S(2)}, u32[]{:S(2)}) collective-permute-start(f32[5,2,8192]{2,1,0:T(2,128)} %get-tuple-element.14), channel_id=1, source_target_pairs={{0,1},{1,2},{2,3},{4,5},{5,6},{6,7},{8,9},{9,10},{10,11},{12,13},{... | collective-permute-start | bytes 983048 | tf_op jit(solution)/shard_map/ppermute | solution.py:548
  30.1 10.9 %collective-permute-start.1 = (f32[5,2,8192]{2,1,0:T(2,128)}, f32[5,2,8192]{2,1,0:T(2,128)S(1)}, u32[]{:S(2)}, u32[]{:S(2)}) collective-permute-start(f32[5,2,8192]{2,1,0:T(2,128)} %get-tuple-element.15), channel_id=1, source_target_pairs={{1,0},{2,1},{3,2},{5,4},{6,5},{7,6},{9,8},{10,9},{11,10},{13,12},{... | collective-permute-start | bytes 983048 | tf_op jit(solution)/shard_map/ppermute | solution.py:549
  35.1 24.1 %copy-start.4 = (f32[2,8,128]{2,1,0:T(8,128)S(1)}, f32[2,8,128]{2,1,0:T(8,128)}, u32[]{:S(2)}) copy-start(f32[2,8,128]{2,1,0:T(8,128)} %cell_sums.1) | copy-start | bytes 24580
  37.2 3.7 %copy-start.1 = (f32[5,2,8192]{2,1,0:T(2,128)}, f32[5,2,8192]{2,1,0:T(2,128)S(1)}, u32[]{:S(2)}) copy-start(f32[5,2,8192]{2,1,0:T(2,128)S(1)} %collective-permute-done.lo_ref.clo_ref) | copy-start | bytes 983044
  40.9 0.7 copy-start.2
  60.8 24.3 %copy-start = (f32[32,4,40,128]{3,2,1,0:T(8,128)}, f32[32,4,40,128]{3,2,1,0:T(8,128)S(1)}, u32[]{:S(2)}) copy-start(f32[32,4,40,128]{3,2,1,0:T(8,128)S(1)} %all-to-all-done.1) | copy-start | bytes 7864324
  80.5 32.6 %all-to-all-start = ((f32[32,4,2,16,128]{4,3,2,1,0:T(8,128)}), f32[32,4,2,16,128]{4,3,2,1,0:T(8,128)}, u32[]{:S(2)}, u32[]{:S(2)}) async-start(f32[32,4,2,16,128]{4,3,2,1,0:T(8,128)} %get-tuple-element.16), calls=%async_computation | async-start | bytes 4194304 | tf_op jit(solution)/shard_map/all_to_all | solution.py:567
  88.3 1.5 collective-permute-start.2
  90.6 7.8 %copy-start.3 = (f32[136,128]{1,0:T(8,128)}, f32[136,128]{1,0:T(8,128)S(1)}, u32[]{:S(2)}) copy-start(f32[136,128]{1,0:T(8,128)S(1)} %add.3.p0_ref) | copy-start | bytes 208900
  90.7 3.8 %collective-permute-start.5 = (f32[136,128]{1,0:T(8,128)S(1)}, f32[136,128]{1,0:T(8,128)S(1)}, u32[]{:S(2)}, u32[]{:S(2)}) collective-permute-start(f32[136,128]{1,0:T(8,128)S(1)} %add.3.p0_ref), channel_id=1, source_target_pairs={{0,3},{1,0},{2,1},{3,2},{4,7},{5,4},{6,5},{7,6},{8,11},{9,8},{10,9... | collective-permute-start | bytes 208904 | tf_op jit(solution)/shard_map/ppermute | solution.py:563
  91.3 5.1 %collective-permute-start.4 = (f32[136,128]{1,0:T(8,128)S(1)}, f32[136,128]{1,0:T(8,128)S(1)}, u32[]{:S(2)}, u32[]{:S(2)}) collective-permute-start(f32[136,128]{1,0:T(8,128)S(1)} %add.3.p0_ref), channel_id=1, source_target_pairs={{0,2},{1,3},{2,0},{3,1},{4,6},{5,7},{6,4},{7,5},{8,10},{9,11},{10,... | collective-permute-start | bytes 208904 | tf_op jit(solution)/shard_map/ppermute | solution.py:563
  93.7 4.8 %collective-permute-start.3 = (f32[136,128]{1,0:T(8,128)S(1)}, f32[136,128]{1,0:T(8,128)S(1)}, u32[]{:S(2)}, u32[]{:S(2)}) collective-permute-start(f32[136,128]{1,0:T(8,128)S(1)} %add.3.p0_ref), channel_id=1, source_target_pairs={{0,1},{1,2},{2,3},{3,0},{4,5},{5,6},{6,7},{7,4},{8,9},{9,10},{10,1... | collective-permute-start | bytes 208904 | tf_op jit(solution)/shard_map/ppermute | solution.py:563
  94.5 4.0 %copy-start.8 = (f32[136,128]{1,0:T(8,128)}, f32[136,128]{1,0:T(8,128)S(1)}, u32[]{:S(2)}) copy-start(f32[136,128]{1,0:T(8,128)S(1)} %collective-permute-done.5.p3_ref) | copy-start | bytes 208900
  96.4 2.1 %copy-start.9 = (f32[136,128]{1,0:T(8,128)}, f32[136,128]{1,0:T(8,128)S(1)}, u32[]{:S(2)}) copy-start(f32[136,128]{1,0:T(8,128)S(1)} %collective-permute-done.4.p2_ref) | copy-start | bytes 208900
  98.5 0.6 copy-start.10

commit v8 on v7

--- a/solution.py
+++ b/solution.py
@@ -29,7 +29,7 @@
 
 
 UNROLL = {2: 8, 3: 8}
-FILL_UNROLL = 16
+FILL_UNROLL = 32
 
 
 def _stencil_step(src, cond, pitch, base, tiles, apart, exs, ey_at, emit, surface):

time: 177 us -> 175 us (0.989)
  no operation moved by 1% of the time
where the time goes in v8:
time: 175 us
  blocking collectives  74.8 us (43%)
  Pallas kernels  51.3 us (29%)
  starting transfers between devices  22 us (13%)
  waiting for transfers between devices  17.2 us (10%)
  local copies, waits for them, and re-layouts  7.45 us (4%)
    all_to_all x1, blocking collectives, per_device(): lax.all_to_all(done.reshape((blocks, members) + done.shape[1:]), MA, 0, 0...  55.8 us
    pallas_call x2, Pallas kernels, _forecast_call(): pl.pallas_call(body, grid=(operands[0].shape[0],), in_specs=[pl.BlockSpec...  31.3 us
    all_to_all x1, blocking collectives, per_device(): seen = lax.all_to_all(rows, MA, 0, 0, tiled=True)  19 us
    all_to_all x1, starting transfers between devices, per_device(): held_in = lax.all_to_all(sent_in, MA, 0, 0, tiled=True)  9.6 us
    pallas_call x2, Pallas kernels, transform(): pl.pallas_call(_transform_body if onto is None else _transform_more, grid...  8.81 us
    pallas_call x1, Pallas kernels, mix_matrices(): pl.pallas_call(_mix_body, out_shape=[shape, shape], scratch_shapes=[pltpu...  6.35 us
    ppermute x3, waiting for transfers between devices, per_device(): lax.ppermute(part, 'sa', [(i, (i + s) % slabs) for i in range(slabs)])  4.58 us
    all_to_all x1, starting transfers between devices, per_device(): held_out = lax.all_to_all(sent_out, MA, 0, 0, tiled=True)  4.55 us
  transfers between devices with their start and end apart: 8, of which 8 were waited for; matrix products, arithmetic and copies ran while one was open for 2% of the time, Pallas kernels for 18%

profile of v8, /device:TPU:1, one launch (start us, length us, event | category | flops | bytes accessed | tf_op | source)
XLA Modules:
  0.0 174.5 jit_solution(13353939945040307136)
XLA Ops:
  0.0 0.1 pad.4.clone
  0.1 0.8 add_add_fusion
  0.8 0.7 copy.23.laser_ref
  1.5 0.0 copy-start.5
  1.5 15.1 %inner.1 = (f32[32,4,40,128]{3,2,1,0:T(8,128)}, f32[5,2,8192]{2,1,0:T(2,128)}, f32[5,2,8192]{2,1,0:T(2,128)}) custom-call(s32[9,2]{1,0:T(8,128)} %copy.23.laser_ref, f32[4,32,8192]{2,1,0:T(8,128)} %u_ref.3, f32[32,8192]{1,0:T(8,128)} %c_ref.3), custom_call_target="tpu_custom_call" | custom-call | flops 100000000 | bytes 7000000 | tf_op jit(solution)/shard_map/inner/pallas_call | solution.py:268
  16.7 9.6 %all-to-all-start.1 = ((f32[32,4,40,128]{3,2,1,0:T(8,128)}), f32[32,4,40,128]{3,2,1,0:T(8,128)S(1)}, u32[]{:S(2)}, u32[]{:S(2)}) async-start(f32[32,4,40,128]{3,2,1,0:T(8,128)} %get-tuple-element.18), calls=%async_computation.1 | async-start | bytes 5242880 | tf_op jit(solution)/shard_map/all_to_all | solution.py:550
  26.3 3.1 %collective-permute-start = (f32[5,2,8192]{2,1,0:T(2,128)}, f32[5,2,8192]{2,1,0:T(2,128)S(1)}, u32[]{:S(2)}, u32[]{:S(2)}) collective-permute-start(f32[5,2,8192]{2,1,0:T(2,128)} %get-tuple-element.14), channel_id=1, source_target_pairs={{0,1},{1,2},{2,3},{4,5},{5,6},{6,7},{8,9},{9,10},{10,11},{12,13},{... | collective-permute-start | bytes 983048 | tf_op jit(solution)/shard_map/ppermute | solution.py:548
  29.4 1.3 collective-permute-start.1
  30.7 0.0 copy-done.5
  30.7 0.7 copy.25.pc_ref
  31.4 0.0 copy-done.6
  31.4 0.7 copy.26.obs_ref
  32.1 0.0 copy-done.7
  32.1 0.7 copy.27.var_ref
  32.8 1.7 cell_sums.1
  34.5 2.1 %collective-permute-done.lo_ref.clo_ref = f32[5,2,8192]{2,1,0:T(2,128)S(1)} collective-permute-done((f32[5,2,8192]{2,1,0:T(2,128)}, f32[5,2,8192]{2,1,0:T(2,128)S(1)}, u32[]{:S(2)}, u32[]{:S(2)}) %collective-permute-start) | collective-permute-done | bytes 327712 | tf_op jit(solution)/shard_map/ppermute | solution.py:548
  36.6 3.7 %collective-permute-done.1.hi_ref.chi_ref = f32[5,2,8192]{2,1,0:T(2,128)S(1)} collective-permute-done((f32[5,2,8192]{2,1,0:T(2,128)}, f32[5,2,8192]{2,1,0:T(2,128)S(1)}, u32[]{:S(2)}, u32[]{:S(2)}) %collective-permute-start.1) | collective-permute-done | bytes 327712 | tf_op jit(solution)/shard_map/ppermute | solution.py:549
  40.3 0.0 copy-done.1
  40.3 0.7 copy-done.2
  41.0 16.1 %outer.1 = (f32[32,4,2,16,128]{4,3,2,1,0:T(8,128)}, f32[4,16,128]{2,1,0:T(8,128)}) custom-call(s32[9,2]{1,0:T(8,128)} %copy.23.laser_ref, f32[4,32,8192]{2,1,0:T(8,128)} %u_ref.3, f32[32,8192]{1,0:T(8,128)} %c_ref.3, f32[5,2,8192]{2,1,0:T(2,128)} %copy-done.1, f32[5,2,8192]{2,1,0:T(2,128)} %copy-done.2, f32[5,2,8192]{2,1,0:T(2,128)} %copy-done.1, ...), custom_call_target="tpu_custom_call" | custom-call | flops 100000000 | bytes 7000000 | tf_op jit(solution)/shard_map/outer/pallas_call | solution.py:268
  57.2 0.8 copy_bitcast_fusion
  57.9 0.0 copy-done.4
  57.9 2.2 %all-to-all-done.1 = f32[32,4,40,128]{3,2,1,0:T(8,128)S(1)} async-done(((f32[32,4,40,128]{3,2,1,0:T(8,128)}), f32[32,4,40,128]{3,2,1,0:T(8,128)S(1)}, u32[]{:S(2)}, u32[]{:S(2)}) %all-to-all-start.1) | async-done | bytes 2621472 | tf_op jit(solution)/shard_map/all_to_all | solution.py:550
  60.2 19.0 %all_to_all.20.seen_ref = f32[32,40,128]{2,1,0:T(8,128)} all-to-all(f32[32,40,128]{2,1,0:T(8,128)S(1)} %bitcast.19), channel_id=1, replica_groups=mesh['ma_0'=4,'ma_1'=4,'ma_2'=2,'sa'=4] {'ma_0','ma_1','ma_2'}, dimensions={0} | all-to-all | bytes 1310720 | tf_op jit(solution)/shard_map/all_to_all | solution.py:558
  79.2 4.5 %all-to-all-start = ((f32[32,4,2,16,128]{4,3,2,1,0:T(8,128)}), f32[32,4,2,16,128]{4,3,2,1,0:T(8,128)}, u32[]{:S(2)}, u32[]{:S(2)}) async-start(f32[32,4,2,16,128]{4,3,2,1,0:T(8,128)} %get-tuple-element.16), calls=%async_computation | async-start | bytes 4194304 | tf_op jit(solution)/shard_map/all_to_all | solution.py:567
  83.8 0.0 copy-done
  83.8 3.2 %gram.1 = f32[136,128]{1,0:T(8,128)} custom-call(f32[128,40,128]{2,1,0:T(8,128)} %bitcast.16, f32[32,40,128]{2,1,0:T(8,128)} %all_to_all.20.seen_ref), custom_call_target="tpu_custom_call" | custom-call | flops 80000000 | bytes 1700000 | tf_op jit(solution)/shard_map/gram/pallas_call | solution.py:395
  87.0 0.0 collective-permute-start.2
  87.0 1.4 collective-permute-done.2
  88.4 0.9 add.3.p0_ref
  89.3 0.0 copy-start.3
  89.3 0.9 collective-permute-start.5
  90.2 2.2 %collective-permute-start.4 = (f32[136,128]{1,0:T(8,128)S(1)}, f32[136,128]{1,0:T(8,128)S(1)}, u32[]{:S(2)}, u32[]{:S(2)}) collective-permute-start(f32[136,128]{1,0:T(8,128)S(1)} %add.3.p0_ref), channel_id=1, source_target_pairs={{0,2},{1,3},{2,0},{3,1},{4,6},{5,7},{6,4},{7,5},{8,10},{9,11},{10,... | collective-permute-start | bytes 208904 | tf_op jit(solution)/shard_map/ppermute | solution.py:563
  92.4 0.3 collective-permute-start.3
  92.7 0.4 collective-permute-done.5.p3_ref
  93.2 2.1 %collective-permute-done.4.p2_ref = f32[136,128]{1,0:T(8,128)S(1)} collective-permute-done((f32[136,128]{1,0:T(8,128)S(1)}, f32[136,128]{1,0:T(8,128)S(1)}, u32[]{:S(2)}, u32[]{:S(2)}) %collective-permute-start.4) | collective-permute-done | bytes 69664 | tf_op jit(solution)/shard_map/ppermute | solution.py:563
  95.3 2.0 %collective-permute-done.3.p1_ref = f32[136,128]{1,0:T(8,128)S(1)} collective-permute-done((f32[136,128]{1,0:T(8,128)S(1)}, f32[136,128]{1,0:T(8,128)S(1)}, u32[]{:S(2)}, u32[]{:S(2)}) %collective-permute-start.3) | collective-permute-done | bytes 69664 | tf_op jit(solution)/shard_map/ppermute | solution.py:563
  97.3 0.0 copy-done.3
  97.3 0.0 copy-done.8
  97.3 0.0 copy-done.9
  97.3 0.0 copy-start.10
  97.3 0.6 copy-done.10
  97.9 6.4 %mix.1 = (bf16[128,128]{1,0:T(8,128)(2,1)}, bf16[128,128]{1,0:T(8,128)(2,1)}) custom-call(f32[136,128]{1,0:T(8,128)} %copy-done.3, f32[136,128]{1,0:T(8,128)} %copy-done.10, f32[136,128]{1,0:T(8,128)} %copy-done.9, f32[136,128]{1,0:T(8,128)} %copy-done.8), custom_call_target="tpu_custom_call" | custom-call | flops 200000000 | bytes 600000 | tf_op jit(solution)/shard_map/mix/pallas_call | solution.py:477
  104.3 4.4 %transform.2._ = f32[128,32,256]{2,1,0:T(8,128)} custom-call(f32[128,40,128]{2,1,0:T(8,128)} %bitcast.17, bf16[128,128]{1,0:T(8,128)(2,1)} %get-tuple-element.21.hi_ref, bf16[128,128]{1,0:T(8,128)(2,1)} %get-tuple-element.22.lo_ref), custom_call_target="tpu_custom_call" | custom-call | flops 450000000 | bytes 4300000 | tf_op jit(solution)/shard_map/transform/pallas_call | solution.py:521
  108.7 3.1 %all-to-all-done = f32[32,4,2,16,128]{4,3,2,1,0:T(8,128)} async-done(((f32[32,4,2,16,128]{4,3,2,1,0:T(8,128)}), f32[32,4,2,16,128]{4,3,2,1,0:T(8,128)}, u32[]{:S(2)}, u32[]{:S(2)}) %all-to-all-start) | async-done | bytes 2097184 | tf_op jit(solution)/shard_map/all_to_all | solution.py:567
  111.8 4.4 %transform.3 = f32[128,32,256]{2,1,0:T(8,128)} custom-call(f32[128,32,128]{2,1,0:T(8,128)} %bitcast.f_ref, bf16[128,128]{1,0:T(8,128)(2,1)} %get-tuple-element.21.hi_ref, bf16[128,128]{1,0:T(8,128)(2,1)} %get-tuple-element.22.lo_ref, f32[128,32,256]{2,1,0:T(8,128)} %transform.2._), custom_call_target="tpu_custom_call", output_to_operand_aliasing={{}: (3, {})} | custom-call | flops 450000000 | bytes 4300000 | tf_op jit(solution)/shard_map/transform/pallas_call | solution.py:521
  116.2 55.8 %all_to_all.21 = f32[32,4,32,256]{3,2,1,0:T(8,128)S(1)} all-to-all(f32[32,4,32,256]{3,2,1,0:T(8,128)} %bitcast.15), channel_id=1, replica_groups=mesh['ma_0'=4,'ma_1'=4,'ma_2'=2,'sa'=4] {'ma_0','ma_1','ma_2'}, dimensions={0} | all-to-all | bytes 8388608 | tf_op jit(solution)/shard_map/all_to_all | solution.py:570
  172.0 2.5 %copy.29 = f32[32,4,4,8,256]{4,3,0,2,1:T(8,128)} copy(f32[32,4,4,8,256]{4,3,2,1,0:T(8,128)S(1)} %bitcast.18) | data formatting | bytes 8388608 | tf_op jit(solution)/shard_map/reshape | solution.py:571
  (10 shorter events, 0.1 us)
Async XLA Ops:
  1.5 29.2 %copy-start.5 = (s32[32,16]{0,1:T(8,128)S(1)}, s32[32,16]{0,1:T(8,128)}, u32[]{:S(2)}) copy-start(s32[32,16]{0,1:T(8,128)} %param.11) | copy-start | bytes 6148
  1.5 29.9 %copy-start.6 = (f32[32,16]{0,1:T(8,128)S(1)}, f32[32,16]{0,1:T(8,128)}, u32[]{:S(2)}) copy-start(f32[32,16]{0,1:T(8,128)} %param.12) | copy-start | bytes 6148
  1.5 30.6 %copy-start.7 = (f32[32,16]{0,1:T(8,128)S(1)}, f32[32,16]{0,1:T(8,128)}, u32[]{:S(2)}) copy-start(f32[32,16]{0,1:T(8,128)} %param.13) | copy-start | bytes 6148
  16.7 43.5 %all-to-all-start.1 = ((f32[32,4,40,128]{3,2,1,0:T(8,128)}), f32[32,4,40,128]{3,2,1,0:T(8,128)S(1)}, u32[]{:S(2)}, u32[]{:S(2)}) async-start(f32[32,4,40,128]{3,2,1,0:T(8,128)} %get-tuple-element.18), calls=%async_computation.1 | async-start | bytes 5242880 | tf_op jit(solution)/shard_map/all_to_all | solution.py:550
  26.3 10.3 %collective-permute-start = (f32[5,2,8192]{2,1,0:T(2,128)}, f32[5,2,8192]{2,1,0:T(2,128)S(1)}, u32[]{:S(2)}, u32[]{:S(2)}) collective-permute-start(f32[5,2,8192]{2,1,0:T(2,128)} %get-tuple-element.14), channel_id=1, source_target_pairs={{0,1},{1,2},{2,3},{4,5},{5,6},{6,7},{8,9},{9,10},{10,11},{12,13},{... | collective-permute-start | bytes 983048 | tf_op jit(solution)/shard_map/ppermute | solution.py:548
  29.4 10.9 %collective-permute-start.1 = (f32[5,2,8192]{2,1,0:T(2,128)}, f32[5,2,8192]{2,1,0:T(2,128)S(1)}, u32[]{:S(2)}, u32[]{:S(2)}) collective-permute-start(f32[5,2,8192]{2,1,0:T(2,128)} %get-tuple-element.15), channel_id=1, source_target_pairs={{1,0},{2,1},{3,2},{5,4},{6,5},{7,6},{9,8},{10,9},{11,10},{13,12},{... | collective-permute-start | bytes 983048 | tf_op jit(solution)/shard_map/ppermute | solution.py:549
  34.5 23.4 %copy-start.4 = (f32[2,8,128]{2,1,0:T(8,128)S(1)}, f32[2,8,128]{2,1,0:T(8,128)}, u32[]{:S(2)}) copy-start(f32[2,8,128]{2,1,0:T(8,128)} %cell_sums.1) | copy-start | bytes 24580
  36.6 3.7 %copy-start.1 = (f32[5,2,8192]{2,1,0:T(2,128)}, f32[5,2,8192]{2,1,0:T(2,128)S(1)}, u32[]{:S(2)}) copy-start(f32[5,2,8192]{2,1,0:T(2,128)S(1)} %collective-permute-done.lo_ref.clo_ref) | copy-start | bytes 983044
  40.3 0.7 copy-start.2
  60.2 23.6 %copy-start = (f32[32,4,40,128]{3,2,1,0:T(8,128)}, f32[32,4,40,128]{3,2,1,0:T(8,128)S(1)}, u32[]{:S(2)}) copy-start(f32[32,4,40,128]{3,2,1,0:T(8,128)S(1)} %all-to-all-done.1) | copy-start | bytes 7864324
  79.2 32.6 %all-to-all-start = ((f32[32,4,2,16,128]{4,3,2,1,0:T(8,128)}), f32[32,4,2,16,128]{4,3,2,1,0:T(8,128)}, u32[]{:S(2)}, u32[]{:S(2)}) async-start(f32[32,4,2,16,128]{4,3,2,1,0:T(8,128)} %get-tuple-element.16), calls=%async_computation | async-start | bytes 4194304 | tf_op jit(solution)/shard_map/all_to_all | solution.py:567
  87.0 1.5 collective-permute-start.2
  89.3 8.0 %copy-start.3 = (f32[136,128]{1,0:T(8,128)}, f32[136,128]{1,0:T(8,128)S(1)}, u32[]{:S(2)}) copy-start(f32[136,128]{1,0:T(8,128)S(1)} %add.3.p0_ref) | copy-start | bytes 208900
  89.3 3.8 %collective-permute-start.5 = (f32[136,128]{1,0:T(8,128)S(1)}, f32[136,128]{1,0:T(8,128)S(1)}, u32[]{:S(2)}, u32[]{:S(2)}) collective-permute-start(f32[136,128]{1,0:T(8,128)S(1)} %add.3.p0_ref), channel_id=1, source_target_pairs={{0,3},{1,0},{2,1},{3,2},{4,7},{5,4},{6,5},{7,6},{8,11},{9,8},{10,9... | collective-permute-start | bytes 208904 | tf_op jit(solution)/shard_map/ppermute | solution.py:563
  90.2 5.1 %collective-permute-start.4 = (f32[136,128]{1,0:T(8,128)S(1)}, f32[136,128]{1,0:T(8,128)S(1)}, u32[]{:S(2)}, u32[]{:S(2)}) collective-permute-start(f32[136,128]{1,0:T(8,128)S(1)} %add.3.p0_ref), channel_id=1, source_target_pairs={{0,2},{1,3},{2,0},{3,1},{4,6},{5,7},{6,4},{7,5},{8,10},{9,11},{10,... | collective-permute-start | bytes 208904 | tf_op jit(solution)/shard_map/ppermute | solution.py:563
  92.4 4.9 %collective-permute-start.3 = (f32[136,128]{1,0:T(8,128)S(1)}, f32[136,128]{1,0:T(8,128)S(1)}, u32[]{:S(2)}, u32[]{:S(2)}) collective-permute-start(f32[136,128]{1,0:T(8,128)S(1)} %add.3.p0_ref), channel_id=1, source_target_pairs={{0,1},{1,2},{2,3},{3,0},{4,5},{5,6},{6,7},{7,4},{8,9},{9,10},{10,1... | collective-permute-start | bytes 208904 | tf_op jit(solution)/shard_map/ppermute | solution.py:563
  93.2 4.2 %copy-start.8 = (f32[136,128]{1,0:T(8,128)}, f32[136,128]{1,0:T(8,128)S(1)}, u32[]{:S(2)}) copy-start(f32[136,128]{1,0:T(8,128)S(1)} %collective-permute-done.5.p3_ref) | copy-start | bytes 208900
  95.3 2.0 %copy-start.9 = (f32[136,128]{1,0:T(8,128)}, f32[136,128]{1,0:T(8,128)S(1)}, u32[]{:S(2)}) copy-start(f32[136,128]{1,0:T(8,128)S(1)} %collective-permute-done.4.p2_ref) | copy-start | bytes 208900
  97.3 0.6 copy-start.10

commit v9 on v8

--- a/solution.py
+++ b/solution.py
@@ -131,14 +131,14 @@
     _close(ref, pitch)
 
 
-def _two_steps(m, members, laser_ref, e_ref, ce_ref, u1_ref, ey_ref, pitch, plane_at, step1, step2, edged, put):
+def _two_steps(m, lx_ref, ly_ref, e_ref, ce_ref, u1_ref, ey_ref, pitch, plane_at, step1, step2, edged, put):
     sub = lax.broadcasted_iota(jnp.int32, (8, LANES), 0)
     lane = lax.broadcasted_iota(jnp.int32, (8, LANES), 1)
     last_layer = (lane & (DEPTH - 1)) == DEPTH - 1
     for t in range(STEPS):
         for g in range(0, DEPTH, 8):
             y = sub + g + jnp.where(lane < DEPTH, 0, DEPTH)
-            dy = (y - laser_ref[members + m, t]).astype(jnp.float32)
+            dy = (y - ly_ref[t, m]).astype(jnp.float32)
             ey_ref[t, pl.ds(g, 8), :] = jnp.where(last_layer, jnp.exp(-(dy * dy) / beam_spot_width), 0.0)
 
     def ey_row(t):
@@ -147,7 +147,7 @@
     def factors(t, base, tiles):
         found = []
         for i in range(tiles):
-            dx = (plane_at(base + i + tiles * sub) - laser_ref[m, t]).astype(jnp.float32)
+            dx = (plane_at(base + i + tiles * sub) - lx_ref[t, m]).astype(jnp.float32)
             found.append((step_dt * laser_power) * jnp.exp(-(dx * dx) / beam_spot_width))
         return found
 
@@ -180,7 +180,7 @@
 
 
 def _inner_body(
-    laser_ref, u_ref, c_ref, out_ref, bottom_ref, top_ref, e_ref, ce_ref, u1_ref, ey_ref, rows_ref
+    lx_ref, ly_ref, u_ref, c_ref, out_ref, bottom_ref, top_ref, e_ref, ce_ref, u1_ref, ey_ref, rows_ref
 ):
     m = pl.program_id(0)
     planes = u_ref.shape[1]
@@ -205,8 +205,8 @@
         out[pl.ds(row + i, 8, stride=2), :] = value
 
     tops = _two_steps(
-        m, pl.num_programs(0), laser_ref, e_ref, ce_ref, u1_ref, ey_ref, pitch,
-        lambda row: laser_ref[laser_ref.shape[0] - 1, 0] + row, (4, 3, 1), (8, 2, 1), False, put,
+        m, lx_ref, ly_ref, e_ref, ce_ref, u1_ref, ey_ref, pitch,
+        lambda row: lax.axis_index("sa") * planes + row, (4, 3, 1), (8, 2, 1), False, put,
     )
     for i in range(2):
         rows_ref[pl.ds(i, 8, stride=2), :] = tops[i]
@@ -215,7 +215,7 @@
 
 
 def _outer_body(
-    laser_ref, u_ref, c_ref, lo_ref, hi_ref, clo_ref, chi_ref, out_ref, surf_ref, e_ref, ce_ref, u1_ref,
+    lx_ref, ly_ref, u_ref, c_ref, lo_ref, hi_ref, clo_ref, chi_ref, out_ref, surf_ref, e_ref, ce_ref, u1_ref,
     ey_ref,
 ):
     m = pl.program_id(0)
@@ -253,10 +253,10 @@
         out[pl.ds(pl.multiple_of(v * half + 8 * i, 8), 8), :] = value
 
     def plane_at(row):
-        return laser_ref[laser_ref.shape[0] - 1, 0] + ((row - OUTER_ROW) >> 1) - 2 + (row & 1) * (planes - 8)
+        return lax.axis_index("sa") * planes + ((row - OUTER_ROW) >> 1) - 2 + (row & 1) * (planes - 8)
 
     tops = _two_steps(
-        m, pl.num_programs(0), laser_ref, e_ref, ce_ref, u1_ref, ey_ref, pitch, plane_at,
+        m, lx_ref, ly_ref, e_ref, ce_ref, u1_ref, ey_ref, pitch, plane_at,
         (OUTER_ROW, 3, 2), (OUTER_ROW + 4, 2, 2), True, put,
     )
     for i in range(2):
@@ -268,7 +268,7 @@
     return pl.pallas_call(
         body,
         grid=(operands[0].shape[0],),
-        in_specs=[pl.BlockSpec(memory_space=pltpu.SMEM)] + specs,
+        in_specs=[pl.BlockSpec(memory_space=pltpu.SMEM)] * 2 + specs,
         out_specs=out_specs,
         out_shape=[jax.ShapeDtypeStruct(shape, jnp.float32) for shape in out_shape],
         scratch_shapes=[scratch, scratch, scratch, pltpu.VMEM((STEPS, DEPTH, LANES), jnp.float32)] + more_scratch,
@@ -277,7 +277,7 @@
         ),
         cost_estimate=pl.CostEstimate(flops=100_000_000, bytes_accessed=7_000_000, transcendentals=0),
         name=name,
-    )(lasers, *operands)
+    )(*lasers, *operands)
 
 
 def forecast_inner(lasers, u, cond, blocks):
@@ -539,11 +539,10 @@
     for axis in MA:
         blocks *= lax.axis_size(axis)
     slabs = lax.axis_size("sa")
-    first = lax.axis_index("sa") * planes
     u = initial_heat_matrix
     forward = [(i, i + 1) for i in range(slabs - 1)]
     backward = [(b, a) for a, b in forward]
-    lasers = jnp.concatenate([laser_x, laser_y, jnp.broadcast_to(first, (1, STEPS))], axis=0)
+    lasers = (laser_x.T, laser_y.T)
     sent_in, bottom, top = forecast_inner(lasers, u, conductivity, blocks)
     low = lax.ppermute(top, "sa", forward)
     high = lax.ppermute(bottom, "sa", backward)

time: 175 us -> 174 us (level)
  no operation moved by 1% of the time
where the time goes in v9:
time: 174 us; the launch traced here: 173 us
  blocking collectives  74.8 us (43%)
  Pallas kernels  51.3 us (29%)
  starting transfers between devices  22 us (13%)
  waiting for transfers between devices  17.2 us (10%)
  local copies, waits for them, and re-layouts  6.69 us (4%)
    all_to_all x1, blocking collectives, per_device(): lax.all_to_all(done.reshape((blocks, members) + done.shape[1:]), MA, 0, 0...  55.8 us
    pallas_call x2, Pallas kernels, _forecast_call(): pl.pallas_call(body, grid=(operands[0].shape[0],), in_specs=[pl.BlockSpec...  31.3 us
    all_to_all x1, blocking collectives, per_device(): seen = lax.all_to_all(rows, MA, 0, 0, tiled=True)  19 us
    all_to_all x1, starting transfers between devices, per_device(): held_in = lax.all_to_all(sent_in, MA, 0, 0, tiled=True)  9.6 us
    pallas_call x2, Pallas kernels, transform(): pl.pallas_call(_transform_body if onto is None else _transform_more, grid...  8.82 us
    pallas_call x1, Pallas kernels, mix_matrices(): pl.pallas_call(_mix_body, out_shape=[shape, shape], scratch_shapes=[pltpu...  6.35 us
    ppermute x3, waiting for transfers between devices, per_device(): lax.ppermute(part, 'sa', [(i, (i + s) % slabs) for i in range(slabs)])  4.55 us
    all_to_all x1, starting transfers between devices, per_device(): held_out = lax.all_to_all(sent_out, MA, 0, 0, tiled=True)  4.55 us
  transfers between devices with their start and end apart: 8, of which 8 were waited for; matrix products, arithmetic and copies ran while one was open for 2% of the time, Pallas kernels for 18%

profile of v9, /device:TPU:1, one launch (start us, length us, event | category | flops | bytes accessed | tf_op | source)
XLA Modules:
  0.0 173.0 jit_solution(11631201427717823820)
XLA Ops:
  0.0 0.0 copy-start.5
  0.0 0.0 copy-start.7
  0.0 15.2 %inner.1 = (f32[32,4,40,128]{3,2,1,0:T(8,128)}, f32[5,2,8192]{2,1,0:T(2,128)}, f32[5,2,8192]{2,1,0:T(2,128)}) custom-call(s32[2,4]{1,0:T(2,128)} %bitcast.21, s32[2,4]{1,0:T(2,128)} %bitcast.23, f32[4,32,8192]{2,1,0:T(8,128)} %u_ref.3, f32[32,8192]{1,0:T(8,128)} %c_ref.3), custom_call_target="tpu_custom_call" | custom-call | flops 100000000 | bytes 7000000 | tf_op jit(solution)/shard_map/inner/pallas_call | solution.py:268
  15.2 9.6 %all-to-all-start.1 = ((f32[32,4,40,128]{3,2,1,0:T(8,128)}), f32[32,4,40,128]{3,2,1,0:T(8,128)S(1)}, u32[]{:S(2)}, u32[]{:S(2)}) async-start(f32[32,4,40,128]{3,2,1,0:T(8,128)} %get-tuple-element.18), calls=%async_computation.1 | async-start | bytes 5242880 | tf_op jit(solution)/shard_map/all_to_all | solution.py:549
  24.8 3.1 %collective-permute-start = (f32[5,2,8192]{2,1,0:T(2,128)}, f32[5,2,8192]{2,1,0:T(2,128)S(1)}, u32[]{:S(2)}, u32[]{:S(2)}) collective-permute-start(f32[5,2,8192]{2,1,0:T(2,128)} %get-tuple-element.14), channel_id=1, source_target_pairs={{0,1},{1,2},{2,3},{4,5},{5,6},{6,7},{8,9},{9,10},{10,11},{12,13},{... | collective-permute-start | bytes 983048 | tf_op jit(solution)/shard_map/ppermute | solution.py:547
  27.9 1.3 collective-permute-start.1
  29.2 0.0 copy-done.5
  29.2 0.7 copy.14.pc_ref
  29.9 0.0 copy-done.6
  29.9 0.7 copy.15.obs_ref
  30.6 0.0 copy-done.7
  30.6 0.7 copy.16.var_ref
  31.3 1.7 cell_sums.1
  33.0 0.0 copy-start.4
  33.0 2.1 %collective-permute-done.lo_ref.clo_ref = f32[5,2,8192]{2,1,0:T(2,128)S(1)} collective-permute-done((f32[5,2,8192]{2,1,0:T(2,128)}, f32[5,2,8192]{2,1,0:T(2,128)S(1)}, u32[]{:S(2)}, u32[]{:S(2)}) %collective-permute-start) | collective-permute-done | bytes 327712 | tf_op jit(solution)/shard_map/ppermute | solution.py:547
  35.1 0.0 copy-start.1
  35.1 3.7 %collective-permute-done.1.hi_ref.chi_ref = f32[5,2,8192]{2,1,0:T(2,128)S(1)} collective-permute-done((f32[5,2,8192]{2,1,0:T(2,128)}, f32[5,2,8192]{2,1,0:T(2,128)S(1)}, u32[]{:S(2)}, u32[]{:S(2)}) %collective-permute-start.1) | collective-permute-done | bytes 327712 | tf_op jit(solution)/shard_map/ppermute | solution.py:548
  38.8 0.0 copy-done.1
  38.8 0.7 copy-done.2
  39.5 16.1 %outer.1 = (f32[32,4,2,16,128]{4,3,2,1,0:T(8,128)}, f32[4,16,128]{2,1,0:T(8,128)}) custom-call(s32[2,4]{1,0:T(2,128)} %bitcast.22, s32[2,4]{1,0:T(2,128)} %bitcast.24, f32[4,32,8192]{2,1,0:T(8,128)} %u_ref.3, f32[32,8192]{1,0:T(8,128)} %c_ref.3, f32[5,2,8192]{2,1,0:T(2,128)} %copy-done.1, f32[5,2,8192]{2,1,0:T(2,128)} %copy-done.2, f32[5,2,8192]{2,1,0:T(2,128)} %copy-done.1, ...), custom_call_target="tpu_custom_call" | custom-call | flops 100000000 | bytes 7000000 | tf_op jit(solution)/shard_map/outer/pallas_call | solution.py:268
  55.6 0.8 copy_bitcast_fusion
  56.4 0.0 copy-done.4
  56.4 2.3 %all-to-all-done.1 = f32[32,4,40,128]{3,2,1,0:T(8,128)S(1)} async-done(((f32[32,4,40,128]{3,2,1,0:T(8,128)}), f32[32,4,40,128]{3,2,1,0:T(8,128)S(1)}, u32[]{:S(2)}, u32[]{:S(2)}) %all-to-all-start.1) | async-done | bytes 2621472 | tf_op jit(solution)/shard_map/all_to_all | solution.py:549
  58.7 19.0 %all_to_all.20.seen_ref = f32[32,40,128]{2,1,0:T(8,128)} all-to-all(f32[32,40,128]{2,1,0:T(8,128)S(1)} %bitcast.20), channel_id=1, replica_groups=mesh['ma_0'=4,'ma_1'=4,'ma_2'=2,'sa'=4] {'ma_0','ma_1','ma_2'}, dimensions={0} | all-to-all | bytes 1310720 | tf_op jit(solution)/shard_map/all_to_all | solution.py:557
  77.7 4.5 %all-to-all-start = ((f32[32,4,2,16,128]{4,3,2,1,0:T(8,128)}), f32[32,4,2,16,128]{4,3,2,1,0:T(8,128)}, u32[]{:S(2)}, u32[]{:S(2)}) async-start(f32[32,4,2,16,128]{4,3,2,1,0:T(8,128)} %get-tuple-element.16), calls=%async_computation | async-start | bytes 4194304 | tf_op jit(solution)/shard_map/all_to_all | solution.py:566
  82.3 0.0 copy-done
  82.3 3.2 %gram.1 = f32[136,128]{1,0:T(8,128)} custom-call(f32[128,40,128]{2,1,0:T(8,128)} %bitcast.17, f32[32,40,128]{2,1,0:T(8,128)} %all_to_all.20.seen_ref), custom_call_target="tpu_custom_call" | custom-call | flops 80000000 | bytes 1700000 | tf_op jit(solution)/shard_map/gram/pallas_call | solution.py:395
  85.4 0.0 collective-permute-start.2
  85.5 1.4 collective-permute-done.2
  86.9 0.9 add.3.p0_ref
  87.8 0.0 copy-start.3
  87.8 0.9 collective-permute-start.5
  88.7 2.1 %collective-permute-start.4 = (f32[136,128]{1,0:T(8,128)S(1)}, f32[136,128]{1,0:T(8,128)S(1)}, u32[]{:S(2)}, u32[]{:S(2)}) collective-permute-start(f32[136,128]{1,0:T(8,128)S(1)} %add.3.p0_ref), channel_id=1, source_target_pairs={{0,2},{1,3},{2,0},{3,1},{4,6},{5,7},{6,4},{7,5},{8,10},{9,11},{10,... | collective-permute-start | bytes 208904 | tf_op jit(solution)/shard_map/ppermute | solution.py:562
  90.9 0.3 collective-permute-start.3
  91.2 0.4 collective-permute-done.5.p3_ref
  91.6 2.2 %collective-permute-done.4.p2_ref = f32[136,128]{1,0:T(8,128)S(1)} collective-permute-done((f32[136,128]{1,0:T(8,128)S(1)}, f32[136,128]{1,0:T(8,128)S(1)}, u32[]{:S(2)}, u32[]{:S(2)}) %collective-permute-start.4) | collective-permute-done | bytes 69664 | tf_op jit(solution)/shard_map/ppermute | solution.py:562
  93.8 1.9 %collective-permute-done.3.p1_ref = f32[136,128]{1,0:T(8,128)S(1)} collective-permute-done((f32[136,128]{1,0:T(8,128)S(1)}, f32[136,128]{1,0:T(8,128)S(1)}, u32[]{:S(2)}, u32[]{:S(2)}) %collective-permute-start.3) | collective-permute-done | bytes 69664 | tf_op jit(solution)/shard_map/ppermute | solution.py:562
  95.7 0.0 copy-done.3
  95.7 0.0 copy-done.8
  95.8 0.0 copy-done.9
  95.8 0.0 copy-start.10
  95.8 0.6 copy-done.10
  96.4 6.4 %mix.1 = (bf16[128,128]{1,0:T(8,128)(2,1)}, bf16[128,128]{1,0:T(8,128)(2,1)}) custom-call(f32[136,128]{1,0:T(8,128)} %copy-done.3, f32[136,128]{1,0:T(8,128)} %copy-done.10, f32[136,128]{1,0:T(8,128)} %copy-done.9, f32[136,128]{1,0:T(8,128)} %copy-done.8), custom_call_target="tpu_custom_call" | custom-call | flops 200000000 | bytes 600000 | tf_op jit(solution)/shard_map/mix/pallas_call | solution.py:477
  102.7 4.4 %transform.2._ = f32[128,32,256]{2,1,0:T(8,128)} custom-call(f32[128,40,128]{2,1,0:T(8,128)} %bitcast.18, bf16[128,128]{1,0:T(8,128)(2,1)} %get-tuple-element.21.hi_ref, bf16[128,128]{1,0:T(8,128)(2,1)} %get-tuple-element.22.lo_ref), custom_call_target="tpu_custom_call" | custom-call | flops 450000000 | bytes 4300000 | tf_op jit(solution)/shard_map/transform/pallas_call | solution.py:521
  107.1 3.2 %all-to-all-done = f32[32,4,2,16,128]{4,3,2,1,0:T(8,128)} async-done(((f32[32,4,2,16,128]{4,3,2,1,0:T(8,128)}), f32[32,4,2,16,128]{4,3,2,1,0:T(8,128)}, u32[]{:S(2)}, u32[]{:S(2)}) %all-to-all-start) | async-done | bytes 2097184 | tf_op jit(solution)/shard_map/all_to_all | solution.py:566
  110.3 4.4 %transform.3 = f32[128,32,256]{2,1,0:T(8,128)} custom-call(f32[128,32,128]{2,1,0:T(8,128)} %bitcast.2.f_ref, bf16[128,128]{1,0:T(8,128)(2,1)} %get-tuple-element.21.hi_ref, bf16[128,128]{1,0:T(8,128)(2,1)} %get-tuple-element.22.lo_ref, f32[128,32,256]{2,1,0:T(8,128)} %transform.2._), custom_call_target="tpu_custom_call", output_to_operand_aliasing={{}: (3, {})} | custom-call | flops 450000000 | bytes 4300000 | tf_op jit(solution)/shard_map/transform/pallas_call | solution.py:521
  114.7 55.8 %all_to_all.21 = f32[32,4,32,256]{3,2,1,0:T(8,128)S(1)} all-to-all(f32[32,4,32,256]{3,2,1,0:T(8,128)} %bitcast.16), channel_id=1, replica_groups=mesh['ma_0'=4,'ma_1'=4,'ma_2'=2,'sa'=4] {'ma_0','ma_1','ma_2'}, dimensions={0} | all-to-all | bytes 8388608 | tf_op jit(solution)/shard_map/all_to_all | solution.py:569
  170.5 2.5 %copy.18 = f32[32,4,4,8,256]{4,3,0,2,1:T(8,128)} copy(f32[32,4,4,8,256]{4,3,2,1,0:T(8,128)S(1)} %bitcast.19) | data formatting | bytes 8388608 | tf_op jit(solution)/shard_map/reshape | solution.py:570
  (7 shorter events, 0.1 us)
Async XLA Ops:
  0.0 29.2 %copy-start.5 = (s32[32,16]{0,1:T(8,128)S(1)}, s32[32,16]{0,1:T(8,128)}, u32[]{:S(2)}) copy-start(s32[32,16]{0,1:T(8,128)} %param.11) | copy-start | bytes 6148
  0.0 29.9 %copy-start.6 = (f32[32,16]{0,1:T(8,128)S(1)}, f32[32,16]{0,1:T(8,128)}, u32[]{:S(2)}) copy-start(f32[32,16]{0,1:T(8,128)} %param.12) | copy-start | bytes 6148
  0.0 30.6 %copy-start.7 = (f32[32,16]{0,1:T(8,128)S(1)}, f32[32,16]{0,1:T(8,128)}, u32[]{:S(2)}) copy-start(f32[32,16]{0,1:T(8,128)} %param.13) | copy-start | bytes 6148
  15.2 43.5 %all-to-all-start.1 = ((f32[32,4,40,128]{3,2,1,0:T(8,128)}), f32[32,4,40,128]{3,2,1,0:T(8,128)S(1)}, u32[]{:S(2)}, u32[]{:S(2)}) async-start(f32[32,4,40,128]{3,2,1,0:T(8,128)} %get-tuple-element.18), calls=%async_computation.1 | async-start | bytes 5242880 | tf_op jit(solution)/shard_map/all_to_all | solution.py:549
  24.8 10.3 %collective-permute-start = (f32[5,2,8192]{2,1,0:T(2,128)}, f32[5,2,8192]{2,1,0:T(2,128)S(1)}, u32[]{:S(2)}, u32[]{:S(2)}) collective-permute-start(f32[5,2,8192]{2,1,0:T(2,128)} %get-tuple-element.14), channel_id=1, source_target_pairs={{0,1},{1,2},{2,3},{4,5},{5,6},{6,7},{8,9},{9,10},{10,11},{12,13},{... | collective-permute-start | bytes 983048 | tf_op jit(solution)/shard_map/ppermute | solution.py:547
  27.9 10.9 %collective-permute-start.1 = (f32[5,2,8192]{2,1,0:T(2,128)}, f32[5,2,8192]{2,1,0:T(2,128)S(1)}, u32[]{:S(2)}, u32[]{:S(2)}) collective-permute-start(f32[5,2,8192]{2,1,0:T(2,128)} %get-tuple-element.15), channel_id=1, source_target_pairs={{1,0},{2,1},{3,2},{5,4},{6,5},{7,6},{9,8},{10,9},{11,10},{13,12},{... | collective-permute-start | bytes 983048 | tf_op jit(solution)/shard_map/ppermute | solution.py:548
  33.0 23.4 %copy-start.4 = (f32[2,8,128]{2,1,0:T(8,128)S(1)}, f32[2,8,128]{2,1,0:T(8,128)}, u32[]{:S(2)}) copy-start(f32[2,8,128]{2,1,0:T(8,128)} %cell_sums.1) | copy-start | bytes 24580
  35.1 3.7 %copy-start.1 = (f32[5,2,8192]{2,1,0:T(2,128)}, f32[5,2,8192]{2,1,0:T(2,128)S(1)}, u32[]{:S(2)}) copy-start(f32[5,2,8192]{2,1,0:T(2,128)S(1)} %collective-permute-done.lo_ref.clo_ref) | copy-start | bytes 983044
  38.8 0.7 copy-start.2
  58.7 23.6 %copy-start = (f32[32,4,40,128]{3,2,1,0:T(8,128)}, f32[32,4,40,128]{3,2,1,0:T(8,128)S(1)}, u32[]{:S(2)}) copy-start(f32[32,4,40,128]{3,2,1,0:T(8,128)S(1)} %all-to-all-done.1) | copy-start | bytes 7864324
  77.7 32.6 %all-to-all-start = ((f32[32,4,2,16,128]{4,3,2,1,0:T(8,128)}), f32[32,4,2,16,128]{4,3,2,1,0:T(8,128)}, u32[]{:S(2)}, u32[]{:S(2)}) async-start(f32[32,4,2,16,128]{4,3,2,1,0:T(8,128)} %get-tuple-element.16), calls=%async_computation | async-start | bytes 4194304 | tf_op jit(solution)/shard_map/all_to_all | solution.py:566
  85.4 1.5 collective-permute-start.2
  87.8 7.9 %copy-start.3 = (f32[136,128]{1,0:T(8,128)}, f32[136,128]{1,0:T(8,128)S(1)}, u32[]{:S(2)}) copy-start(f32[136,128]{1,0:T(8,128)S(1)} %add.3.p0_ref) | copy-start | bytes 208900
  87.8 3.8 %collective-permute-start.5 = (f32[136,128]{1,0:T(8,128)S(1)}, f32[136,128]{1,0:T(8,128)S(1)}, u32[]{:S(2)}, u32[]{:S(2)}) collective-permute-start(f32[136,128]{1,0:T(8,128)S(1)} %add.3.p0_ref), channel_id=1, source_target_pairs={{0,3},{1,0},{2,1},{3,2},{4,7},{5,4},{6,5},{7,6},{8,11},{9,8},{10,9... | collective-permute-start | bytes 208904 | tf_op jit(solution)/shard_map/ppermute | solution.py:562
  88.7 5.1 %collective-permute-start.4 = (f32[136,128]{1,0:T(8,128)S(1)}, f32[136,128]{1,0:T(8,128)S(1)}, u32[]{:S(2)}, u32[]{:S(2)}) collective-permute-start(f32[136,128]{1,0:T(8,128)S(1)} %add.3.p0_ref), channel_id=1, source_target_pairs={{0,2},{1,3},{2,0},{3,1},{4,6},{5,7},{6,4},{7,5},{8,10},{9,11},{10,... | collective-permute-start | bytes 208904 | tf_op jit(solution)/shard_map/ppermute | solution.py:562
  90.9 4.9 %collective-permute-start.3 = (f32[136,128]{1,0:T(8,128)S(1)}, f32[136,128]{1,0:T(8,128)S(1)}, u32[]{:S(2)}, u32[]{:S(2)}) collective-permute-start(f32[136,128]{1,0:T(8,128)S(1)} %add.3.p0_ref), channel_id=1, source_target_pairs={{0,1},{1,2},{2,3},{3,0},{4,5},{5,6},{6,7},{7,4},{8,9},{9,10},{10,1... | collective-permute-start | bytes 208904 | tf_op jit(solution)/shard_map/ppermute | solution.py:562
  91.6 4.1 %copy-start.8 = (f32[136,128]{1,0:T(8,128)}, f32[136,128]{1,0:T(8,128)S(1)}, u32[]{:S(2)}) copy-start(f32[136,128]{1,0:T(8,128)S(1)} %collective-permute-done.5.p3_ref) | copy-start | bytes 208900
  93.8 2.0 %copy-start.9 = (f32[136,128]{1,0:T(8,128)}, f32[136,128]{1,0:T(8,128)S(1)}, u32[]{:S(2)}) copy-start(f32[136,128]{1,0:T(8,128)S(1)} %collective-permute-done.4.p2_ref) | copy-start | bytes 208900
  95.8 0.6 copy-start.10
